TPU v7x, 512 devices: a whole 4x4x16 slice. The times are simulated.
512 devices in a mesh: seq: 64 (over x, z), head: 8 (over y, core).
Axes of the slice: x: 4, y: 4, z: 16, core: 2. Of those that a mesh axis runs over, the one named last changes fastest.
Arguments:
- query: bfloat16 [8192, 4096], P('seq', 'head'), may hold values from -20 to 20
- keys: bfloat16 [8192, 4096], P('seq', 'head'), may hold values from -6 to 6
- values: bfloat16 [8192, 4096], P('seq', 'head'), may hold values from -20 to 20
- grad_normed: bfloat16 [8192, 4096], P('seq', 'head'), may hold values from -18 to 18
- norm_gain: float32 [4096], P('head'), may hold values from 0.25 to 1.75
- doc_ids: int32 [8192], P('seq'), may hold values from 0 to 15, never falling along the last dimension, each value on 1 to 1024 neighbouring positions
- home: int32 [8192], P('seq'), may hold values from 0 to 8191, as said below
Outputs:
- input_grads: bfloat16 [8192, 3, 4096], P('seq', None, 'head')
Inputs may be any that keep to these rules, and one draw needn't show every extreme that they name: home is a permutation of 0 to 8191; the owner index along seq of token t is home[t] // 128. Of the 128 tokens on one index of seq, at most 4 have one owner index, and that many is reached for some pairs; every index of seq sends the same multiset of counts to the owners, in a drawn order of owners.
All inputs are finite; a program needn't handle non-finite values.
Results may differ from a plain program's by a relative error of at most 0.0058.
Values may be sent and summed in bfloat16 or wider, within the bound.
No kernel may reach another device: no remote copies, remote signals or barrier semaphores. Data moves between devices by JAX's collectives and lax.ppermute only.
A program may use at most 128 MiB of HBM per device.

v0:
```python
import jax
import jax.numpy as jnp
from jax import lax
from jax.sharding import PartitionSpec as P

HEADS = 32
HS = 128


EPSILON = 1e-05
LOW_SENTINEL = -1.0
HIGH_SENTINEL = 1000000000.0


def entering(value, axis, join, neutral, backward):
    count, mine = (lax.axis_size(axis), lax.axis_index(axis))
    pieces = jax.tree.map(lambda part: lax.all_gather(part, axis), value)
    if backward:
        pieces = jax.tree.map(lambda part: part[::-1], pieces)
        mine = count - 1 - mine
    total = jax.tree.map(
        lambda part, zero: jnp.full_like(part, 0) + jnp.asarray(zero, part.dtype), value, neutral
    )

    def step(position, total):
        longer = join(total, jax.tree.map(lambda part: part[position], pieces))
        return jax.tree.map(lambda new, old: jnp.where(position < mine, new, old), longer, total)

    return lax.fori_loop(0, count - 1, step, total)


def masked_scores(left, right, doc_block):
    places = jnp.arange(doc_block.shape[0])
    visible = (doc_block[:, None] == doc_block[None, :]) & (places[:, None] >= places[None, :])
    raw = jnp.einsum("thd,shd->hts", left, right, preferred_element_type=jnp.float32)
    return jnp.where(visible[None], raw, 0.0).astype(jnp.bfloat16)


def outer_sum(left, right, keep):
    kept = jnp.where(keep[:, None, None], left, jnp.zeros_like(left))
    return jnp.einsum("tha,thb->hab", kept, right, preferred_element_type=jnp.float32)


def join_high(earlier, later):
    top = jnp.maximum(earlier[0], later[0])
    state = jnp.where(earlier[0] == top, earlier[1], 0.0) + jnp.where(
        later[0] == top, later[1], 0.0
    )
    return (top, state)


def join_low(earlier, later):
    bottom = jnp.minimum(earlier[0], later[0])
    state = jnp.where(earlier[0] == bottom, earlier[1], 0.0) + jnp.where(
        later[0] == bottom, later[1], 0.0
    )
    return (bottom, state)


def mixed(left, right, form):
    return jnp.einsum(form, left, right, preferred_element_type=jnp.float32)


def local(query, keys, values, grad_normed, norm_gain, doc_ids, home):
    tok_rows, width = query.shape
    heads_here = width // HS
    full_width = HEADS * HS
    query_h = query.reshape(tok_rows, heads_here, HS)
    keys_h = keys.reshape(tok_rows, heads_here, HS)
    values_h = values.reshape(tok_rows, heads_here, HS)
    first_doc = doc_ids[0].astype(jnp.float32)
    last_doc = doc_ids[-1].astype(jnp.float32)
    first_rows = doc_ids == doc_ids[0]
    last_rows = doc_ids == doc_ids[-1]
    first_mask = first_rows[:, None, None]
    last_mask = last_rows[:, None, None]
    attn = masked_scores(query_h, keys_h, doc_ids)
    own_forward = outer_sum(keys_h, values_h, last_rows)
    zero_state = jnp.zeros_like(own_forward)
    into_key, into_state = entering(
        (last_doc, own_forward),
        "seq",
        join_high,
        (jnp.array(LOW_SENTINEL, jnp.float32), zero_state),
        False,
    )
    forward_carry = jnp.where(into_key == first_doc, into_state, 0.0).astype(jnp.bfloat16)
    output = mixed(attn, values_h, "hts,shd->thd") + jnp.where(
        first_mask, mixed(query_h, forward_carry, "tha,hab->thb"), 0.0
    )
    flat = output.reshape(tok_rows, width)
    scaled = norm_gain[None, :] * grad_normed.astype(jnp.float32)
    squares, inner = lax.psum(
        (jnp.sum(flat * flat, axis=1), jnp.sum(scaled * flat, axis=1)), "head"
    )
    inv_rms = lax.rsqrt(squares / full_width + EPSILON)
    grad_out = (
        inv_rms[:, None] * scaled
        - flat * (inv_rms * inv_rms * inv_rms * inner / full_width)[:, None]
    ).astype(jnp.bfloat16)
    grad_h = grad_out.reshape(tok_rows, heads_here, HS)
    back = masked_scores(grad_h, values_h, doc_ids)
    grad_query = mixed(back, keys_h, "hts,shd->thd") + jnp.where(
        first_mask, mixed(grad_h, forward_carry, "thb,hab->tha"), 0.0
    )
    grad_query = grad_query.astype(jnp.bfloat16).reshape(tok_rows, width)
    own_reverse = outer_sum(query_h, grad_h, first_rows)
    seq_count = lax.axis_size("seq")
    capacity = 2 * tok_rows // seq_count
    owner = home // tok_rows
    target_row = home % tok_rows
    places = jnp.arange(tok_rows)
    chosen = (owner[:, None] == jnp.arange(seq_count)[None, :]).astype(jnp.bfloat16)
    earlier_rows = (places[:, None] > places[None, :]).astype(jnp.bfloat16)
    before = jnp.dot(earlier_rows, chosen, preferred_element_type=jnp.float32)
    ranks = jnp.sum(before * chosen.astype(jnp.float32), axis=1).astype(jnp.int32)
    row_index = (
        jnp.full((seq_count, capacity), tok_rows, jnp.int32).at[owner, ranks].set(target_row)
    )
    back_key, back_state = entering(
        (first_doc, own_reverse),
        "seq",
        join_low,
        (jnp.array(HIGH_SENTINEL, jnp.float32), zero_state),
        True,
    )
    reverse_carry = jnp.where(back_key == last_doc, back_state, 0.0).astype(jnp.bfloat16)
    grad_keys = mixed(back, query_h, "hts,thd->shd") + jnp.where(
        last_mask, mixed(values_h, reverse_carry, "thb,hab->tha"), 0.0
    )
    grad_values = mixed(attn, grad_h, "hts,thd->shd") + jnp.where(
        last_mask, mixed(keys_h, reverse_carry, "tha,hab->thb"), 0.0
    )
    pair = jnp.stack(
        [
            grad_keys.astype(jnp.bfloat16).reshape(tok_rows, width),
            grad_values.astype(jnp.bfloat16).reshape(tok_rows, width),
        ],
        axis=1,
    )
    stacked = jnp.concatenate([grad_query[:, None, :], pair], axis=1)
    bucket = jnp.zeros((seq_count, capacity, 3, width), jnp.bfloat16).at[owner, ranks].set(stacked)
    received, index_back = (
        lax.all_to_all(bucket, "seq", split_axis=0, concat_axis=0, tiled=True),
        lax.all_to_all(row_index, "seq", split_axis=0, concat_axis=0, tiled=True),
    )
    result = jnp.zeros((tok_rows, 3, width), jnp.bfloat16)
    return result.at[index_back.reshape(-1)].set(received.reshape(-1, 3, width), mode="drop")


def solution(mesh):
    placed = (
        P("seq", "head"),
        P("seq", "head"),
        P("seq", "head"),
        P("seq", "head"),
        P("head"),
        P("seq"),
        P("seq"),
    )
    return jax.shard_map(
        local, mesh=mesh, in_specs=placed, out_specs=P("seq", None, "head"), check_vma=False
    )
```

profile of v0, /device:TPU:6, one launch (start us, length us, event | category | flops | bytes accessed | tf_op | source)
XLA Modules:
  0.0 886.5 jit_solution(3774605126130692993)
XLA Ops:
  6.5 1.3 fusion.49
  8.9 1.9 broadcast_compare_fusion
  14.1 1.3 dynamic-slice
  16.8 129.5 %all-reduce.2 = (f32[64]{0:T(128)S(1)}, f32[64]{0:T(128)S(1)}) all-reduce(f32[64]{0:T(128)S(1)} %dynamic-update-slice, f32[64]{0:T(128)S(1)} %dynamic-update-slice.1), channel_id=1, replica_groups=mesh['seq'=64,'head'=8] {'seq'}, use_global_device_ids=true, to_apply=%add | all-reduce | flops 128 | bytes 1024
  147.1 1.1 fusion.9
  148.5 60.4 %all-gather.5.cloned.1.call-done = f32[256,128,128]{2,1,0:T(8,128)} async-done(((f32[4,128,128]{2,1,0:T(8,128)}), f32[256,128,128]{2,1,0:T(8,128)}) %all-gather.5.cloned.1.call-update) | async-done | bytes 16777232 | tf_op jit(solution)/shard_map/all_gather | solution.py:17
  208.9 190.3 %while.32 = (s32[]{:T(128)}, f32[]{:T(128)}, f32[4,128,128]{2,1,0:T(8,128)S(1)}, s32[]{:T(128)}, f32[64]{0:T(128)S(1)}, /*index=5*/f32[64,4,128,128]{3,2,1,0:T(8,128)}, s32[]{:T(128)}, s32[]{:T(128)}) while((s32[]{:T(128)}, f32[]{:T(128)}, f32[4,128,128]{2,1,0:T(8,128)S(1)}, s32[]{:T(128)}, f32[64]{0:T(128)S(1)}, ...), condition=%wide.region_3.4_spmd.clone, body=%wide.region_2.3_spmd.clone.sunk | while | flops 327688 | bytes 786598 | solution.py:29
  400.7 14.3 %all-reduce.3 = (f32[128]{0:T(128)S(1)}, f32[128]{0:T(128)S(1)}) all-reduce(f32[128]{0:T(128)S(1)} %multiply_reduce_fusion, f32[128]{0:T(128)S(1)} %get-tuple-element.307), channel_id=1, replica_groups=mesh['seq'=64,'head'=8] {'head'}, use_global_device_ids=true, to_apply=%region_7.8 | all-reduce | flops 256 | bytes 2048 | tf_op jit(solution)/shard_map/psum | solution.py:93
  418.0 6.5 scatter_fusion
  425.1 12.2 %all-to-all-start = ((s32[64,1,4]{2,1,0:T(1,128)}), s32[64,1,4]{2,1,0:T(1,128)S(1)}, u32[]{:S(2)}, u32[]{:S(2)}) async-start(s32[64,1,4]{2,1,0:T(1,128)} %copy.79), calls=%async_computation | async-start | bytes 65536 | tf_op jit(solution)/shard_map/all_to_all | solution.py:145
  438.6 165.9 %all-gather.7.cloned.1.call-done = f32[256,128,128]{2,1,0:T(8,128)} async-done(((f32[4,128,128]{2,1,0:T(8,128)}), f32[256,128,128]{2,1,0:T(8,128)}) %all-gather.7.cloned.1.call-update) | async-done | bytes 16777232 | tf_op jit(solution)/shard_map/all_gather | solution.py:17
  604.5 11.7 %rev.7 = f32[64,4,128,128]{3,2,1,0:T(8,128)} reverse(f32[64,4,128,128]{3,2,1,0:T(8,128)} %bitcast.118), dimensions={0} | reverse | bytes 33554432 | tf_op jit(solution)/shard_map/rev | solution.py:19
  616.2 190.5 %while.33 = (s32[]{:T(128)}, f32[]{:T(128)}, f32[4,128,128]{2,1,0:T(8,128)S(1)}, s32[]{:T(128)}, f32[64]{0:T(128)S(1)}, /*index=5*/f32[64,4,128,128]{3,2,1,0:T(8,128)}, s32[]{:T(128)}, s32[]{:T(128)}) while((s32[]{:T(128)}, f32[]{:T(128)}, f32[4,128,128]{2,1,0:T(8,128)S(1)}, s32[]{:T(128)}, f32[64]{0:T(128)S(1)}, ...), condition=%wide.region_9.10_spmd.clone, body=%wide.region_8.9_spmd.clone.sunk | while | flops 327688 | bytes 786598 | solution.py:29
  618.0 1.1 fusion.72
  621.1 1.1 fusion.72
  624.1 1.1 fusion.72
  627.1 1.1 fusion.72
  630.1 1.1 fusion.72
  633.2 1.1 fusion.72
  636.2 1.1 fusion.72
  639.2 1.1 fusion.72
  642.2 1.1 fusion.72
  690.6 1.1 fusion.72
  696.7 1.1 fusion.72
  748.1 1.1 fusion.72
  754.1 1.1 fusion.72
  805.5 1.1 fusion.72
  809.0 5.7 scatter_fusion.1
  814.7 1.2 copy.103
  815.9 12.8 %all-to-all-start.1 = ((bf16[64,4,3,512]{3,1,2,0:T(4,128)(2,1)}), bf16[64,4,3,512]{3,1,2,0:T(4,128)(2,1)S(1)}, u32[]{:S(2)}, u32[]{:S(2)}) async-start(bf16[64,4,3,512]{3,1,2,0:T(4,128)(2,1)} %copy.103), calls=%async_computation.1 | async-start | bytes 1572864 | tf_op jit(solution)/shard_map/all_to_all | solution.py:144
  830.1 40.8 %all-to-all-done.1 = bf16[64,4,3,512]{3,1,2,0:T(4,128)(2,1)S(1)} async-done(((bf16[64,4,3,512]{3,1,2,0:T(4,128)(2,1)}), bf16[64,4,3,512]{3,1,2,0:T(4,128)(2,1)S(1)}, u32[]{:S(2)}, u32[]{:S(2)}) %all-to-all-start.1) | async-done | bytes 786464 | tf_op jit(solution)/shard_map/all_to_all | solution.py:144
  871.6 7.3 scatter_fusion.2
  (290 shorter events, 214.6 us)
Async XLA Ops:
  6.5 4.3 copy-start
  6.5 202.4 %all-gather.5.cloned.1.call-start = ((), (), s32[]{:S(2)}) async-start(), calls=%async_computation.2 | async-start | bytes 17039360 | tf_op jit(solution)/shard_map/all_gather | solution.py:17
  11.7 592.8 %all-gather.7.cloned.1.call-start = ((), (), s32[]{:S(2)}) async-start(), calls=%async_computation.3 | async-start | bytes 17039360 | tf_op jit(solution)/shard_map/all_gather | solution.py:17
  425.1 390.8 %all-to-all-start = ((s32[64,1,4]{2,1,0:T(1,128)}), s32[64,1,4]{2,1,0:T(1,128)S(1)}, u32[]{:S(2)}, u32[]{:S(2)}) async-start(s32[64,1,4]{2,1,0:T(1,128)} %copy.79), calls=%async_computation | async-start | bytes 65536 | tf_op jit(solution)/shard_map/all_to_all | solution.py:145
  604.5 202.6 %copy-start.1 = (bf16[128,512]{1,0:T(8,128)(2,1)S(1)}, bf16[128,512]{1,0:T(8,128)(2,1)}, u32[]{:S(2)}) copy-start(bf16[128,512]{1,0:T(8,128)(2,1)} %param.12) | copy-start | bytes 393220
  815.9 55.0 %all-to-all-start.1 = ((bf16[64,4,3,512]{3,1,2,0:T(4,128)(2,1)}), bf16[64,4,3,512]{3,1,2,0:T(4,128)(2,1)S(1)}, u32[]{:S(2)}, u32[]{:S(2)}) async-start(bf16[64,4,3,512]{3,1,2,0:T(4,128)(2,1)} %copy.103), calls=%async_computation.1 | async-start | bytes 1572864 | tf_op jit(solution)/shard_map/all_to_all | solution.py:144
Sparse Core Ops, SparseCore 0:
  11.8 197.0 all-gather.4
  417.2 187.2 all-gather.6
where the time goes:
time: 893 us; the launch traced here: 887 us
  waiting for transfers between devices  267 us (30%)
  loops' own time  168 us (19%)
  other arithmetic  146 us (16%)
  blocking collectives  144 us (16%)
  local copies, waits for them, and re-layouts  117 us (13%)
  starting transfers between devices  25 us (3%)
  between operations  14.9 us (2%)
    all_gather x2, waiting for transfers between devices, entering(): pieces = jax.tree.map(lambda part: lax.all_gather(part, axis), value)  226 us
    another operation x2, loops' own time, entering(): return lax.fori_loop(0, count - 1, step, total)  168 us
    select_n x126, other arithmetic, step(): jnp.where(position < mine, new, old)  139 us
    unnamed x1, blocking collectives  129 us
    dynamic_slice x126, local copies, waits for them, and re-layouts, step(): longer = join(total, jax.tree.map(lambda part: part[position], pieces))  73.9 us
    all_to_all x1, waiting for transfers between devices, local(): lax.all_to_all(bucket, 'seq', split_axis=0, concat_axis=0, tiled=True)  40.8 us
  transfers between devices with their start and end apart: 4, of which 3 were waited for; matrix products, arithmetic and copies ran while one was open for 16% of the time, Pallas kernels for 0%

commit v1 on v0

v1 whole, which is shorter than its diff:
```python
import jax
import jax.numpy as jnp
from jax import lax
from jax.sharding import PartitionSpec as P

HEADS = 32
HS = 128
EPSILON = 1e-05
SUB = 4
EXTRA = 16


def mixed(left, right, form):
    return jnp.einsum(form, left, right, preferred_element_type=jnp.float32)


def heads_first(array):
    tok_rows, width = array.shape
    return array.reshape(tok_rows, width // HS, HS).transpose(1, 0, 2)


def local(query, keys, values, grad_normed, norm_gain, doc_ids, home):
    tok_rows, width = query.shape
    full_width = HEADS * HS
    seq_count = lax.axis_size("seq")
    head_count = lax.axis_size("head")
    capacity = 2 * tok_rows // seq_count
    groups = [[g * SUB + s for s in range(SUB)] for g in range(seq_count // SUB)]
    wide_groups = [[i * head_count + h for i in one for h in range(head_count)] for one in groups]
    mine = lax.axis_index("seq") % SUB

    owner = home // tok_rows
    target_row = home % tok_rows
    places = jnp.arange(tok_rows)
    same_owner = owner[:, None] == owner[None, :]
    ranks = jnp.sum(jnp.where(same_owner & (places[None, :] < places[:, None]), 1, 0), axis=1)
    local_slot = owner * capacity + ranks
    slot_match = local_slot[None, :] == jnp.arange(seq_count * capacity)[:, None]
    row_index = jnp.max(jnp.where(slot_match, target_row[None, :], -1), axis=1)
    row_index = row_index.reshape(seq_count, capacity)

    def regroup(arrays):
        return lax.all_to_all(
            jnp.concatenate(arrays, axis=1), "seq", 0, 0, tiled=True, axis_index_groups=groups
        )

    small = jnp.stack([doc_ids, owner, ranks]).astype(jnp.bfloat16)
    small = jnp.pad(small, ((0, EXTRA - 3), (0, 0)))
    small = jnp.broadcast_to(small[None], (SUB, EXTRA, tok_rows))
    key_value = regroup([heads_first(keys), heads_first(values), small])
    query_grad = regroup([heads_first(query), heads_first(grad_normed)])
    key = key_value[:, :tok_rows]
    value = key_value[:, tok_rows : 2 * tok_rows]
    small = key_value[:, 2 * tok_rows :]
    doc = small[:, 0].astype(jnp.int32)
    slot = (small[:, 1].astype(jnp.int32) * SUB + jnp.arange(SUB)[:, None]) * capacity
    slot = (slot + small[:, 2].astype(jnp.int32)).reshape(-1)
    quer = query_grad[:, :tok_rows]
    normed = query_grad[:, tok_rows:]

    first, last = doc[:, 0], doc[:, -1]
    first_rows = (doc == first[:, None])[:, :, None]
    last_rows = (doc == last[:, None])[:, :, None]
    zero = jnp.zeros((), jnp.bfloat16)

    def exchange(state, doc_number, sign):
        payload = jnp.concatenate(
            [state.astype(jnp.bfloat16), jnp.full((EXTRA, HS), doc_number, jnp.bfloat16)], axis=0
        )
        pieces = []
        for far in (1, 2):
            step = sign * far * SUB
            pairs = [(i, i + step) for i in range(seq_count) if 0 <= i + step < seq_count]
            pieces.append(lax.ppermute(payload, "seq", pairs))
        return pieces

    def arriving(pieces, doc_number):
        doc_number = doc_number.astype(jnp.bfloat16)
        return sum(
            jnp.where(p[HS, 0] == doc_number, p[:HS].astype(jnp.float32), 0.0) for p in pieces
        )

    sent = mixed(jnp.where((doc == last[-1])[:, :, None], key, zero), value, "bta,btc->ac")
    pieces = exchange(sent, last[-1], 1)
    own = mixed(jnp.where(last_rows, key, zero), value, "bta,btc->bac")
    places = jnp.arange(tok_rows)
    visible = (doc[:, :, None] == doc[:, None, :]) & (places[:, None] >= places[None, :])
    attn = jnp.where(visible, mixed(quer, key, "bta,bsa->bts"), 0.0).astype(jnp.bfloat16)
    state = arriving(pieces, first[0])
    carries = [state]
    for b in range(1, SUB):
        state = own[b - 1] + jnp.where(first[b - 1] == last[b - 1], state, 0.0)
        state = jnp.where(last[b - 1] == first[b], state, 0.0)
        carries.append(state)
    carry = jnp.stack(carries).astype(jnp.bfloat16)
    output = mixed(attn, value, "bts,bsc->btc") + jnp.where(
        first_rows, mixed(quer, carry, "bta,bac->btc"), 0.0
    )
    gain = lax.dynamic_slice(norm_gain, (mine * HS,), (HS,))
    scaled = gain * normed.astype(jnp.float32)
    sums = jnp.concatenate([jnp.sum(output * output, -1), jnp.sum(scaled * output, -1)])
    sums = jnp.broadcast_to(sums[None], (SUB * head_count, 2 * SUB, tok_rows))
    sums = lax.all_to_all(
        sums, ("seq", "head"), 0, 0, tiled=True, axis_index_groups=wide_groups
    ).sum(0)
    squares, inner = sums[:SUB, :, None], sums[SUB:, :, None]
    inv_rms = lax.rsqrt(squares / full_width + EPSILON)
    grad = (
        inv_rms * scaled - output * (inv_rms * inv_rms * inv_rms * inner / full_width)
    ).astype(jnp.bfloat16)

    sent = mixed(jnp.where((doc == first[0])[:, :, None], quer, zero), grad, "bta,btc->ac")
    pieces = exchange(sent, first[0], -1)
    back = jnp.where(visible, mixed(grad, value, "btc,bsc->bts"), 0.0).astype(jnp.bfloat16)
    grad_query = mixed(back, key, "bts,bsa->bta") + jnp.where(
        first_rows, mixed(grad, carry, "btc,bac->bta"), 0.0
    )
    own = mixed(jnp.where(first_rows, quer, zero), grad, "bta,btc->bac")
    state = arriving(pieces, last[-1])
    carries = [state]
    for b in range(SUB - 2, -1, -1):
        state = own[b + 1] + jnp.where(first[b + 1] == last[b + 1], state, 0.0)
        state = jnp.where(first[b + 1] == last[b], state, 0.0)
        carries.append(state)
    carry = jnp.stack(carries[::-1]).astype(jnp.bfloat16)
    grad_keys = mixed(back, quer, "bts,bta->bsa") + jnp.where(
        last_rows, mixed(value, carry, "bsc,bac->bsa"), 0.0
    )
    grad_values = mixed(attn, grad, "bts,btc->bsc") + jnp.where(
        last_rows, mixed(key, carry, "bsa,bac->bsc"), 0.0
    )

    rows = jnp.concatenate([grad_query, grad_keys, grad_values], -1).astype(jnp.bfloat16)
    rows = rows.reshape(SUB * tok_rows, 3 * HS)
    slots = SUB * capacity
    place = slot[None, :] == jnp.arange(seq_count * slots)[:, None]
    packed = jnp.dot(
        place.astype(jnp.bfloat16), rows, preferred_element_type=jnp.float32
    ).astype(jnp.bfloat16)
    index = lax.all_to_all(row_index, "seq", 0, 0, tiled=True)
    received = lax.all_to_all(
        packed.reshape(seq_count, slots, 3 * HS), "seq", 0, 0, tiled=True
    )
    received = received.reshape(seq_count // SUB, SUB, slots, 3, HS)
    choose = index.reshape(-1)[None, :] == jnp.arange(tok_rows)[:, None]
    choose = choose.astype(jnp.bfloat16).reshape(tok_rows, seq_count // SUB, slots)
    return mixed(choose, received, "rgk,gskjd->rjsd").astype(jnp.bfloat16).reshape(
        tok_rows, 3, width
    )


def solution(mesh):
    placed = (
        P("seq", "head"),
        P("seq", "head"),
        P("seq", "head"),
        P("seq", "head"),
        P("head"),
        P("seq"),
        P("seq"),
    )
    return jax.shard_map(
        local, mesh=mesh, in_specs=placed, out_specs=P("seq", None, "head"), check_vma=False
    )
```

time: 893 us -> 164 us (0.18)
  waiting for transfers between devices: 267 us -> 53.7 us
  loops' own time: 168 us -> 0 us
  blocking collectives: 144 us -> 0 us
  other arithmetic: 146 us -> 5.53 us
  local copies, waits for them, and re-layouts: 117 us -> 9.67 us
  starting transfers between devices: 25 us -> 71.6 us
    all_gather x2 -> x0, waiting for transfers between devices: 226 us -> none  [entering(): pieces = jax.tree.map(lambda part: lax.all_gather(part, axis), value)]
    another operation x2 -> x0, loops' own time: 168 us -> none  [entering(): return lax.fori_loop(0, count - 1, step, total)]
    select_n x128 -> x0, other arithmetic: 140 us -> none  [the longest x126 139 us: step(): jnp.where(position < mine, new, old)]
    unnamed x1 -> x0, blocking collectives: 129 us -> none
    dynamic_slice x126 -> x1, local copies, waits for them, and re-layouts: 73.9 us -> 0.76 us  [local(): gain = lax.dynamic_slice(norm_gain, (mine * HS,), (HS,))]
    ppermute x0 -> x4, starting transfers between devices: none -> 32.6 us  [exchange(): pieces.append(lax.ppermute(payload, 'seq', pairs))]
    scatter x5 -> x0, local copies, waits for them, and re-layouts: 21.4 us -> none  [the longest x2 8.1 us: local(): result.at[index_back.reshape(-1)]]
    psum x1 -> x0, blocking collectives: 14.3 us -> none  [local(): lax.psum((jnp.sum(flat * flat, axis=1), jnp.sum(scaled * flat, axis=1)),...]
  transfers between devices with their start and end apart: 4 -> 9, of which waited for: 3 -> 4; matrix products, arithmetic and copies ran while one was open for 16% -> 8% of each run, Pallas kernels for 0% -> 0%
where the time goes in v1:
time: 164 us; the launch traced here: 163 us
  starting transfers between devices  71.6 us (44%)
  waiting for transfers between devices  53.7 us (33%)
  between operations  16.7 us (10%)
  local copies, waits for them, and re-layouts  9.67 us (6%)
  matrix products  5.62 us (3%)
  other arithmetic  5.53 us (3%)
    all_to_all x1, waiting for transfers between devices, local(): lax.all_to_all(packed.reshape(seq_count, slots, 3 * HS), 'seq', 0, 0, til...  38.8 us
    ppermute x4, starting transfers between devices, exchange(): pieces.append(lax.ppermute(payload, 'seq', pairs))  32.6 us
    all_to_all x1, starting transfers between devices, local(): lax.all_to_all(packed.reshape(seq_count, slots, 3 * HS), 'seq', 0, 0, til...  12.1 us
    all_to_all x1, starting transfers between devices, local(): index = lax.all_to_all(row_index, 'seq', 0, 0, tiled=True)  9.54 us
    all_to_all x2, starting transfers between devices, regroup(): lax.all_to_all(jnp.concatenate(arrays, axis=1), 'seq', 0, 0, tiled=True,...  9.3 us
    all_to_all x1, starting transfers between devices, local(): lax.all_to_all(sums, ('seq', 'head'), 0, 0, tiled=True, axis_index_groups...  8.08 us
    all_to_all x2, waiting for transfers between devices, regroup(): lax.all_to_all(jnp.concatenate(arrays, axis=1), 'seq', 0, 0, tiled=True,...  7.24 us
    ppermute x4, waiting for transfers between devices, exchange(): pieces.append(lax.ppermute(payload, 'seq', pairs))  4.73 us
  transfers between devices with their start and end apart: 9, of which 4 were waited for; matrix products, arithmetic and copies ran while one was open for 8% of the time, Pallas kernels for 0%

profile of v1, /device:TPU:6, one launch (start us, length us, event | category | flops | bytes accessed | tf_op | source)
XLA Modules:
  0.0 162.8 jit_solution(2767426050695511478)
XLA Ops:
  0.0 0.7 convert_bitcast_fusion.5
  0.9 0.7 convert_bitcast_fusion.6
  1.5 1.0 copy.61
  2.7 1.0 copy.63
  3.9 0.7 pad_maximum_fusion
  4.6 5.9 %all-to-all-start = ((bf16[4,272,128]{2,1,0:T(8,128)(2,1)}), bf16[4,272,128]{2,1,0:T(8,128)(2,1)S(1)}, u32[]{:S(2)}, u32[]{:S(2)}) async-start(bf16[4,272,128]{2,1,0:T(8,128)(2,1)} %pad_maximum_fusion), calls=%async_computation | async-start | bytes 557056 | tf_op jit(solution)/shard_map/all_to_all | solution.py:43
  11.1 0.8 dynamic_slice.3
  11.8 0.7 pad_maximum_fusion.1
  12.6 7.2 %all-to-all-done = bf16[4,272,128]{2,1,0:T(8,128)(2,1)S(1)} async-done(((bf16[4,272,128]{2,1,0:T(8,128)(2,1)}), bf16[4,272,128]{2,1,0:T(8,128)(2,1)S(1)}, u32[]{:S(2)}, u32[]{:S(2)}) %all-to-all-start) | async-done | bytes 278560 | tf_op jit(solution)/shard_map/all_to_all | solution.py:43
  19.8 3.4 %all-to-all-start.1 = ((bf16[4,256,128]{2,1,0:T(8,128)(2,1)}), bf16[4,256,128]{2,1,0:T(8,128)(2,1)S(1)}, u32[]{:S(2)}, u32[]{:S(2)}) async-start(bf16[4,256,128]{2,1,0:T(8,128)(2,1)} %pad_maximum_fusion.1), calls=%async_computation.1 | async-start | bytes 524288 | tf_op jit(solution)/shard_map/all_to_all | solution.py:43
  23.2 0.7 fusion.99
  24.7 1.3 broadcast_compare_fusion
  26.3 9.1 %collective-permute-start = (bf16[144,128]{1,0:T(8,128)(2,1)S(1)}, bf16[144,128]{1,0:T(8,128)(2,1)S(1)}, u32[]{:S(2)}, u32[]{:S(2)}) collective-permute-start(bf16[144,128]{1,0:T(8,128)(2,1)S(1)} %concatenate.28), channel_id=1, source_target_pairs={{0,32},{8,40},{16,48},{24,56},{32,64},{40,72},{48,80},{56,88},{64,... | collective-permute-start | bytes 110600 | tf_op jit(solution)/shard_map/ppermute | solution.py:74
  35.4 8.7 %collective-permute-start.1 = (bf16[144,128]{1,0:T(8,128)(2,1)S(1)}, bf16[144,128]{1,0:T(8,128)(2,1)S(1)}, u32[]{:S(2)}, u32[]{:S(2)}) collective-permute-start(bf16[144,128]{1,0:T(8,128)(2,1)S(1)} %concatenate.28), channel_id=1, source_target_pairs={{0,64},{8,72},{16,80},{24,88},{32,96},{40,104},{48,112},{56,120},{... | collective-permute-start | bytes 110600 | tf_op jit(solution)/shard_map/ppermute | solution.py:74
  53.1 0.5 slice.186
  54.2 0.5 slice.188
  55.9 0.7 broadcast_in_dim.139
  56.5 8.1 %all-to-all-start.2 = ((f32[32,8,128]{2,1,0:T(8,128)}), f32[32,8,128]{2,1,0:T(8,128)S(1)}, u32[]{:S(2)}, u32[]{:S(2)}) async-start(f32[32,8,128]{2,1,0:T(8,128)} %broadcast_in_dim.139), calls=%async_computation.2 | async-start | bytes 262144 | tf_op jit(solution)/shard_map/all_to_all | solution.py:103
  64.7 0.7 all_to_all.22
  70.5 2.9 %all-to-all-done.2 = f32[32,8,128]{2,1,0:T(8,128)S(1)} async-done(((f32[32,8,128]{2,1,0:T(8,128)}), f32[32,8,128]{2,1,0:T(8,128)S(1)}, u32[]{:S(2)}, u32[]{:S(2)}) %all-to-all-start.2) | async-done | bytes 131104 | tf_op jit(solution)/shard_map/all_to_all | solution.py:103
  73.3 9.5 %all-to-all-start.4 = ((s32[64,1,4]{2,1,0:T(1,128)}), s32[64,1,4]{2,1,0:T(1,128)S(1)}, u32[]{:S(2)}, u32[]{:S(2)}) async-start(s32[64,1,4]{2,1,0:T(1,128)} %bitcast.47), calls=%async_computation.4 | async-start | bytes 65536 | tf_op jit(solution)/shard_map/all_to_all | solution.py:140
  83.5 7.5 %collective-permute-start.2 = (bf16[144,128]{1,0:T(8,128)(2,1)S(1)}, bf16[144,128]{1,0:T(8,128)(2,1)S(1)}, u32[]{:S(2)}, u32[]{:S(2)}) collective-permute-start(bf16[144,128]{1,0:T(8,128)(2,1)S(1)} %concatenate.31), channel_id=1, source_target_pairs={{32,0},{40,8},{48,16},{56,24},{64,32},{72,40},{80,48},{88,56},{96,... | collective-permute-start | bytes 110600 | tf_op jit(solution)/shard_map/ppermute | solution.py:74
  91.1 7.2 %collective-permute-start.3 = (bf16[144,128]{1,0:T(8,128)(2,1)S(1)}, bf16[144,128]{1,0:T(8,128)(2,1)S(1)}, u32[]{:S(2)}, u32[]{:S(2)}) collective-permute-start(bf16[144,128]{1,0:T(8,128)(2,1)S(1)} %concatenate.31), channel_id=1, source_target_pairs={{64,0},{72,8},{80,16},{88,24},{96,32},{104,40},{112,48},{120,56},{... | collective-permute-start | bytes 110600 | tf_op jit(solution)/shard_map/ppermute | solution.py:74
  99.7 0.5 slice.197
  100.9 4.7 %collective-permute-done.3 = bf16[144,128]{1,0:T(8,128)(2,1)S(1)} collective-permute-done((bf16[144,128]{1,0:T(8,128)(2,1)S(1)}, bf16[144,128]{1,0:T(8,128)(2,1)S(1)}, u32[]{:S(2)}, u32[]{:S(2)}) %collective-permute-start.3) | collective-permute-done | bytes 36896 | tf_op jit(solution)/shard_map/ppermute | solution.py:74
  105.6 0.5 slice.199
  107.3 1.6 fusion.1
  108.9 12.1 %all-to-all-start.3 = ((bf16[64,16,384]{2,1,0:T(8,128)(2,1)}), bf16[64,16,384]{2,1,0:T(8,128)(2,1)S(1)}, u32[]{:S(2)}, u32[]{:S(2)}) async-start(bf16[64,16,384]{2,1,0:T(8,128)(2,1)} %bitcast.46), calls=%async_computation.3 | async-start | bytes 1572864 | tf_op jit(solution)/shard_map/all_to_all | solution.py:141
  121.0 0.5 broadcast.147
  121.5 0.7 reduce.7
  122.3 38.8 %all-to-all-done.3 = bf16[64,16,384]{2,1,0:T(8,128)(2,1)S(1)} async-done(((bf16[64,16,384]{2,1,0:T(8,128)(2,1)}), bf16[64,16,384]{2,1,0:T(8,128)(2,1)S(1)}, u32[]{:S(2)}, u32[]{:S(2)}) %all-to-all-start.3) | async-done | bytes 786464 | tf_op jit(solution)/shard_map/all_to_all | solution.py:141
  161.9 0.9 copy.82
  (53 shorter events, 6.1 us)
Async XLA Ops:
  2.5 8.0 %copy-start = (bf16[128,512]{1,0:T(8,128)(2,1)S(1)}, bf16[128,512]{1,0:T(8,128)(2,1)}, u32[]{:S(2)}) copy-start(bf16[128,512]{1,0:T(8,128)(2,1)} %param.7) | copy-start | bytes 393220
  3.7 7.1 %copy-start.1 = (bf16[128,512]{1,0:T(8,128)(2,1)S(1)}, bf16[128,512]{1,0:T(8,128)(2,1)}, u32[]{:S(2)}) copy-start(bf16[128,512]{1,0:T(8,128)(2,1)} %param.10) | copy-start | bytes 393220
  4.6 15.2 %all-to-all-start = ((bf16[4,272,128]{2,1,0:T(8,128)(2,1)}), bf16[4,272,128]{2,1,0:T(8,128)(2,1)S(1)}, u32[]{:S(2)}, u32[]{:S(2)}) async-start(bf16[4,272,128]{2,1,0:T(8,128)(2,1)} %pad_maximum_fusion), calls=%async_computation | async-start | bytes 557056 | tf_op jit(solution)/shard_map/all_to_all | solution.py:43
  19.8 24.7 %all-to-all-start.1 = ((bf16[4,256,128]{2,1,0:T(8,128)(2,1)}), bf16[4,256,128]{2,1,0:T(8,128)(2,1)S(1)}, u32[]{:S(2)}, u32[]{:S(2)}) async-start(bf16[4,256,128]{2,1,0:T(8,128)(2,1)} %pad_maximum_fusion.1), calls=%async_computation.1 | async-start | bytes 524288 | tf_op jit(solution)/shard_map/all_to_all | solution.py:43
  26.3 26.7 %collective-permute-start = (bf16[144,128]{1,0:T(8,128)(2,1)S(1)}, bf16[144,128]{1,0:T(8,128)(2,1)S(1)}, u32[]{:S(2)}, u32[]{:S(2)}) collective-permute-start(bf16[144,128]{1,0:T(8,128)(2,1)S(1)} %concatenate.28), channel_id=1, source_target_pairs={{0,32},{8,40},{16,48},{24,56},{32,64},{40,72},{48,80},{56,88},{64,... | collective-permute-start | bytes 110600 | tf_op jit(solution)/shard_map/ppermute | solution.py:74
  35.4 18.8 %collective-permute-start.1 = (bf16[144,128]{1,0:T(8,128)(2,1)S(1)}, bf16[144,128]{1,0:T(8,128)(2,1)S(1)}, u32[]{:S(2)}, u32[]{:S(2)}) collective-permute-start(bf16[144,128]{1,0:T(8,128)(2,1)S(1)} %concatenate.28), channel_id=1, source_target_pairs={{0,64},{8,72},{16,80},{24,88},{32,96},{40,104},{48,112},{56,120},{... | collective-permute-start | bytes 110600 | tf_op jit(solution)/shard_map/ppermute | solution.py:74
  56.5 16.8 %all-to-all-start.2 = ((f32[32,8,128]{2,1,0:T(8,128)}), f32[32,8,128]{2,1,0:T(8,128)S(1)}, u32[]{:S(2)}, u32[]{:S(2)}) async-start(f32[32,8,128]{2,1,0:T(8,128)} %broadcast_in_dim.139), calls=%async_computation.2 | async-start | bytes 262144 | tf_op jit(solution)/shard_map/all_to_all | solution.py:103
  73.3 35.6 %all-to-all-start.4 = ((s32[64,1,4]{2,1,0:T(1,128)}), s32[64,1,4]{2,1,0:T(1,128)S(1)}, u32[]{:S(2)}, u32[]{:S(2)}) async-start(s32[64,1,4]{2,1,0:T(1,128)} %bitcast.47), calls=%async_computation.4 | async-start | bytes 65536 | tf_op jit(solution)/shard_map/all_to_all | solution.py:140
  83.5 16.2 %collective-permute-start.2 = (bf16[144,128]{1,0:T(8,128)(2,1)S(1)}, bf16[144,128]{1,0:T(8,128)(2,1)S(1)}, u32[]{:S(2)}, u32[]{:S(2)}) collective-permute-start(bf16[144,128]{1,0:T(8,128)(2,1)S(1)} %concatenate.31), channel_id=1, source_target_pairs={{32,0},{40,8},{48,16},{56,24},{64,32},{72,40},{80,48},{88,56},{96,... | collective-permute-start | bytes 110600 | tf_op jit(solution)/shard_map/ppermute | solution.py:74
  91.1 14.6 %collective-permute-start.3 = (bf16[144,128]{1,0:T(8,128)(2,1)S(1)}, bf16[144,128]{1,0:T(8,128)(2,1)S(1)}, u32[]{:S(2)}, u32[]{:S(2)}) collective-permute-start(bf16[144,128]{1,0:T(8,128)(2,1)S(1)} %concatenate.31), channel_id=1, source_target_pairs={{64,0},{72,8},{80,16},{88,24},{96,32},{104,40},{112,48},{120,56},{... | collective-permute-start | bytes 110600 | tf_op jit(solution)/shard_map/ppermute | solution.py:74
  108.9 52.3 %all-to-all-start.3 = ((bf16[64,16,384]{2,1,0:T(8,128)(2,1)}), bf16[64,16,384]{2,1,0:T(8,128)(2,1)S(1)}, u32[]{:S(2)}, u32[]{:S(2)}) async-start(bf16[64,16,384]{2,1,0:T(8,128)(2,1)} %bitcast.46), calls=%async_computation.3 | async-start | bytes 1572864 | tf_op jit(solution)/shard_map/all_to_all | solution.py:141

commit v2 on v1

v2 whole, which is shorter than its diff:
```python
import jax
import jax.numpy as jnp
from jax import lax
from jax.sharding import PartitionSpec as P

HEADS = 32
HS = 128
EPSILON = 1e-05
SUB = 4
EXTRA = 16


def mixed(left, right, form):
    return jnp.einsum(form, left, right, preferred_element_type=jnp.float32)


def heads_first(array):
    return jnp.stack([array[:, at : at + HS] for at in range(0, array.shape[1], HS)])


def together(*values):
    return lax.optimization_barrier(values)


def local(query, keys, values, grad_normed, norm_gain, doc_ids, home):
    tok_rows, width = query.shape
    full_width = HEADS * HS
    seq_count = lax.axis_size("seq")
    head_count = lax.axis_size("head")
    capacity = 2 * tok_rows // seq_count
    slots = SUB * capacity
    groups = [[g * SUB + s for s in range(SUB)] for g in range(seq_count // SUB)]
    wide_groups = [[i * head_count + h for i in one for h in range(head_count)] for one in groups]
    places = jnp.arange(tok_rows)
    blocks = jnp.arange(SUB)

    owner = home // tok_rows
    target_row = home % tok_rows
    same_owner = owner[:, None] == owner[None, :]
    ranks = jnp.sum(jnp.where(same_owner & (places[:, None] < places[None, :]), 1, 0), axis=0)
    local_slot = owner * capacity + ranks
    slot_match = local_slot[None, :] == jnp.arange(seq_count * capacity)[:, None]
    row_index = jnp.max(jnp.where(slot_match, target_row[None, :], -1), axis=1)
    row_index = row_index.reshape(seq_count, capacity)

    def regroup(array):
        return lax.all_to_all(array, "seq", 0, 0, tiled=True, axis_index_groups=groups)

    later = places[:, None] >= places[None, :]
    last_row = jnp.max(jnp.where(later, doc_ids[:, None], -1), axis=0)
    first_row = jnp.min(jnp.where(later, tok_rows, doc_ids[:, None]), axis=0, initial=tok_rows)
    first_row = jnp.minimum(first_row, doc_ids)
    small = jnp.stack([doc_ids, owner, ranks, first_row, last_row]).astype(jnp.bfloat16)
    small = jnp.pad(small, ((0, EXTRA - 5), (0, 0)))
    small = jnp.broadcast_to(small[None], (SUB, EXTRA, tok_rows))
    key_value = regroup(jnp.concatenate([heads_first(keys), heads_first(values), small], axis=1))
    key = key_value[:, :tok_rows]
    value = key_value[:, tok_rows : 2 * tok_rows]
    small = key_value[:, 2 * tok_rows :].astype(jnp.float32)
    doc = small[:, 0]
    gain = norm_gain.reshape(SUB, HS)
    gain = jnp.sum(jnp.where((blocks == lax.axis_index("seq") % SUB)[:, None], gain, 0.0), axis=0)

    first, last = small[:, 3], small[:, 4]
    first_rows = (doc == first)[:, :, None]
    last_rows = (doc == last)[:, :, None]
    zero = jnp.zeros((), jnp.bfloat16)

    def exchange(state, number, sign):
        number = jnp.broadcast_to(number.astype(jnp.bfloat16), (EXTRA, HS))
        payload = jnp.concatenate([state.astype(jnp.bfloat16), number], axis=0)
        pieces = []
        for far in (1, 2):
            step = sign * far * SUB
            pairs = [(i, i + step) for i in range(seq_count) if 0 <= i + step < seq_count]
            pieces.append(lax.ppermute(payload, "seq", pairs))
        return pieces

    def entering(pieces, own, numbers, own_numbers, order):
        state = sum(
            jnp.where(
                p[HS : HS + 1].astype(jnp.float32)[None] == numbers[:, None],
                p[:HS].astype(jnp.float32)[None],
                0.0,
            )
            for p in pieces
        )
        joined = order[:, :, None] & (numbers[:, None] == own_numbers[None, :])
        inside = jnp.sum(jnp.where(joined[:, :, None], own[None], 0.0), axis=1)
        return (state + inside).astype(jnp.bfloat16)

    sent = mixed(jnp.where((doc == last[SUB - 1])[:, :, None], key, zero), value, "bta,btc->ac")
    pieces = exchange(sent, last[SUB - 1], 1)
    own = mixed(jnp.where(last_rows, key, zero), value, "bta,btc->bac")
    query_grad = jnp.concatenate([heads_first(query), heads_first(grad_normed)], axis=1)
    query_grad, own = together(query_grad, own)
    query_grad = regroup(query_grad)
    quer = query_grad[:, :tok_rows]
    normed = query_grad[:, tok_rows:]
    visible = (doc[:, :, None] == doc[:, None, :]) & (places[:, None] >= places[None, :])
    attn = jnp.where(visible, mixed(quer, key, "bta,bsa->bts"), 0.0).astype(jnp.bfloat16)
    carry = entering(pieces, own, first, last, blocks[:, None] > blocks[None, :])
    output = mixed(attn, value, "bts,bsc->btc") + jnp.where(
        first_rows, mixed(quer, carry, "bta,bac->btc"), 0.0
    )
    scaled = gain * normed.astype(jnp.float32)
    sums = jnp.concatenate([jnp.sum(output * output, -1), jnp.sum(scaled * output, -1)])
    sums = jnp.broadcast_to(sums[None], (SUB * head_count, 2 * SUB, tok_rows))
    sums = lax.all_to_all(
        sums, ("seq", "head"), 0, 0, tiled=True, axis_index_groups=wide_groups
    ).sum(0)
    squares, inner = sums[:SUB, :, None], sums[SUB:, :, None]
    inv_rms = lax.rsqrt(squares / full_width + EPSILON)
    grad = (
        inv_rms * scaled - output * (inv_rms * inv_rms * inv_rms * inner / full_width)
    ).astype(jnp.bfloat16)

    sent = mixed(jnp.where((doc == first[0])[:, :, None], quer, zero), grad, "bta,btc->ac")
    pieces = exchange(sent, first[0], -1)
    back = jnp.where(visible, mixed(grad, value, "btc,bsc->bts"), 0.0).astype(jnp.bfloat16)
    grad_query = mixed(back, key, "bts,bsa->bta") + jnp.where(
        first_rows, mixed(grad, carry, "btc,bac->bta"), 0.0
    )
    grad_query = grad_query.astype(jnp.bfloat16)
    own = mixed(jnp.where(first_rows, quer, zero), grad, "bta,btc->bac")

    slot = (small[:, 1] * slots + small[:, 2] + (blocks * capacity)[:, None]).reshape(-1)
    place = slot[None, :] == jnp.arange(seq_count * slots)[:, None].astype(jnp.float32)
    row_index, grad_query = together(row_index, grad_query)
    index = lax.all_to_all(row_index, "seq", 0, 0, tiled=True)
    choose = index.reshape(-1)[None, :] == places[:, None]
    choose = choose.astype(jnp.bfloat16).reshape(tok_rows, seq_count // SUB, slots)

    carry = entering(pieces, own, last, first, blocks[:, None] < blocks[None, :])
    grad_keys = mixed(back, quer, "bts,bta->bsa") + jnp.where(
        last_rows, mixed(value, carry, "bsc,bac->bsa"), 0.0
    )
    grad_values = mixed(attn, grad, "bts,btc->bsc") + jnp.where(
        last_rows, mixed(key, carry, "bsa,bac->bsc"), 0.0
    )
    rows = jnp.concatenate(
        [grad_query, grad_keys.astype(jnp.bfloat16), grad_values.astype(jnp.bfloat16)], -1
    )
    rows = rows.reshape(SUB * tok_rows, 3 * HS)
    packed = jnp.dot(
        place.astype(jnp.bfloat16), rows, preferred_element_type=jnp.float32
    ).astype(jnp.bfloat16)
    packed, choose = together(packed, choose)
    received = lax.all_to_all(
        packed.reshape(seq_count, slots, 3 * HS), "seq", 0, 0, tiled=True
    )
    received = received.reshape(seq_count // SUB, SUB, slots, 3, HS)
    return mixed(choose, received, "rgk,gskjd->rjsd").astype(jnp.bfloat16).reshape(
        tok_rows, 3, width
    )


def solution(mesh):
    placed = (
        P("seq", "head"),
        P("seq", "head"),
        P("seq", "head"),
        P("seq", "head"),
        P("head"),
        P("seq"),
        P("seq"),
    )
    return jax.shard_map(
        local, mesh=mesh, in_specs=placed, out_specs=P("seq", None, "head"), check_vma=False
    )
```

time: 164 us -> 154 us (0.939)
  blocking collectives: 0 us -> 46.5 us
  waiting for transfers between devices: 53.7 us -> 34.4 us
  between operations: 16.7 us -> 0.44 us
  starting transfers between devices: 71.6 us -> 57.6 us
  local copies, waits for them, and re-layouts: 9.67 us -> 4.19 us
    all_to_all x0 -> x1, blocking collectives: none -> 46.5 us  [local(): lax.all_to_all(packed.reshape(seq_count, slots, 3 * HS), 'seq', 0, 0, til...]
    all_to_all x3 -> x2, waiting for transfers between devices: 46.1 us -> 12.3 us  [regroup(): lax.all_to_all(array, 'seq', 0, 0, tiled=True, axis_index_groups=groups)]
    all_to_all x3 -> x2, starting transfers between devices: 21.4 us -> 9.3 us  [regroup(): lax.all_to_all(array, 'seq', 0, 0, tiled=True, axis_index_groups=groups)]
    all_to_all x1, waiting for transfers between devices: 0.01 us -> 11.8 us  [local(): index = lax.all_to_all(row_index, 'seq', 0, 0, tiled=True)]
    all_to_all x1, waiting for transfers between devices: 2.88 us -> 7.79 us  [local(): lax.all_to_all(sums, ('seq', 'head'), 0, 0, tiled=True, axis_index_groups...]
    ppermute x4, starting transfers between devices: 32.6 us -> 28.4 us  [exchange(): pieces.append(lax.ppermute(payload, 'seq', pairs))]
    all_to_all x1, starting transfers between devices: 9.54 us -> 13.4 us  [local(): index = lax.all_to_all(row_index, 'seq', 0, 0, tiled=True)]
    slice x6 -> x0, local copies, waits for them, and re-layouts: 2.91 us -> none  [the longest x4 2.05 us: arriving(): p[HS, 0] == doc_number]
  transfers between devices with their start and end apart: 9 -> 8, of which waited for: 4 -> 5; matrix products, arithmetic and copies ran while one was open for 8% -> 3% of each run, Pallas kernels for 0% -> 0%
where the time goes in v2:
time: 154 us
  starting transfers between devices  57.6 us (37%)
  blocking collectives  46.5 us (30%)
  waiting for transfers between devices  34.4 us (22%)
  other arithmetic  5.66 us (4%)
  matrix products  4.71 us (3%)
  local copies, waits for them, and re-layouts  4.19 us (3%)
    all_to_all x1, blocking collectives, local(): lax.all_to_all(packed.reshape(seq_count, slots, 3 * HS), 'seq', 0, 0, til...  46.5 us
    ppermute x4, starting transfers between devices, exchange(): pieces.append(lax.ppermute(payload, 'seq', pairs))  28.4 us
    all_to_all x1, starting transfers between devices, local(): index = lax.all_to_all(row_index, 'seq', 0, 0, tiled=True)  13.4 us
    all_to_all x2, waiting for transfers between devices, regroup(): lax.all_to_all(array, 'seq', 0, 0, tiled=True, axis_index_groups=groups)  12.3 us
    all_to_all x1, waiting for transfers between devices, local(): index = lax.all_to_all(row_index, 'seq', 0, 0, tiled=True)  11.8 us
    all_to_all x2, starting transfers between devices, regroup(): lax.all_to_all(array, 'seq', 0, 0, tiled=True, axis_index_groups=groups)  9.3 us
    all_to_all x1, waiting for transfers between devices, local(): lax.all_to_all(sums, ('seq', 'head'), 0, 0, tiled=True, axis_index_groups...  7.79 us
    all_to_all x1, starting transfers between devices, local(): lax.all_to_all(sums, ('seq', 'head'), 0, 0, tiled=True, axis_index_groups...  6.47 us
  transfers between devices with their start and end apart: 8, of which 5 were waited for; matrix products, arithmetic and copies ran while one was open for 3% of the time, Pallas kernels for 0%

profile of v2, /device:TPU:6, one launch (start us, length us, event | category | flops | bytes accessed | tf_op | source)
XLA Modules:
  0.0 153.5 jit_solution(10248166929503194800)
XLA Ops:
  0.0 0.8 select_reduce_fusion.3
  0.8 0.7 convert_bitcast_fusion.3
  1.6 0.7 convert_bitcast_fusion.1
  2.4 0.9 slice_bitcast_fusion.11
  3.3 0.7 pad_maximum_fusion.1
  4.0 5.9 %all-to-all-start = ((bf16[4,272,128]{2,1,0:T(8,128)(2,1)}), bf16[4,272,128]{2,1,0:T(8,128)(2,1)S(1)}, u32[]{:S(2)}, u32[]{:S(2)}) async-start(bf16[4,272,128]{2,1,0:T(8,128)(2,1)} %pad_maximum_fusion.1), calls=%async_computation | async-start | bytes 557056 | tf_op jit(solution)/shard_map/all_to_all | solution.py:47
  10.1 0.7 maximum_maximum_fusion
  10.8 8.4 %all-to-all-done = bf16[4,272,128]{2,1,0:T(8,128)(2,1)S(1)} async-done(((bf16[4,272,128]{2,1,0:T(8,128)(2,1)}), bf16[4,272,128]{2,1,0:T(8,128)(2,1)S(1)}, u32[]{:S(2)}, u32[]{:S(2)}) %all-to-all-start) | async-done | bytes 278560 | tf_op jit(solution)/shard_map/all_to_all | solution.py:47
  19.2 0.3 fusion.16
  19.6 13.5 %collective-permute-start.1 = (bf16[144,128]{1,0:T(8,128)(2,1)S(1)}, bf16[144,128]{1,0:T(8,128)(2,1)S(1)}, u32[]{:S(2)}, u32[]{:S(2)}) collective-permute-start(bf16[144,128]{1,0:T(8,128)(2,1)S(1)} %pad_maximum_fusion.2), channel_id=1, source_target_pairs={{0,64},{8,72},{16,80},{24,88},{32,96},{40,104},{48,112},{56,120},{... | collective-permute-start | bytes 110600 | tf_op jit(solution)/shard_map/ppermute | solution.py:76
  33.1 4.3 %collective-permute-start = (bf16[144,128]{1,0:T(8,128)(2,1)S(1)}, bf16[144,128]{1,0:T(8,128)(2,1)S(1)}, u32[]{:S(2)}, u32[]{:S(2)}) collective-permute-start(bf16[144,128]{1,0:T(8,128)(2,1)S(1)} %pad_maximum_fusion.2), channel_id=1, source_target_pairs={{0,32},{8,40},{16,48},{24,56},{32,64},{40,72},{48,80},{56,88},{64,... | collective-permute-start | bytes 110600 | tf_op jit(solution)/shard_map/ppermute | solution.py:76
  37.4 0.3 fusion.25
  37.8 3.4 %all-to-all-start.1 = ((bf16[4,256,128]{2,1,0:T(8,128)(2,1)}), bf16[4,256,128]{2,1,0:T(8,128)(2,1)S(1)}, u32[]{:S(2)}, u32[]{:S(2)}) async-start(bf16[4,256,128]{2,1,0:T(8,128)(2,1)} %maximum_maximum_fusion), calls=%async_computation.1 | async-start | bytes 524288 | tf_op jit(solution)/shard_map/all_to_all | solution.py:47
  41.4 2.4 %collective-permute-done = bf16[144,128]{1,0:T(8,128)(2,1)S(1)} collective-permute-done((bf16[144,128]{1,0:T(8,128)(2,1)S(1)}, bf16[144,128]{1,0:T(8,128)(2,1)S(1)}, u32[]{:S(2)}, u32[]{:S(2)}) %collective-permute-start) | collective-permute-done | bytes 36896 | tf_op jit(solution)/shard_map/ppermute | solution.py:76
  43.9 4.0 %all-to-all-done.1 = bf16[4,256,128]{2,1,0:T(8,128)(2,1)S(1)} async-done(((bf16[4,256,128]{2,1,0:T(8,128)(2,1)}), bf16[4,256,128]{2,1,0:T(8,128)(2,1)S(1)}, u32[]{:S(2)}, u32[]{:S(2)}) %all-to-all-start.1) | async-done | bytes 262176 | tf_op jit(solution)/shard_map/all_to_all | solution.py:47
  48.3 0.4 multiply_reduce_fusion.1
  48.7 0.7 broadcast_in_dim.285
  49.4 6.5 %all-to-all-start.2 = ((f32[32,8,128]{2,1,0:T(8,128)}), f32[32,8,128]{2,1,0:T(8,128)S(1)}, u32[]{:S(2)}, u32[]{:S(2)}) async-start(f32[32,8,128]{2,1,0:T(8,128)} %broadcast_in_dim.285), calls=%async_computation.2 | async-start | bytes 262144 | tf_op jit(solution)/shard_map/all_to_all | solution.py:109
  56.0 0.7 reshape.208
  56.7 7.8 %all-to-all-done.2 = f32[32,8,128]{2,1,0:T(8,128)S(1)} async-done(((f32[32,8,128]{2,1,0:T(8,128)}), f32[32,8,128]{2,1,0:T(8,128)S(1)}, u32[]{:S(2)}, u32[]{:S(2)}) %all-to-all-start.2) | async-done | bytes 131104 | tf_op jit(solution)/shard_map/all_to_all | solution.py:109
  64.8 0.3 fusion.17
  65.2 6.7 %collective-permute-start.3 = (bf16[144,128]{1,0:T(8,128)(2,1)S(1)}, bf16[144,128]{1,0:T(8,128)(2,1)S(1)}, u32[]{:S(2)}, u32[]{:S(2)}) collective-permute-start(bf16[144,128]{1,0:T(8,128)(2,1)S(1)} %pad_maximum_fusion.3), channel_id=1, source_target_pairs={{64,0},{72,8},{80,16},{88,24},{96,32},{104,40},{112,48},{120,56},{... | collective-permute-start | bytes 110600 | tf_op jit(solution)/shard_map/ppermute | solution.py:76
  71.9 3.8 %collective-permute-start.2 = (bf16[144,128]{1,0:T(8,128)(2,1)S(1)}, bf16[144,128]{1,0:T(8,128)(2,1)S(1)}, u32[]{:S(2)}, u32[]{:S(2)}) collective-permute-start(bf16[144,128]{1,0:T(8,128)(2,1)S(1)} %pad_maximum_fusion.3), channel_id=1, source_target_pairs={{32,0},{40,8},{48,16},{56,24},{64,32},{72,40},{80,48},{88,56},{96,... | collective-permute-start | bytes 110600 | tf_op jit(solution)/shard_map/ppermute | solution.py:76
  76.6 13.4 %all-to-all-start.3 = ((s32[64,1,4]{2,1,0:T(1,128)}), s32[64,1,4]{2,1,0:T(1,128)S(1)}, u32[]{:S(2)}, u32[]{:S(2)}) async-start(s32[64,1,4]{2,1,0:T(1,128)} %bitcast.39), calls=%async_computation.3 | async-start | bytes 65536 | tf_op jit(solution)/shard_map/all_to_all | solution.py:130
  90.3 0.3 fusion.21
  90.7 11.8 %all-to-all-done.3 = s32[64,1,4]{2,1,0:T(1,128)S(1)} async-done(((s32[64,1,4]{2,1,0:T(1,128)}), s32[64,1,4]{2,1,0:T(1,128)S(1)}, u32[]{:S(2)}, u32[]{:S(2)}) %all-to-all-start.3) | async-done | bytes 1056 | tf_op jit(solution)/shard_map/all_to_all | solution.py:130
  102.5 0.5 broadcast.144
  103.1 0.7 reduce.3
  104.6 0.8 fusion.2
  105.4 46.5 %all_to_all.29 = bf16[64,16,384]{2,1,0:T(8,128)(2,1)S(1)} all-to-all(bf16[64,16,384]{2,1,0:T(8,128)(2,1)S(1)} %bitcast.137), channel_id=1, replica_groups=mesh['seq'=64,'head'=8] {'seq'}, dimensions={0} | all-to-all | bytes 1572864 | tf_op jit(solution)/shard_map/all_to_all | solution.py:149
  152.1 0.4 fusion.6
  152.6 0.9 copy.86
  (67 shorter events, 3.6 us)
Async XLA Ops:
  0.0 9.9 %copy-start.2 = (f32[512]{0:T(512)S(1)}, f32[512]{0:T(512)}, u32[]{:S(2)}) copy-start(f32[512]{0:T(512)} %param.11) | copy-start | bytes 6148
  0.0 10.0 %copy-start = (bf16[128,512]{1,0:T(8,128)(2,1)S(1)}, bf16[128,512]{1,0:T(8,128)(2,1)}, u32[]{:S(2)}) copy-start(bf16[128,512]{1,0:T(8,128)(2,1)} %param.10) | copy-start | bytes 393220
  0.0 10.0 %copy-start.1 = (bf16[128,512]{1,0:T(8,128)(2,1)S(1)}, bf16[128,512]{1,0:T(8,128)(2,1)}, u32[]{:S(2)}) copy-start(bf16[128,512]{1,0:T(8,128)(2,1)} %param.7) | copy-start | bytes 393220
  4.0 15.2 %all-to-all-start = ((bf16[4,272,128]{2,1,0:T(8,128)(2,1)}), bf16[4,272,128]{2,1,0:T(8,128)(2,1)S(1)}, u32[]{:S(2)}, u32[]{:S(2)}) async-start(bf16[4,272,128]{2,1,0:T(8,128)(2,1)} %pad_maximum_fusion.1), calls=%async_computation | async-start | bytes 557056 | tf_op jit(solution)/shard_map/all_to_all | solution.py:47
  19.6 21.8 %collective-permute-start.1 = (bf16[144,128]{1,0:T(8,128)(2,1)S(1)}, bf16[144,128]{1,0:T(8,128)(2,1)S(1)}, u32[]{:S(2)}, u32[]{:S(2)}) collective-permute-start(bf16[144,128]{1,0:T(8,128)(2,1)S(1)} %pad_maximum_fusion.2), channel_id=1, source_target_pairs={{0,64},{8,72},{16,80},{24,88},{32,96},{40,104},{48,112},{56,120},{... | collective-permute-start | bytes 110600 | tf_op jit(solution)/shard_map/ppermute | solution.py:76
  33.1 10.7 %collective-permute-start = (bf16[144,128]{1,0:T(8,128)(2,1)S(1)}, bf16[144,128]{1,0:T(8,128)(2,1)S(1)}, u32[]{:S(2)}, u32[]{:S(2)}) collective-permute-start(bf16[144,128]{1,0:T(8,128)(2,1)S(1)} %pad_maximum_fusion.2), channel_id=1, source_target_pairs={{0,32},{8,40},{16,48},{24,56},{32,64},{40,72},{48,80},{56,88},{64,... | collective-permute-start | bytes 110600 | tf_op jit(solution)/shard_map/ppermute | solution.py:76
  37.8 10.2 %all-to-all-start.1 = ((bf16[4,256,128]{2,1,0:T(8,128)(2,1)}), bf16[4,256,128]{2,1,0:T(8,128)(2,1)S(1)}, u32[]{:S(2)}, u32[]{:S(2)}) async-start(bf16[4,256,128]{2,1,0:T(8,128)(2,1)} %maximum_maximum_fusion), calls=%async_computation.1 | async-start | bytes 524288 | tf_op jit(solution)/shard_map/all_to_all | solution.py:47
  49.4 15.2 %all-to-all-start.2 = ((f32[32,8,128]{2,1,0:T(8,128)}), f32[32,8,128]{2,1,0:T(8,128)S(1)}, u32[]{:S(2)}, u32[]{:S(2)}) async-start(f32[32,8,128]{2,1,0:T(8,128)} %broadcast_in_dim.285), calls=%async_computation.2 | async-start | bytes 262144 | tf_op jit(solution)/shard_map/all_to_all | solution.py:109
  65.2 38.8 %collective-permute-start.3 = (bf16[144,128]{1,0:T(8,128)(2,1)S(1)}, bf16[144,128]{1,0:T(8,128)(2,1)S(1)}, u32[]{:S(2)}, u32[]{:S(2)}) collective-permute-start(bf16[144,128]{1,0:T(8,128)(2,1)S(1)} %pad_maximum_fusion.3), channel_id=1, source_target_pairs={{64,0},{72,8},{80,16},{88,24},{96,32},{104,40},{112,48},{120,56},{... | collective-permute-start | bytes 110600 | tf_op jit(solution)/shard_map/ppermute | solution.py:76
  71.9 32.1 %collective-permute-start.2 = (bf16[144,128]{1,0:T(8,128)(2,1)S(1)}, bf16[144,128]{1,0:T(8,128)(2,1)S(1)}, u32[]{:S(2)}, u32[]{:S(2)}) collective-permute-start(bf16[144,128]{1,0:T(8,128)(2,1)S(1)} %pad_maximum_fusion.3), channel_id=1, source_target_pairs={{32,0},{40,8},{48,16},{56,24},{64,32},{72,40},{80,48},{88,56},{96,... | collective-permute-start | bytes 110600 | tf_op jit(solution)/shard_map/ppermute | solution.py:76
  76.6 25.9 %all-to-all-start.3 = ((s32[64,1,4]{2,1,0:T(1,128)}), s32[64,1,4]{2,1,0:T(1,128)S(1)}, u32[]{:S(2)}, u32[]{:S(2)}) async-start(s32[64,1,4]{2,1,0:T(1,128)} %bitcast.39), calls=%async_computation.3 | async-start | bytes 65536 | tf_op jit(solution)/shard_map/all_to_all | solution.py:130

commit v3 on v2

--- a/solution.py
+++ b/solution.py
@@ -7,6 +7,7 @@
 HS = 128
 EPSILON = 1e-05
 SUB = 4
+WIDE = 32
 EXTRA = 16
 
 
@@ -35,13 +36,10 @@
     blocks = jnp.arange(SUB)
 
     owner = home // tok_rows
-    target_row = home % tok_rows
     same_owner = owner[:, None] == owner[None, :]
     ranks = jnp.sum(jnp.where(same_owner & (places[:, None] < places[None, :]), 1, 0), axis=0)
-    local_slot = owner * capacity + ranks
-    slot_match = local_slot[None, :] == jnp.arange(seq_count * capacity)[:, None]
-    row_index = jnp.max(jnp.where(slot_match, target_row[None, :], -1), axis=1)
-    row_index = row_index.reshape(seq_count, capacity)
+    (homes,) = together(jnp.broadcast_to(home[None], (WIDE, tok_rows)))
+    homes = lax.all_gather(homes, "seq")
 
     def regroup(array):
         return lax.all_to_all(array, "seq", 0, 0, tiled=True, axis_index_groups=groups)
@@ -126,8 +124,16 @@
 
     slot = (small[:, 1] * slots + small[:, 2] + (blocks * capacity)[:, None]).reshape(-1)
     place = slot[None, :] == jnp.arange(seq_count * slots)[:, None].astype(jnp.float32)
-    row_index, grad_query = together(row_index, grad_query)
-    index = lax.all_to_all(row_index, "seq", 0, 0, tiled=True)
+    (homes,) = together(homes)
+    homes = homes[:, 0]
+    to_me = homes // tok_rows == lax.axis_index("seq")
+    order = jnp.dot(
+        to_me.astype(jnp.bfloat16),
+        (places[:, None] < places[None, :]).astype(jnp.bfloat16),
+        preferred_element_type=jnp.float32,
+    )
+    taken = to_me[:, None] & (order[:, None] == jnp.arange(capacity)[:, None].astype(jnp.float32))
+    index = jnp.max(jnp.where(taken, (homes % tok_rows)[:, None], -1), axis=-1)
     choose = index.reshape(-1)[None, :] == places[:, None]
     choose = choose.astype(jnp.bfloat16).reshape(tok_rows, seq_count // SUB, slots)
 

time: 154 us -> 226 us (1.47)
  waiting for transfers between devices: 34.4 us -> 109 us
  between operations: 0.44 us -> 13.8 us
  starting transfers between devices: 57.6 us -> 45.9 us
  blocking collectives: 46.5 us -> 39.3 us
    all_gather x0 -> x1, waiting for transfers between devices: none -> 89 us  [local(): homes = lax.all_gather(homes, 'seq')]
    all_to_all x1 -> x0, starting transfers between devices: 13.4 us -> none  [local(): index = lax.all_to_all(row_index, 'seq', 0, 0, tiled=True)]
    all_to_all x1 -> x0, waiting for transfers between devices: 11.8 us -> none  [local(): index = lax.all_to_all(row_index, 'seq', 0, 0, tiled=True)]
    all_to_all x1, waiting for transfers between devices: 7.79 us -> 0.01 us  [local(): lax.all_to_all(sums, ('seq', 'head'), 0, 0, tiled=True, axis_index_groups...]
    all_to_all x1, blocking collectives: 46.5 us -> 39.3 us  [local(): lax.all_to_all(packed.reshape(seq_count, slots, 3 * HS), 'seq', 0, 0, til...]
    ppermute x4, waiting for transfers between devices: 2.44 us -> 7.93 us  [exchange(): pieces.append(lax.ppermute(payload, 'seq', pairs))]
  transfers between devices with their start and end apart: 8 -> 8, of which waited for: 5 -> 6; matrix products, arithmetic and copies ran while one was open for 3% -> 5% of each run, Pallas kernels for 0% -> 0%
where the time goes in v3:
time: 226 us; the launch traced here: 225 us
  waiting for transfers between devices  109 us (48%)
  starting transfers between devices  45.9 us (20%)
  blocking collectives  39.3 us (17%)
  between operations  13.8 us (6%)
  other arithmetic  6.21 us (3%)
  local copies, waits for them, and re-layouts  5.34 us (2%)
  matrix products  4.89 us (2%)
    all_gather x1, waiting for transfers between devices, local(): homes = lax.all_gather(homes, 'seq')  89 us
    all_to_all x1, blocking collectives, local(): lax.all_to_all(packed.reshape(seq_count, slots, 3 * HS), 'seq', 0, 0, til...  39.3 us
    ppermute x4, starting transfers between devices, exchange(): pieces.append(lax.ppermute(payload, 'seq', pairs))  30.1 us
    all_to_all x2, waiting for transfers between devices, regroup(): lax.all_to_all(array, 'seq', 0, 0, tiled=True, axis_index_groups=groups)  12.2 us
    all_to_all x2, starting transfers between devices, regroup(): lax.all_to_all(array, 'seq', 0, 0, tiled=True, axis_index_groups=groups)  9.3 us
    ppermute x4, waiting for transfers between devices, exchange(): pieces.append(lax.ppermute(payload, 'seq', pairs))  7.93 us
    all_to_all x1, starting transfers between devices, local(): lax.all_to_all(sums, ('seq', 'head'), 0, 0, tiled=True, axis_index_groups...  6.46 us
  transfers between devices with their start and end apart: 8, of which 6 were waited for; matrix products, arithmetic and copies ran while one was open for 5% of the time, Pallas kernels for 0%

profile of v3, /device:TPU:6, one launch (start us, length us, event | category | flops | bytes accessed | tf_op | source)
XLA Modules:
  0.0 224.7 jit_solution(13377815444935633034)
XLA Ops:
  6.5 1.3 broadcast_in_dim.306
  7.9 0.7 convert_bitcast_fusion.3
  8.5 0.8 select_reduce_fusion.3
  9.4 0.7 convert_bitcast_fusion.1
  10.2 0.9 slice_bitcast_fusion.11
  11.1 0.7 pad_maximum_fusion.1
  11.8 5.9 %all-to-all-start = ((bf16[4,272,128]{2,1,0:T(8,128)(2,1)}), bf16[4,272,128]{2,1,0:T(8,128)(2,1)S(1)}, u32[]{:S(2)}, u32[]{:S(2)}) async-start(bf16[4,272,128]{2,1,0:T(8,128)(2,1)} %pad_maximum_fusion.1), calls=%async_computation | async-start | bytes 557056 | tf_op jit(solution)/shard_map/all_to_all | solution.py:45
  18.0 0.7 maximum_maximum_fusion
  18.7 8.3 %all-to-all-done = bf16[4,272,128]{2,1,0:T(8,128)(2,1)S(1)} async-done(((bf16[4,272,128]{2,1,0:T(8,128)(2,1)}), bf16[4,272,128]{2,1,0:T(8,128)(2,1)S(1)}, u32[]{:S(2)}, u32[]{:S(2)}) %all-to-all-start) | async-done | bytes 278560 | tf_op jit(solution)/shard_map/all_to_all | solution.py:45
  27.0 0.3 fusion.16
  27.4 13.5 %collective-permute-start.1 = (bf16[144,128]{1,0:T(8,128)(2,1)S(1)}, bf16[144,128]{1,0:T(8,128)(2,1)S(1)}, u32[]{:S(2)}, u32[]{:S(2)}) collective-permute-start(bf16[144,128]{1,0:T(8,128)(2,1)S(1)} %pad_maximum_fusion.2), channel_id=1, source_target_pairs={{0,64},{8,72},{16,80},{24,88},{32,96},{40,104},{48,112},{56,120},{... | collective-permute-start | bytes 110600 | tf_op jit(solution)/shard_map/ppermute | solution.py:74
  41.0 4.3 %collective-permute-start = (bf16[144,128]{1,0:T(8,128)(2,1)S(1)}, bf16[144,128]{1,0:T(8,128)(2,1)S(1)}, u32[]{:S(2)}, u32[]{:S(2)}) collective-permute-start(bf16[144,128]{1,0:T(8,128)(2,1)S(1)} %pad_maximum_fusion.2), channel_id=1, source_target_pairs={{0,32},{8,40},{16,48},{24,56},{32,64},{40,72},{48,80},{56,88},{64,... | collective-permute-start | bytes 110600 | tf_op jit(solution)/shard_map/ppermute | solution.py:74
  45.3 0.3 fusion.25
  45.6 3.4 %all-to-all-start.1 = ((bf16[4,256,128]{2,1,0:T(8,128)(2,1)}), bf16[4,256,128]{2,1,0:T(8,128)(2,1)S(1)}, u32[]{:S(2)}, u32[]{:S(2)}) async-start(bf16[4,256,128]{2,1,0:T(8,128)(2,1)} %maximum_maximum_fusion), calls=%async_computation.1 | async-start | bytes 524288 | tf_op jit(solution)/shard_map/all_to_all | solution.py:45
  49.3 2.4 %collective-permute-done = bf16[144,128]{1,0:T(8,128)(2,1)S(1)} collective-permute-done((bf16[144,128]{1,0:T(8,128)(2,1)S(1)}, bf16[144,128]{1,0:T(8,128)(2,1)S(1)}, u32[]{:S(2)}, u32[]{:S(2)}) %collective-permute-start) | collective-permute-done | bytes 36896 | tf_op jit(solution)/shard_map/ppermute | solution.py:74
  51.8 3.9 %all-to-all-done.1 = bf16[4,256,128]{2,1,0:T(8,128)(2,1)S(1)} async-done(((bf16[4,256,128]{2,1,0:T(8,128)(2,1)}), bf16[4,256,128]{2,1,0:T(8,128)(2,1)S(1)}, u32[]{:S(2)}, u32[]{:S(2)}) %all-to-all-start.1) | async-done | bytes 262176 | tf_op jit(solution)/shard_map/all_to_all | solution.py:45
  56.2 0.4 multiply_reduce_fusion.1
  56.5 0.7 broadcast_in_dim.295
  57.2 6.5 %all-to-all-start.2 = ((f32[32,8,128]{2,1,0:T(8,128)}), f32[32,8,128]{2,1,0:T(8,128)S(1)}, u32[]{:S(2)}, u32[]{:S(2)}) async-start(f32[32,8,128]{2,1,0:T(8,128)} %broadcast_in_dim.295), calls=%async_computation.2 | async-start | bytes 262144 | tf_op jit(solution)/shard_map/all_to_all | solution.py:107
  63.7 89.0 %all-gather.3.cloned.1.call-done = s32[2048,128]{1,0:T(8,128)} async-done(((s32[32,128]{1,0:T(8,128)}), s32[2048,128]{1,0:T(8,128)}) %all-gather.3.cloned.1.call-update) | async-done | bytes 1048592 | tf_op jit(solution)/shard_map/all_gather | solution.py:42
  152.7 1.0 slice.182
  153.7 1.1 fusion.63
  155.8 0.3 fusion.17
  156.2 8.9 %collective-permute-start.3 = (bf16[144,128]{1,0:T(8,128)(2,1)S(1)}, bf16[144,128]{1,0:T(8,128)(2,1)S(1)}, u32[]{:S(2)}, u32[]{:S(2)}) collective-permute-start(bf16[144,128]{1,0:T(8,128)(2,1)S(1)} %pad_maximum_fusion.3), channel_id=1, source_target_pairs={{64,0},{72,8},{80,16},{88,24},{96,32},{104,40},{112,48},{120,56},{... | collective-permute-start | bytes 110600 | tf_op jit(solution)/shard_map/ppermute | solution.py:74
  165.1 3.4 %collective-permute-start.2 = (bf16[144,128]{1,0:T(8,128)(2,1)S(1)}, bf16[144,128]{1,0:T(8,128)(2,1)S(1)}, u32[]{:S(2)}, u32[]{:S(2)}) collective-permute-start(bf16[144,128]{1,0:T(8,128)(2,1)S(1)} %pad_maximum_fusion.3), channel_id=1, source_target_pairs={{32,0},{40,8},{48,16},{56,24},{64,32},{72,40},{80,48},{88,56},{96,... | collective-permute-start | bytes 110600 | tf_op jit(solution)/shard_map/ppermute | solution.py:74
  169.6 0.3 fusion.21
  170.0 0.7 collective-permute-done.3
  170.8 4.8 %collective-permute-done.2 = bf16[144,128]{1,0:T(8,128)(2,1)S(1)} collective-permute-done((bf16[144,128]{1,0:T(8,128)(2,1)S(1)}, bf16[144,128]{1,0:T(8,128)(2,1)S(1)}, u32[]{:S(2)}, u32[]{:S(2)}) %collective-permute-start.2) | collective-permute-done | bytes 36896 | tf_op jit(solution)/shard_map/ppermute | solution.py:74
  176.1 0.8 fusion.2
  176.9 39.3 %all_to_all.20 = bf16[64,16,384]{2,1,0:T(8,128)(2,1)S(1)} all-to-all(bf16[64,16,384]{2,1,0:T(8,128)(2,1)S(1)} %bitcast.140), channel_id=1, replica_groups=mesh['seq'=64,'head'=8] {'seq'}, dimensions={0} | all-to-all | bytes 1572864 | tf_op jit(solution)/shard_map/all_to_all | solution.py:155
  216.4 0.4 fusion.6
  216.9 0.9 copy.97
  (73 shorter events, 4.1 us)
Async XLA Ops:
  6.5 11.3 %copy-start.2 = (f32[512]{0:T(512)S(1)}, f32[512]{0:T(512)}, u32[]{:S(2)}) copy-start(f32[512]{0:T(512)} %param.11) | copy-start | bytes 6148
  6.5 11.4 %copy-start = (bf16[128,512]{1,0:T(8,128)(2,1)S(1)}, bf16[128,512]{1,0:T(8,128)(2,1)}, u32[]{:S(2)}) copy-start(bf16[128,512]{1,0:T(8,128)(2,1)} %param.10) | copy-start | bytes 393220
  6.5 11.4 %copy-start.1 = (bf16[128,512]{1,0:T(8,128)(2,1)S(1)}, bf16[128,512]{1,0:T(8,128)(2,1)}, u32[]{:S(2)}) copy-start(bf16[128,512]{1,0:T(8,128)(2,1)} %param.7) | copy-start | bytes 393220
  6.5 146.2 %all-gather.3.cloned.1.call-start = ((), (), s32[]{:S(2)}) async-start(), calls=%async_computation.4 | async-start | bytes 1064960 | tf_op jit(solution)/shard_map/all_gather | solution.py:42
  11.8 15.2 %all-to-all-start = ((bf16[4,272,128]{2,1,0:T(8,128)(2,1)}), bf16[4,272,128]{2,1,0:T(8,128)(2,1)S(1)}, u32[]{:S(2)}, u32[]{:S(2)}) async-start(bf16[4,272,128]{2,1,0:T(8,128)(2,1)} %pad_maximum_fusion.1), calls=%async_computation | async-start | bytes 557056 | tf_op jit(solution)/shard_map/all_to_all | solution.py:45
  27.4 21.8 %collective-permute-start.1 = (bf16[144,128]{1,0:T(8,128)(2,1)S(1)}, bf16[144,128]{1,0:T(8,128)(2,1)S(1)}, u32[]{:S(2)}, u32[]{:S(2)}) collective-permute-start(bf16[144,128]{1,0:T(8,128)(2,1)S(1)} %pad_maximum_fusion.2), channel_id=1, source_target_pairs={{0,64},{8,72},{16,80},{24,88},{32,96},{40,104},{48,112},{56,120},{... | collective-permute-start | bytes 110600 | tf_op jit(solution)/shard_map/ppermute | solution.py:74
  41.0 10.7 %collective-permute-start = (bf16[144,128]{1,0:T(8,128)(2,1)S(1)}, bf16[144,128]{1,0:T(8,128)(2,1)S(1)}, u32[]{:S(2)}, u32[]{:S(2)}) collective-permute-start(bf16[144,128]{1,0:T(8,128)(2,1)S(1)} %pad_maximum_fusion.2), channel_id=1, source_target_pairs={{0,32},{8,40},{16,48},{24,56},{32,64},{40,72},{48,80},{56,88},{64,... | collective-permute-start | bytes 110600 | tf_op jit(solution)/shard_map/ppermute | solution.py:74
  45.6 10.2 %all-to-all-start.1 = ((bf16[4,256,128]{2,1,0:T(8,128)(2,1)}), bf16[4,256,128]{2,1,0:T(8,128)(2,1)S(1)}, u32[]{:S(2)}, u32[]{:S(2)}) async-start(bf16[4,256,128]{2,1,0:T(8,128)(2,1)} %maximum_maximum_fusion), calls=%async_computation.1 | async-start | bytes 524288 | tf_op jit(solution)/shard_map/all_to_all | solution.py:45
  57.2 98.3 %all-to-all-start.2 = ((f32[32,8,128]{2,1,0:T(8,128)}), f32[32,8,128]{2,1,0:T(8,128)S(1)}, u32[]{:S(2)}, u32[]{:S(2)}) async-start(f32[32,8,128]{2,1,0:T(8,128)} %broadcast_in_dim.295), calls=%async_computation.2 | async-start | bytes 262144 | tf_op jit(solution)/shard_map/all_to_all | solution.py:107
  156.2 14.6 %collective-permute-start.3 = (bf16[144,128]{1,0:T(8,128)(2,1)S(1)}, bf16[144,128]{1,0:T(8,128)(2,1)S(1)}, u32[]{:S(2)}, u32[]{:S(2)}) collective-permute-start(bf16[144,128]{1,0:T(8,128)(2,1)S(1)} %pad_maximum_fusion.3), channel_id=1, source_target_pairs={{64,0},{72,8},{80,16},{88,24},{96,32},{104,40},{112,48},{120,56},{... | collective-permute-start | bytes 110600 | tf_op jit(solution)/shard_map/ppermute | solution.py:74
  165.1 10.4 %collective-permute-start.2 = (bf16[144,128]{1,0:T(8,128)(2,1)S(1)}, bf16[144,128]{1,0:T(8,128)(2,1)S(1)}, u32[]{:S(2)}, u32[]{:S(2)}) collective-permute-start(bf16[144,128]{1,0:T(8,128)(2,1)S(1)} %pad_maximum_fusion.3), channel_id=1, source_target_pairs={{32,0},{40,8},{48,16},{56,24},{64,32},{72,40},{80,48},{88,56},{96,... | collective-permute-start | bytes 110600 | tf_op jit(solution)/shard_map/ppermute | solution.py:74
Sparse Core Ops, SparseCore 0:
  10.3 142.3 all-gather.2

commit v4 on v2

--- a/solution.py
+++ b/solution.py
@@ -38,10 +38,6 @@
     target_row = home % tok_rows
     same_owner = owner[:, None] == owner[None, :]
     ranks = jnp.sum(jnp.where(same_owner & (places[:, None] < places[None, :]), 1, 0), axis=0)
-    local_slot = owner * capacity + ranks
-    slot_match = local_slot[None, :] == jnp.arange(seq_count * capacity)[:, None]
-    row_index = jnp.max(jnp.where(slot_match, target_row[None, :], -1), axis=1)
-    row_index = row_index.reshape(seq_count, capacity)
 
     def regroup(array):
         return lax.all_to_all(array, "seq", 0, 0, tiled=True, axis_index_groups=groups)
@@ -50,8 +46,8 @@
     last_row = jnp.max(jnp.where(later, doc_ids[:, None], -1), axis=0)
     first_row = jnp.min(jnp.where(later, tok_rows, doc_ids[:, None]), axis=0, initial=tok_rows)
     first_row = jnp.minimum(first_row, doc_ids)
-    small = jnp.stack([doc_ids, owner, ranks, first_row, last_row]).astype(jnp.bfloat16)
-    small = jnp.pad(small, ((0, EXTRA - 5), (0, 0)))
+    small = jnp.stack([doc_ids, owner, ranks, first_row, last_row, target_row]).astype(jnp.bfloat16)
+    small = jnp.pad(small, ((0, EXTRA - 6), (0, 0)))
     small = jnp.broadcast_to(small[None], (SUB, EXTRA, tok_rows))
     key_value = regroup(jnp.concatenate([heads_first(keys), heads_first(values), small], axis=1))
     key = key_value[:, :tok_rows]
@@ -126,10 +122,14 @@
 
     slot = (small[:, 1] * slots + small[:, 2] + (blocks * capacity)[:, None]).reshape(-1)
     place = slot[None, :] == jnp.arange(seq_count * slots)[:, None].astype(jnp.float32)
-    row_index, grad_query = together(row_index, grad_query)
-    index = lax.all_to_all(row_index, "seq", 0, 0, tiled=True)
-    choose = index.reshape(-1)[None, :] == places[:, None]
-    choose = choose.astype(jnp.bfloat16).reshape(tok_rows, seq_count // SUB, slots)
+    peers = [[g * SUB + s for g in range(seq_count // SUB)] for s in range(SUB)]
+    peer_slot = jnp.arange(seq_count // SUB)[:, None] * SUB + lax.axis_index("seq") % SUB
+    peer_slot = (peer_slot * slots + jnp.arange(slots)[None, :]).astype(jnp.float32)
+    row = small[:, 5].reshape(-1)
+    row_index = jnp.max(jnp.where(slot == peer_slot[:, :, None], row, -1.0), axis=-1)
+    row_index, grad_query = together(row_index[:, None], grad_query)
+    index = lax.all_to_all(row_index, "seq", 0, 0, tiled=True, axis_index_groups=peers)[:, 0]
+    choose = (index[None] == places[:, None, None].astype(jnp.float32)).astype(jnp.bfloat16)
 
     carry = entering(pieces, own, last, first, blocks[:, None] < blocks[None, :])
     grad_keys = mixed(back, quer, "bts,bta->bsa") + jnp.where(

time: 154 us -> 152 us (0.987)
  no operation moved by 1% of the time
where the time goes in v4:
time: 152 us; the launch traced here: 151 us
  starting transfers between devices  56.8 us (37%)
  blocking collectives  46.2 us (30%)
  waiting for transfers between devices  34.6 us (23%)
  other arithmetic  5.69 us (4%)
  matrix products  4.71 us (3%)
  local copies, waits for them, and re-layouts  2.89 us (2%)
    all_to_all x1, blocking collectives, local(): lax.all_to_all(packed.reshape(seq_count, slots, 3 * HS), 'seq', 0, 0, til...  46.2 us
    ppermute x4, starting transfers between devices, exchange(): pieces.append(lax.ppermute(payload, 'seq', pairs))  28.4 us
    all_to_all x1, starting transfers between devices, local(): lax.all_to_all(row_index, 'seq', 0, 0, tiled=True, axis_index_groups=peers)  12.7 us
    all_to_all x2, waiting for transfers between devices, regroup(): lax.all_to_all(array, 'seq', 0, 0, tiled=True, axis_index_groups=groups)  12.2 us
    all_to_all x1, waiting for transfers between devices, local(): lax.all_to_all(row_index, 'seq', 0, 0, tiled=True, axis_index_groups=peers)  12.1 us
    all_to_all x2, starting transfers between devices, regroup(): lax.all_to_all(array, 'seq', 0, 0, tiled=True, axis_index_groups=groups)  9.3 us
    all_to_all x1, waiting for transfers between devices, local(): lax.all_to_all(sums, ('seq', 'head'), 0, 0, tiled=True, axis_index_groups...  7.82 us
    all_to_all x1, starting transfers between devices, local(): lax.all_to_all(sums, ('seq', 'head'), 0, 0, tiled=True, axis_index_groups...  6.47 us
  transfers between devices with their start and end apart: 8, of which 5 were waited for; matrix products, arithmetic and copies ran while one was open for 3% of the time, Pallas kernels for 0%

profile of v4, /device:TPU:6, one launch (start us, length us, event | category | flops | bytes accessed | tf_op | source)
XLA Modules:
  0.0 151.5 jit_solution(17915773874845079546)
XLA Ops:
  0.0 0.8 select_reduce_fusion.3
  0.8 0.7 convert_bitcast_fusion.3
  1.6 0.7 convert_bitcast_fusion.1
  2.4 0.9 slice_bitcast_fusion.11
  3.3 0.7 pad_maximum_fusion.1
  4.0 5.9 %all-to-all-start = ((bf16[4,272,128]{2,1,0:T(8,128)(2,1)}), bf16[4,272,128]{2,1,0:T(8,128)(2,1)S(1)}, u32[]{:S(2)}, u32[]{:S(2)}) async-start(bf16[4,272,128]{2,1,0:T(8,128)(2,1)} %pad_maximum_fusion.1), calls=%async_computation | async-start | bytes 557056 | tf_op jit(solution)/shard_map/all_to_all | solution.py:43
  10.1 0.7 maximum_maximum_fusion
  10.9 8.3 %all-to-all-done = bf16[4,272,128]{2,1,0:T(8,128)(2,1)S(1)} async-done(((bf16[4,272,128]{2,1,0:T(8,128)(2,1)}), bf16[4,272,128]{2,1,0:T(8,128)(2,1)S(1)}, u32[]{:S(2)}, u32[]{:S(2)}) %all-to-all-start) | async-done | bytes 278560 | tf_op jit(solution)/shard_map/all_to_all | solution.py:43
  19.2 0.3 fusion.16
  19.6 13.5 %collective-permute-start.1 = (bf16[144,128]{1,0:T(8,128)(2,1)S(1)}, bf16[144,128]{1,0:T(8,128)(2,1)S(1)}, u32[]{:S(2)}, u32[]{:S(2)}) collective-permute-start(bf16[144,128]{1,0:T(8,128)(2,1)S(1)} %pad_maximum_fusion.2), channel_id=1, source_target_pairs={{0,64},{8,72},{16,80},{24,88},{32,96},{40,104},{48,112},{56,120},{... | collective-permute-start | bytes 110600 | tf_op jit(solution)/shard_map/ppermute | solution.py:72
  33.1 4.3 %collective-permute-start = (bf16[144,128]{1,0:T(8,128)(2,1)S(1)}, bf16[144,128]{1,0:T(8,128)(2,1)S(1)}, u32[]{:S(2)}, u32[]{:S(2)}) collective-permute-start(bf16[144,128]{1,0:T(8,128)(2,1)S(1)} %pad_maximum_fusion.2), channel_id=1, source_target_pairs={{0,32},{8,40},{16,48},{24,56},{32,64},{40,72},{48,80},{56,88},{64,... | collective-permute-start | bytes 110600 | tf_op jit(solution)/shard_map/ppermute | solution.py:72
  37.4 0.3 fusion.25
  37.8 3.4 %all-to-all-start.1 = ((bf16[4,256,128]{2,1,0:T(8,128)(2,1)}), bf16[4,256,128]{2,1,0:T(8,128)(2,1)S(1)}, u32[]{:S(2)}, u32[]{:S(2)}) async-start(bf16[4,256,128]{2,1,0:T(8,128)(2,1)} %maximum_maximum_fusion), calls=%async_computation.1 | async-start | bytes 524288 | tf_op jit(solution)/shard_map/all_to_all | solution.py:43
  41.4 2.4 %collective-permute-done = bf16[144,128]{1,0:T(8,128)(2,1)S(1)} collective-permute-done((bf16[144,128]{1,0:T(8,128)(2,1)S(1)}, bf16[144,128]{1,0:T(8,128)(2,1)S(1)}, u32[]{:S(2)}, u32[]{:S(2)}) %collective-permute-start) | collective-permute-done | bytes 36896 | tf_op jit(solution)/shard_map/ppermute | solution.py:72
  43.9 4.0 %all-to-all-done.1 = bf16[4,256,128]{2,1,0:T(8,128)(2,1)S(1)} async-done(((bf16[4,256,128]{2,1,0:T(8,128)(2,1)}), bf16[4,256,128]{2,1,0:T(8,128)(2,1)S(1)}, u32[]{:S(2)}, u32[]{:S(2)}) %all-to-all-start.1) | async-done | bytes 262176 | tf_op jit(solution)/shard_map/all_to_all | solution.py:43
  48.3 0.4 multiply_reduce_fusion.1
  48.7 0.7 broadcast_in_dim.285
  49.4 6.5 %all-to-all-start.2 = ((f32[32,8,128]{2,1,0:T(8,128)}), f32[32,8,128]{2,1,0:T(8,128)S(1)}, u32[]{:S(2)}, u32[]{:S(2)}) async-start(f32[32,8,128]{2,1,0:T(8,128)} %broadcast_in_dim.285), calls=%async_computation.2 | async-start | bytes 262144 | tf_op jit(solution)/shard_map/all_to_all | solution.py:105
  55.9 0.8 select_reduce_fusion.2
  56.7 7.8 %all-to-all-done.2 = f32[32,8,128]{2,1,0:T(8,128)S(1)} async-done(((f32[32,8,128]{2,1,0:T(8,128)}), f32[32,8,128]{2,1,0:T(8,128)S(1)}, u32[]{:S(2)}, u32[]{:S(2)}) %all-to-all-start.2) | async-done | bytes 131104 | tf_op jit(solution)/shard_map/all_to_all | solution.py:105
  64.8 0.3 fusion.17
  65.2 6.7 %collective-permute-start.3 = (bf16[144,128]{1,0:T(8,128)(2,1)S(1)}, bf16[144,128]{1,0:T(8,128)(2,1)S(1)}, u32[]{:S(2)}, u32[]{:S(2)}) collective-permute-start(bf16[144,128]{1,0:T(8,128)(2,1)S(1)} %pad_maximum_fusion.3), channel_id=1, source_target_pairs={{64,0},{72,8},{80,16},{88,24},{96,32},{104,40},{112,48},{120,56},{... | collective-permute-start | bytes 110600 | tf_op jit(solution)/shard_map/ppermute | solution.py:72
  71.9 3.8 %collective-permute-start.2 = (bf16[144,128]{1,0:T(8,128)(2,1)S(1)}, bf16[144,128]{1,0:T(8,128)(2,1)S(1)}, u32[]{:S(2)}, u32[]{:S(2)}) collective-permute-start(bf16[144,128]{1,0:T(8,128)(2,1)S(1)} %pad_maximum_fusion.3), channel_id=1, source_target_pairs={{32,0},{40,8},{48,16},{56,24},{64,32},{72,40},{80,48},{88,56},{96,... | collective-permute-start | bytes 110600 | tf_op jit(solution)/shard_map/ppermute | solution.py:72
  75.7 0.2 fusion.70
  76.6 12.7 %all-to-all-start.3 = ((f32[16,1,16]{2,1,0:T(1,128)}), f32[16,1,16]{2,1,0:T(1,128)S(1)}, u32[]{:S(2)}, u32[]{:S(2)}) async-start(f32[16,1,16]{2,1,0:T(1,128)} %bitcast.41), calls=%async_computation.3 | async-start | bytes 16384 | tf_op jit(solution)/shard_map/all_to_all | solution.py:131
  89.5 0.3 fusion.21
  90.0 12.1 %all-to-all-done.3 = f32[16,1,16]{2,1,0:T(1,128)S(1)} async-done(((f32[16,1,16]{2,1,0:T(1,128)}), f32[16,1,16]{2,1,0:T(1,128)S(1)}, u32[]{:S(2)}, u32[]{:S(2)}) %all-to-all-start.3) | async-done | bytes 1056 | tf_op jit(solution)/shard_map/all_to_all | solution.py:131
  102.8 0.8 fusion.2
  103.6 46.2 %all_to_all.25 = bf16[64,16,384]{2,1,0:T(8,128)(2,1)S(1)} all-to-all(bf16[64,16,384]{2,1,0:T(8,128)(2,1)S(1)} %bitcast.140), channel_id=1, replica_groups=mesh['seq'=64,'head'=8] {'seq'}, dimensions={0} | all-to-all | bytes 1572864 | tf_op jit(solution)/shard_map/all_to_all | solution.py:149
  149.8 0.2 reshape.246
  150.1 0.4 fusion.6
  150.5 0.9 copy.85
  (66 shorter events, 3.0 us)
Async XLA Ops:
  0.0 10.0 %copy-start.2 = (f32[512]{0:T(512)S(1)}, f32[512]{0:T(512)}, u32[]{:S(2)}) copy-start(f32[512]{0:T(512)} %param.11) | copy-start | bytes 6148
  0.0 10.1 %copy-start = (bf16[128,512]{1,0:T(8,128)(2,1)S(1)}, bf16[128,512]{1,0:T(8,128)(2,1)}, u32[]{:S(2)}) copy-start(bf16[128,512]{1,0:T(8,128)(2,1)} %param.10) | copy-start | bytes 393220
  0.0 10.1 %copy-start.1 = (bf16[128,512]{1,0:T(8,128)(2,1)S(1)}, bf16[128,512]{1,0:T(8,128)(2,1)}, u32[]{:S(2)}) copy-start(bf16[128,512]{1,0:T(8,128)(2,1)} %param.7) | copy-start | bytes 393220
  4.0 15.2 %all-to-all-start = ((bf16[4,272,128]{2,1,0:T(8,128)(2,1)}), bf16[4,272,128]{2,1,0:T(8,128)(2,1)S(1)}, u32[]{:S(2)}, u32[]{:S(2)}) async-start(bf16[4,272,128]{2,1,0:T(8,128)(2,1)} %pad_maximum_fusion.1), calls=%async_computation | async-start | bytes 557056 | tf_op jit(solution)/shard_map/all_to_all | solution.py:43
  19.6 21.8 %collective-permute-start.1 = (bf16[144,128]{1,0:T(8,128)(2,1)S(1)}, bf16[144,128]{1,0:T(8,128)(2,1)S(1)}, u32[]{:S(2)}, u32[]{:S(2)}) collective-permute-start(bf16[144,128]{1,0:T(8,128)(2,1)S(1)} %pad_maximum_fusion.2), channel_id=1, source_target_pairs={{0,64},{8,72},{16,80},{24,88},{32,96},{40,104},{48,112},{56,120},{... | collective-permute-start | bytes 110600 | tf_op jit(solution)/shard_map/ppermute | solution.py:72
  33.1 10.7 %collective-permute-start = (bf16[144,128]{1,0:T(8,128)(2,1)S(1)}, bf16[144,128]{1,0:T(8,128)(2,1)S(1)}, u32[]{:S(2)}, u32[]{:S(2)}) collective-permute-start(bf16[144,128]{1,0:T(8,128)(2,1)S(1)} %pad_maximum_fusion.2), channel_id=1, source_target_pairs={{0,32},{8,40},{16,48},{24,56},{32,64},{40,72},{48,80},{56,88},{64,... | collective-permute-start | bytes 110600 | tf_op jit(solution)/shard_map/ppermute | solution.py:72
  37.8 10.2 %all-to-all-start.1 = ((bf16[4,256,128]{2,1,0:T(8,128)(2,1)}), bf16[4,256,128]{2,1,0:T(8,128)(2,1)S(1)}, u32[]{:S(2)}, u32[]{:S(2)}) async-start(bf16[4,256,128]{2,1,0:T(8,128)(2,1)} %maximum_maximum_fusion), calls=%async_computation.1 | async-start | bytes 524288 | tf_op jit(solution)/shard_map/all_to_all | solution.py:43
  49.4 15.2 %all-to-all-start.2 = ((f32[32,8,128]{2,1,0:T(8,128)}), f32[32,8,128]{2,1,0:T(8,128)S(1)}, u32[]{:S(2)}, u32[]{:S(2)}) async-start(f32[32,8,128]{2,1,0:T(8,128)} %broadcast_in_dim.285), calls=%async_computation.2 | async-start | bytes 262144 | tf_op jit(solution)/shard_map/all_to_all | solution.py:105
  65.2 37.0 %collective-permute-start.3 = (bf16[144,128]{1,0:T(8,128)(2,1)S(1)}, bf16[144,128]{1,0:T(8,128)(2,1)S(1)}, u32[]{:S(2)}, u32[]{:S(2)}) collective-permute-start(bf16[144,128]{1,0:T(8,128)(2,1)S(1)} %pad_maximum_fusion.3), channel_id=1, source_target_pairs={{64,0},{72,8},{80,16},{88,24},{96,32},{104,40},{112,48},{120,56},{... | collective-permute-start | bytes 110600 | tf_op jit(solution)/shard_map/ppermute | solution.py:72
  71.9 30.3 %collective-permute-start.2 = (bf16[144,128]{1,0:T(8,128)(2,1)S(1)}, bf16[144,128]{1,0:T(8,128)(2,1)S(1)}, u32[]{:S(2)}, u32[]{:S(2)}) collective-permute-start(bf16[144,128]{1,0:T(8,128)(2,1)S(1)} %pad_maximum_fusion.3), channel_id=1, source_target_pairs={{32,0},{40,8},{48,16},{56,24},{64,32},{72,40},{80,48},{88,56},{96,... | collective-permute-start | bytes 110600 | tf_op jit(solution)/shard_map/ppermute | solution.py:72
  76.6 25.5 %all-to-all-start.3 = ((f32[16,1,16]{2,1,0:T(1,128)}), f32[16,1,16]{2,1,0:T(1,128)S(1)}, u32[]{:S(2)}, u32[]{:S(2)}) async-start(f32[16,1,16]{2,1,0:T(1,128)} %bitcast.41), calls=%async_computation.3 | async-start | bytes 16384 | tf_op jit(solution)/shard_map/all_to_all | solution.py:131

commit v5 on v4

--- a/solution.py
+++ b/solution.py
@@ -120,16 +120,19 @@
     grad_query = grad_query.astype(jnp.bfloat16)
     own = mixed(jnp.where(first_rows, quer, zero), grad, "bta,btc->bac")
 
-    slot = (small[:, 1] * slots + small[:, 2] + (blocks * capacity)[:, None]).reshape(-1)
+    owners, ranks, row = (small[:, at].reshape(-1) for at in (1, 2, 5))
+    rank_slot = (small[:, 2] + (blocks * capacity)[:, None]).reshape(-1)
+    slot = owners * slots + rank_slot
     place = slot[None, :] == jnp.arange(seq_count * slots)[:, None].astype(jnp.float32)
-    peers = [[g * SUB + s for g in range(seq_count // SUB)] for s in range(SUB)]
-    peer_slot = jnp.arange(seq_count // SUB)[:, None] * SUB + lax.axis_index("seq") % SUB
-    peer_slot = (peer_slot * slots + jnp.arange(slots)[None, :]).astype(jnp.float32)
-    row = small[:, 5].reshape(-1)
-    row_index = jnp.max(jnp.where(slot == peer_slot[:, :, None], row, -1.0), axis=-1)
-    row_index, grad_query = together(row_index[:, None], grad_query)
-    index = lax.all_to_all(row_index, "seq", 0, 0, tiled=True, axis_index_groups=peers)[:, 0]
-    choose = (index[None] == places[:, None, None].astype(jnp.float32)).astype(jnp.bfloat16)
+    to_owner = owners[None, :] == jnp.arange(seq_count)[:, None].astype(jnp.float32)
+    at_slot = rank_slot[:, None] == jnp.arange(HS)[None, :].astype(jnp.float32)
+    index = jnp.dot(
+        to_owner.astype(jnp.bfloat16),
+        jnp.where(at_slot, row[:, None] + 1.0, 0.0).astype(jnp.bfloat16),
+        preferred_element_type=jnp.float32,
+    ).astype(jnp.bfloat16)
+    index = jnp.pad(index[:, None, None], ((0, 0), (0, 0), (0, 1), (0, 0)))
+    index, grad_query = together(index, grad_query)
 
     carry = entering(pieces, own, last, first, blocks[:, None] < blocks[None, :])
     grad_keys = mixed(back, quer, "bts,bta->bsa") + jnp.where(
@@ -145,12 +148,17 @@
     packed = jnp.dot(
         place.astype(jnp.bfloat16), rows, preferred_element_type=jnp.float32
     ).astype(jnp.bfloat16)
-    packed, choose = together(packed, choose)
-    received = lax.all_to_all(
-        packed.reshape(seq_count, slots, 3 * HS), "seq", 0, 0, tiled=True
-    )
-    received = received.reshape(seq_count // SUB, SUB, slots, 3, HS)
-    return mixed(choose, received, "rgk,gskjd->rjsd").astype(jnp.bfloat16).reshape(
+    halves = slots // 8
+    packed = packed.reshape(seq_count, halves, 8, 3, HS).transpose(0, 1, 3, 2, 4)
+    packed = packed.reshape(seq_count, halves * 12, 2, HS)
+    packed = jnp.concatenate([packed, index], axis=1)
+    packed, numbers = together(packed, (places + 1).astype(jnp.float32))
+    received = lax.all_to_all(packed, "seq", 0, 0, tiled=True)
+    index = received[::SUB, halves * 12, 0, :slots].astype(jnp.float32)
+    choose = (index[None] == numbers[:, None, None]).astype(jnp.bfloat16)
+    choose = choose.reshape(tok_rows, seq_count // SUB, halves, 8)
+    received = received[:, : halves * 12].reshape(seq_count // SUB, SUB, halves, 3, 8, HS)
+    return mixed(choose, received, "rghk,gshjkd->rjsd").astype(jnp.bfloat16).reshape(
         tok_rows, 3, width
     )
 

time: 152 us -> 143 us (0.941)
  starting transfers between devices: 56.8 us -> 44.2 us
  blocking collectives: 46.2 us -> 53.1 us
  waiting for transfers between devices: 34.6 us -> 30.1 us
    all_to_all x1 -> x0, starting transfers between devices: 12.7 us -> none  [local(): lax.all_to_all(row_index, 'seq', 0, 0, tiled=True, axis_index_groups=peers)]
    all_to_all x1 -> x0, waiting for transfers between devices: 12.1 us -> none  [local(): lax.all_to_all(row_index, 'seq', 0, 0, tiled=True, axis_index_groups=peers)]
    ppermute x4, waiting for transfers between devices: 2.44 us -> 9.55 us  [exchange(): pieces.append(lax.ppermute(payload, 'seq', pairs))]
    all_to_all x1, blocking collectives: 46.2 us -> 53.1 us  [local(): received = lax.all_to_all(packed, 'seq', 0, 0, tiled=True)]
  transfers between devices with their start and end apart: 8 -> 7, of which waited for: 5 -> 6; matrix products, arithmetic and copies ran while one was open for 3% -> 2% of each run, Pallas kernels for 0% -> 0%
where the time goes in v5:
time: 143 us; the launch traced here: 142 us
  blocking collectives  53.1 us (37%)
  starting transfers between devices  44.2 us (31%)
  waiting for transfers between devices  30.1 us (21%)
  other arithmetic  5.76 us (4%)
  matrix products  5.17 us (4%)
  local copies, waits for them, and re-layouts  3.47 us (2%)
    all_to_all x1, blocking collectives, local(): received = lax.all_to_all(packed, 'seq', 0, 0, tiled=True)  53.1 us
    ppermute x4, starting transfers between devices, exchange(): pieces.append(lax.ppermute(payload, 'seq', pairs))  28.4 us
    all_to_all x2, waiting for transfers between devices, regroup(): lax.all_to_all(array, 'seq', 0, 0, tiled=True, axis_index_groups=groups)  12.3 us
    ppermute x4, waiting for transfers between devices, exchange(): pieces.append(lax.ppermute(payload, 'seq', pairs))  9.55 us
    all_to_all x2, starting transfers between devices, regroup(): lax.all_to_all(array, 'seq', 0, 0, tiled=True, axis_index_groups=groups)  9.3 us
    all_to_all x1, waiting for transfers between devices, local(): lax.all_to_all(sums, ('seq', 'head'), 0, 0, tiled=True, axis_index_groups...  8.24 us
    all_to_all x1, starting transfers between devices, local(): lax.all_to_all(sums, ('seq', 'head'), 0, 0, tiled=True, axis_index_groups...  6.47 us
    dot_general x15, matrix products, mixed(): return jnp.einsum(form, left, right, preferred_element_type=jnp.float32)  4.06 us
  transfers between devices with their start and end apart: 7, of which 6 were waited for; matrix products, arithmetic and copies ran while one was open for 2% of the time, Pallas kernels for 0%

profile of v5, /device:TPU:6, one launch (start us, length us, event | category | flops | bytes accessed | tf_op | source)
XLA Modules:
  0.0 142.2 jit_solution(220032453309832428)
XLA Ops:
  0.0 0.8 select_reduce_fusion.2
  0.8 0.7 convert_bitcast_fusion.3
  1.5 0.7 convert_bitcast_fusion.1
  2.3 0.9 slice_bitcast_fusion.11
  3.3 0.7 pad_maximum_fusion.2
  4.0 5.9 %all-to-all-start = ((bf16[4,272,128]{2,1,0:T(8,128)(2,1)}), bf16[4,272,128]{2,1,0:T(8,128)(2,1)S(1)}, u32[]{:S(2)}, u32[]{:S(2)}) async-start(bf16[4,272,128]{2,1,0:T(8,128)(2,1)} %pad_maximum_fusion.2), calls=%async_computation | async-start | bytes 557056 | tf_op jit(solution)/shard_map/all_to_all | solution.py:43
  10.2 0.7 maximum_maximum_fusion
  10.9 8.3 %all-to-all-done = bf16[4,272,128]{2,1,0:T(8,128)(2,1)S(1)} async-done(((bf16[4,272,128]{2,1,0:T(8,128)(2,1)}), bf16[4,272,128]{2,1,0:T(8,128)(2,1)S(1)}, u32[]{:S(2)}, u32[]{:S(2)}) %all-to-all-start) | async-done | bytes 278560 | tf_op jit(solution)/shard_map/all_to_all | solution.py:43
  19.3 0.3 fusion.14
  19.6 13.5 %collective-permute-start.1 = (bf16[144,128]{1,0:T(8,128)(2,1)S(1)}, bf16[144,128]{1,0:T(8,128)(2,1)S(1)}, u32[]{:S(2)}, u32[]{:S(2)}) collective-permute-start(bf16[144,128]{1,0:T(8,128)(2,1)S(1)} %pad_maximum_fusion.3), channel_id=1, source_target_pairs={{0,64},{8,72},{16,80},{24,88},{32,96},{40,104},{48,112},{56,120},{... | collective-permute-start | bytes 110600 | tf_op jit(solution)/shard_map/ppermute | solution.py:72
  33.2 4.3 %collective-permute-start = (bf16[144,128]{1,0:T(8,128)(2,1)S(1)}, bf16[144,128]{1,0:T(8,128)(2,1)S(1)}, u32[]{:S(2)}, u32[]{:S(2)}) collective-permute-start(bf16[144,128]{1,0:T(8,128)(2,1)S(1)} %pad_maximum_fusion.3), channel_id=1, source_target_pairs={{0,32},{8,40},{16,48},{24,56},{32,64},{40,72},{48,80},{56,88},{64,... | collective-permute-start | bytes 110600 | tf_op jit(solution)/shard_map/ppermute | solution.py:72
  37.5 0.3 fusion.23
  37.8 3.4 %all-to-all-start.1 = ((bf16[4,256,128]{2,1,0:T(8,128)(2,1)}), bf16[4,256,128]{2,1,0:T(8,128)(2,1)S(1)}, u32[]{:S(2)}, u32[]{:S(2)}) async-start(bf16[4,256,128]{2,1,0:T(8,128)(2,1)} %maximum_maximum_fusion), calls=%async_computation.1 | async-start | bytes 524288 | tf_op jit(solution)/shard_map/all_to_all | solution.py:43
  41.4 2.4 %collective-permute-done = bf16[144,128]{1,0:T(8,128)(2,1)S(1)} collective-permute-done((bf16[144,128]{1,0:T(8,128)(2,1)S(1)}, bf16[144,128]{1,0:T(8,128)(2,1)S(1)}, u32[]{:S(2)}, u32[]{:S(2)}) %collective-permute-start) | collective-permute-done | bytes 36896 | tf_op jit(solution)/shard_map/ppermute | solution.py:72
  44.0 4.0 %all-to-all-done.1 = bf16[4,256,128]{2,1,0:T(8,128)(2,1)S(1)} async-done(((bf16[4,256,128]{2,1,0:T(8,128)(2,1)}), bf16[4,256,128]{2,1,0:T(8,128)(2,1)S(1)}, u32[]{:S(2)}, u32[]{:S(2)}) %all-to-all-start.1) | async-done | bytes 262176 | tf_op jit(solution)/shard_map/all_to_all | solution.py:43
  48.3 0.4 multiply_reduce_fusion.1
  48.7 0.7 broadcast_in_dim.290
  49.4 6.5 %all-to-all-start.2 = ((f32[32,8,128]{2,1,0:T(8,128)}), f32[32,8,128]{2,1,0:T(8,128)S(1)}, u32[]{:S(2)}, u32[]{:S(2)}) async-start(f32[32,8,128]{2,1,0:T(8,128)} %broadcast_in_dim.290), calls=%async_computation.2 | async-start | bytes 262144 | tf_op jit(solution)/shard_map/all_to_all | solution.py:105
  56.0 0.3 fusion.16
  56.3 8.2 %all-to-all-done.2 = f32[32,8,128]{2,1,0:T(8,128)S(1)} async-done(((f32[32,8,128]{2,1,0:T(8,128)}), f32[32,8,128]{2,1,0:T(8,128)S(1)}, u32[]{:S(2)}, u32[]{:S(2)}) %all-to-all-start.2) | async-done | bytes 131104 | tf_op jit(solution)/shard_map/all_to_all | solution.py:105
  64.8 0.3 fusion.15
  65.2 6.7 %collective-permute-start.3 = (bf16[144,128]{1,0:T(8,128)(2,1)S(1)}, bf16[144,128]{1,0:T(8,128)(2,1)S(1)}, u32[]{:S(2)}, u32[]{:S(2)}) collective-permute-start(bf16[144,128]{1,0:T(8,128)(2,1)S(1)} %pad_maximum_fusion.4), channel_id=1, source_target_pairs={{64,0},{72,8},{80,16},{88,24},{96,32},{104,40},{112,48},{120,56},{... | collective-permute-start | bytes 110600 | tf_op jit(solution)/shard_map/ppermute | solution.py:72
  71.9 3.8 %collective-permute-start.2 = (bf16[144,128]{1,0:T(8,128)(2,1)S(1)}, bf16[144,128]{1,0:T(8,128)(2,1)S(1)}, u32[]{:S(2)}, u32[]{:S(2)}) collective-permute-start(bf16[144,128]{1,0:T(8,128)(2,1)S(1)} %pad_maximum_fusion.4), channel_id=1, source_target_pairs={{32,0},{40,8},{48,16},{56,24},{64,32},{72,40},{80,48},{88,56},{96,... | collective-permute-start | bytes 110600 | tf_op jit(solution)/shard_map/ppermute | solution.py:72
  76.9 0.3 fusion.19
  77.3 2.4 %collective-permute-done.3 = bf16[144,128]{1,0:T(8,128)(2,1)S(1)} collective-permute-done((bf16[144,128]{1,0:T(8,128)(2,1)S(1)}, bf16[144,128]{1,0:T(8,128)(2,1)S(1)}, u32[]{:S(2)}, u32[]{:S(2)}) %collective-permute-start.3) | collective-permute-done | bytes 36896 | tf_op jit(solution)/shard_map/ppermute | solution.py:72
  79.8 4.7 %collective-permute-done.2 = bf16[144,128]{1,0:T(8,128)(2,1)S(1)} collective-permute-done((bf16[144,128]{1,0:T(8,128)(2,1)S(1)}, bf16[144,128]{1,0:T(8,128)(2,1)S(1)}, u32[]{:S(2)}, u32[]{:S(2)}) %collective-permute-start.2) | collective-permute-done | bytes 36896 | tf_op jit(solution)/shard_map/ppermute | solution.py:72
  85.0 0.8 fusion.2
  85.8 1.1 pad_maximum_fusion
  86.9 53.1 %all_to_all.20 = bf16[64,25,2,128]{3,2,1,0:T(2,128)(2,1)S(1)} all-to-all(bf16[64,25,2,128]{3,2,1,0:T(2,128)(2,1)S(1)} %pad_maximum_fusion), channel_id=1, replica_groups=mesh['seq'=64,'head'=8] {'seq'}, dimensions={0} | all-to-all | bytes 1638400 | tf_op jit(solution)/shard_map/all_to_all | solution.py:156
  140.2 0.5 slice.191
  140.7 0.5 convolution_bitcast_fusion
  141.3 0.9 copy.116
  (70 shorter events, 3.3 us)
Async XLA Ops:
  2.3 7.7 %copy-start.2 = (f32[512]{0:T(512)S(1)}, f32[512]{0:T(512)}, u32[]{:S(2)}) copy-start(f32[512]{0:T(512)} %param.11) | copy-start | bytes 6148
  2.3 7.8 %copy-start = (bf16[128,512]{1,0:T(8,128)(2,1)S(1)}, bf16[128,512]{1,0:T(8,128)(2,1)}, u32[]{:S(2)}) copy-start(bf16[128,512]{1,0:T(8,128)(2,1)} %param.10) | copy-start | bytes 393220
  2.3 7.8 %copy-start.1 = (bf16[128,512]{1,0:T(8,128)(2,1)S(1)}, bf16[128,512]{1,0:T(8,128)(2,1)}, u32[]{:S(2)}) copy-start(bf16[128,512]{1,0:T(8,128)(2,1)} %param.7) | copy-start | bytes 393220
  4.0 15.2 %all-to-all-start = ((bf16[4,272,128]{2,1,0:T(8,128)(2,1)}), bf16[4,272,128]{2,1,0:T(8,128)(2,1)S(1)}, u32[]{:S(2)}, u32[]{:S(2)}) async-start(bf16[4,272,128]{2,1,0:T(8,128)(2,1)} %pad_maximum_fusion.2), calls=%async_computation | async-start | bytes 557056 | tf_op jit(solution)/shard_map/all_to_all | solution.py:43
  19.6 21.8 %collective-permute-start.1 = (bf16[144,128]{1,0:T(8,128)(2,1)S(1)}, bf16[144,128]{1,0:T(8,128)(2,1)S(1)}, u32[]{:S(2)}, u32[]{:S(2)}) collective-permute-start(bf16[144,128]{1,0:T(8,128)(2,1)S(1)} %pad_maximum_fusion.3), channel_id=1, source_target_pairs={{0,64},{8,72},{16,80},{24,88},{32,96},{40,104},{48,112},{56,120},{... | collective-permute-start | bytes 110600 | tf_op jit(solution)/shard_map/ppermute | solution.py:72
  33.2 10.7 %collective-permute-start = (bf16[144,128]{1,0:T(8,128)(2,1)S(1)}, bf16[144,128]{1,0:T(8,128)(2,1)S(1)}, u32[]{:S(2)}, u32[]{:S(2)}) collective-permute-start(bf16[144,128]{1,0:T(8,128)(2,1)S(1)} %pad_maximum_fusion.3), channel_id=1, source_target_pairs={{0,32},{8,40},{16,48},{24,56},{32,64},{40,72},{48,80},{56,88},{64,... | collective-permute-start | bytes 110600 | tf_op jit(solution)/shard_map/ppermute | solution.py:72
  37.8 10.2 %all-to-all-start.1 = ((bf16[4,256,128]{2,1,0:T(8,128)(2,1)}), bf16[4,256,128]{2,1,0:T(8,128)(2,1)S(1)}, u32[]{:S(2)}, u32[]{:S(2)}) async-start(bf16[4,256,128]{2,1,0:T(8,128)(2,1)} %maximum_maximum_fusion), calls=%async_computation.1 | async-start | bytes 524288 | tf_op jit(solution)/shard_map/all_to_all | solution.py:43
  49.4 15.2 %all-to-all-start.2 = ((f32[32,8,128]{2,1,0:T(8,128)}), f32[32,8,128]{2,1,0:T(8,128)S(1)}, u32[]{:S(2)}, u32[]{:S(2)}) async-start(f32[32,8,128]{2,1,0:T(8,128)} %broadcast_in_dim.290), calls=%async_computation.2 | async-start | bytes 262144 | tf_op jit(solution)/shard_map/all_to_all | solution.py:105
  65.2 14.6 %collective-permute-start.3 = (bf16[144,128]{1,0:T(8,128)(2,1)S(1)}, bf16[144,128]{1,0:T(8,128)(2,1)S(1)}, u32[]{:S(2)}, u32[]{:S(2)}) collective-permute-start(bf16[144,128]{1,0:T(8,128)(2,1)S(1)} %pad_maximum_fusion.4), channel_id=1, source_target_pairs={{64,0},{72,8},{80,16},{88,24},{96,32},{104,40},{112,48},{120,56},{... | collective-permute-start | bytes 110600 | tf_op jit(solution)/shard_map/ppermute | solution.py:72
  71.9 12.5 %collective-permute-start.2 = (bf16[144,128]{1,0:T(8,128)(2,1)S(1)}, bf16[144,128]{1,0:T(8,128)(2,1)S(1)}, u32[]{:S(2)}, u32[]{:S(2)}) collective-permute-start(bf16[144,128]{1,0:T(8,128)(2,1)S(1)} %pad_maximum_fusion.4), channel_id=1, source_target_pairs={{32,0},{40,8},{48,16},{56,24},{64,32},{72,40},{80,48},{88,56},{96,... | collective-permute-start | bytes 110600 | tf_op jit(solution)/shard_map/ppermute | solution.py:72

commit v6 on v5

--- a/solution.py
+++ b/solution.py
@@ -1,13 +1,15 @@
 import jax
 import jax.numpy as jnp
 from jax import lax
+from jax.experimental import pallas as pl
+from jax.experimental.pallas import tpu as pltpu
 from jax.sharding import PartitionSpec as P
 
 HEADS = 32
 HS = 128
 EPSILON = 1e-05
 SUB = 4
-EXTRA = 16
+EXTRA = 8
 
 
 def mixed(left, right, form):
@@ -16,6 +18,30 @@
 
 def heads_first(array):
     return jnp.stack([array[:, at : at + HS] for at in range(0, array.shape[1], HS)])
+
+
+def prepare(key_ref, value_ref, doc_ref, home_ref, out_ref):
+    tok_rows = key_ref.shape[0]
+    for s in range(SUB):
+        out_ref[s, :tok_rows] = key_ref[:, s * HS : (s + 1) * HS]
+        out_ref[s, tok_rows : 2 * tok_rows] = value_ref[:, s * HS : (s + 1) * HS]
+    doc = doc_ref[...].astype(jnp.float32)
+    home = home_ref[...]
+    owner = lax.shift_right_logical(home, tok_rows.bit_length() - 1).astype(jnp.float32)
+    target_row = (home & (tok_rows - 1)).astype(jnp.float32)
+    across = jnp.broadcast_to(owner, (tok_rows, tok_rows))
+    above = lax.broadcasted_iota(jnp.int32, across.shape, 0)
+    along = lax.broadcasted_iota(jnp.int32, across.shape, 1)
+    earlier = (across == across.T) & (above < along)
+    ranks = jnp.sum(jnp.where(earlier, 1.0, 0.0), axis=0, keepdims=True)
+    first = jnp.min(doc, axis=1, keepdims=True)
+    last = jnp.max(doc, axis=1, keepdims=True)
+    line = lax.broadcasted_iota(jnp.int32, (EXTRA, tok_rows), 0)
+    small = jnp.zeros((EXTRA, tok_rows), jnp.float32)
+    for at, value in enumerate((doc, owner, ranks, first, last, target_row)):
+        small = jnp.where(line == at, value, small)
+    for s in range(SUB):
+        out_ref[s, 2 * tok_rows :] = small.astype(jnp.bfloat16)
 
 
 def together(*values):
@@ -34,22 +60,16 @@
     places = jnp.arange(tok_rows)
     blocks = jnp.arange(SUB)
 
-    owner = home // tok_rows
-    target_row = home % tok_rows
-    same_owner = owner[:, None] == owner[None, :]
-    ranks = jnp.sum(jnp.where(same_owner & (places[:, None] < places[None, :]), 1, 0), axis=0)
-
     def regroup(array):
         return lax.all_to_all(array, "seq", 0, 0, tiled=True, axis_index_groups=groups)
 
-    later = places[:, None] >= places[None, :]
-    last_row = jnp.max(jnp.where(later, doc_ids[:, None], -1), axis=0)
-    first_row = jnp.min(jnp.where(later, tok_rows, doc_ids[:, None]), axis=0, initial=tok_rows)
-    first_row = jnp.minimum(first_row, doc_ids)
-    small = jnp.stack([doc_ids, owner, ranks, first_row, last_row, target_row]).astype(jnp.bfloat16)
-    small = jnp.pad(small, ((0, EXTRA - 6), (0, 0)))
-    small = jnp.broadcast_to(small[None], (SUB, EXTRA, tok_rows))
-    key_value = regroup(jnp.concatenate([heads_first(keys), heads_first(values), small], axis=1))
+    key_value = pl.pallas_call(
+        prepare,
+        out_shape=jax.ShapeDtypeStruct((SUB, 2 * tok_rows + EXTRA, HS), jnp.bfloat16),
+        in_specs=[pl.BlockSpec(memory_space=pltpu.VMEM)] * 4,
+        out_specs=pl.BlockSpec(memory_space=pltpu.VMEM),
+    )(keys, values, doc_ids.reshape(1, -1), home.reshape(1, -1))
+    key_value = regroup(key_value)
     key = key_value[:, :tok_rows]
     value = key_value[:, tok_rows : 2 * tok_rows]
     small = key_value[:, 2 * tok_rows :].astype(jnp.float32)

time: 143 us -> 140 us (0.979)
  other arithmetic: 5.76 us -> 2.77 us
  Pallas kernels: 0 us -> 1.84 us
    pallas_call x0 -> x1, Pallas kernels: none -> 1.84 us  [local(): pl.pallas_call(prepare, out_shape=jax.ShapeDtypeStruct((SUB, 2 * tok_rows...]
where the time goes in v6:
time: 140 us
  blocking collectives  53.3 us (38%)
  starting transfers between devices  44.1 us (32%)
  waiting for transfers between devices  29.7 us (21%)
  matrix products  5.19 us (4%)
  other arithmetic  2.77 us (2%)
  local copies, waits for them, and re-layouts  2.47 us (2%)
  Pallas kernels  1.84 us (1%)
    all_to_all x1, blocking collectives, local(): received = lax.all_to_all(packed, 'seq', 0, 0, tiled=True)  53.3 us
    ppermute x4, starting transfers between devices, exchange(): pieces.append(lax.ppermute(payload, 'seq', pairs))  28.3 us
    all_to_all x2, waiting for transfers between devices, regroup(): lax.all_to_all(array, 'seq', 0, 0, tiled=True, axis_index_groups=groups)  12.2 us
    all_to_all x2, starting transfers between devices, regroup(): lax.all_to_all(array, 'seq', 0, 0, tiled=True, axis_index_groups=groups)  9.3 us
    ppermute x4, waiting for transfers between devices, exchange(): pieces.append(lax.ppermute(payload, 'seq', pairs))  9.28 us
    all_to_all x1, waiting for transfers between devices, local(): lax.all_to_all(sums, ('seq', 'head'), 0, 0, tiled=True, axis_index_groups...  8.24 us
    all_to_all x1, starting transfers between devices, local(): lax.all_to_all(sums, ('seq', 'head'), 0, 0, tiled=True, axis_index_groups...  6.46 us
    dot_general x15, matrix products, mixed(): return jnp.einsum(form, left, right, preferred_element_type=jnp.float32)  4.08 us
  transfers between devices with their start and end apart: 7, of which 6 were waited for; matrix products, arithmetic and copies ran while one was open for 2% of the time, Pallas kernels for 0%

profile of v6, /device:TPU:6, one launch (start us, length us, event | category | flops | bytes accessed | tf_op | source)
XLA Modules:
  0.0 139.7 jit_solution(14197463028539738244)
XLA Ops:
  0.0 1.8 %shard_map.73 = bf16[4,264,128]{2,1,0:T(8,128)(2,1)} custom-call(bf16[128,512]{1,0:T(8,128)(2,1)} %key_ref.1, bf16[128,512]{1,0:T(8,128)(2,1)} %value_ref.1, s32[1,128]{1,0:T(1,128)} %bitcast.137, s32[1,128]{1,0:T(1,128)} %bitcast.138), custom_call_target="tpu_custom_call" | custom-call | tf_op jit(solution)/shard_map/pallas_call | solution.py:66
  1.8 5.9 %all-to-all-start = ((bf16[4,264,128]{2,1,0:T(8,128)(2,1)}), bf16[4,264,128]{2,1,0:T(8,128)(2,1)S(1)}, u32[]{:S(2)}, u32[]{:S(2)}) async-start(bf16[4,264,128]{2,1,0:T(8,128)(2,1)} %shard_map.73), calls=%async_computation | async-start | bytes 540672 | tf_op jit(solution)/shard_map/all_to_all | solution.py:64
  8.0 0.7 maximum_maximum_fusion
  8.7 8.1 %all-to-all-done = bf16[4,264,128]{2,1,0:T(8,128)(2,1)S(1)} async-done(((bf16[4,264,128]{2,1,0:T(8,128)(2,1)}), bf16[4,264,128]{2,1,0:T(8,128)(2,1)S(1)}, u32[]{:S(2)}, u32[]{:S(2)}) %all-to-all-start) | async-done | bytes 270368 | tf_op jit(solution)/shard_map/all_to_all | solution.py:64
  16.9 0.3 fusion.14
  17.3 13.5 %collective-permute-start.1 = (bf16[136,128]{1,0:T(8,128)(2,1)S(1)}, bf16[136,128]{1,0:T(8,128)(2,1)S(1)}, u32[]{:S(2)}, u32[]{:S(2)}) collective-permute-start(bf16[136,128]{1,0:T(8,128)(2,1)S(1)} %pad_maximum_fusion.2), channel_id=1, source_target_pairs={{0,64},{8,72},{16,80},{24,88},{32,96},{40,104},{48,112},{56,120},{... | collective-permute-start | bytes 104456 | tf_op jit(solution)/shard_map/ppermute | solution.py:92
  30.8 4.3 %collective-permute-start = (bf16[136,128]{1,0:T(8,128)(2,1)S(1)}, bf16[136,128]{1,0:T(8,128)(2,1)S(1)}, u32[]{:S(2)}, u32[]{:S(2)}) collective-permute-start(bf16[136,128]{1,0:T(8,128)(2,1)S(1)} %pad_maximum_fusion.2), channel_id=1, source_target_pairs={{0,32},{8,40},{16,48},{24,56},{32,64},{40,72},{48,80},{56,88},{64,... | collective-permute-start | bytes 104456 | tf_op jit(solution)/shard_map/ppermute | solution.py:92
  35.1 0.3 fusion.23
  35.4 3.4 %all-to-all-start.1 = ((bf16[4,256,128]{2,1,0:T(8,128)(2,1)}), bf16[4,256,128]{2,1,0:T(8,128)(2,1)S(1)}, u32[]{:S(2)}, u32[]{:S(2)}) async-start(bf16[4,256,128]{2,1,0:T(8,128)(2,1)} %maximum_maximum_fusion), calls=%async_computation.1 | async-start | bytes 524288 | tf_op jit(solution)/shard_map/all_to_all | solution.py:64
  39.0 2.4 %collective-permute-done = bf16[136,128]{1,0:T(8,128)(2,1)S(1)} collective-permute-done((bf16[136,128]{1,0:T(8,128)(2,1)S(1)}, bf16[136,128]{1,0:T(8,128)(2,1)S(1)}, u32[]{:S(2)}, u32[]{:S(2)}) %collective-permute-start) | collective-permute-done | bytes 34848 | tf_op jit(solution)/shard_map/ppermute | solution.py:92
  41.6 4.0 %all-to-all-done.1 = bf16[4,256,128]{2,1,0:T(8,128)(2,1)S(1)} async-done(((bf16[4,256,128]{2,1,0:T(8,128)(2,1)}), bf16[4,256,128]{2,1,0:T(8,128)(2,1)S(1)}, u32[]{:S(2)}, u32[]{:S(2)}) %all-to-all-start.1) | async-done | bytes 262176 | tf_op jit(solution)/shard_map/all_to_all | solution.py:64
  46.0 0.4 multiply_reduce_fusion.1
  46.4 0.7 broadcast_in_dim.240
  47.0 6.5 %all-to-all-start.2 = ((f32[32,8,128]{2,1,0:T(8,128)}), f32[32,8,128]{2,1,0:T(8,128)S(1)}, u32[]{:S(2)}, u32[]{:S(2)}) async-start(f32[32,8,128]{2,1,0:T(8,128)} %broadcast_in_dim.240), calls=%async_computation.2 | async-start | bytes 262144 | tf_op jit(solution)/shard_map/all_to_all | solution.py:125
  53.6 0.3 fusion.16
  54.0 8.2 %all-to-all-done.2 = f32[32,8,128]{2,1,0:T(8,128)S(1)} async-done(((f32[32,8,128]{2,1,0:T(8,128)}), f32[32,8,128]{2,1,0:T(8,128)S(1)}, u32[]{:S(2)}, u32[]{:S(2)}) %all-to-all-start.2) | async-done | bytes 131104 | tf_op jit(solution)/shard_map/all_to_all | solution.py:125
  62.5 0.3 fusion.15
  62.8 6.7 %collective-permute-start.3 = (bf16[136,128]{1,0:T(8,128)(2,1)S(1)}, bf16[136,128]{1,0:T(8,128)(2,1)S(1)}, u32[]{:S(2)}, u32[]{:S(2)}) collective-permute-start(bf16[136,128]{1,0:T(8,128)(2,1)S(1)} %pad_maximum_fusion.3), channel_id=1, source_target_pairs={{64,0},{72,8},{80,16},{88,24},{96,32},{104,40},{112,48},{120,56},{... | collective-permute-start | bytes 104456 | tf_op jit(solution)/shard_map/ppermute | solution.py:92
  69.6 3.7 %collective-permute-start.2 = (bf16[136,128]{1,0:T(8,128)(2,1)S(1)}, bf16[136,128]{1,0:T(8,128)(2,1)S(1)}, u32[]{:S(2)}, u32[]{:S(2)}) collective-permute-start(bf16[136,128]{1,0:T(8,128)(2,1)S(1)} %pad_maximum_fusion.3), channel_id=1, source_target_pairs={{32,0},{40,8},{48,16},{56,24},{64,32},{72,40},{80,48},{88,56},{96,... | collective-permute-start | bytes 104456 | tf_op jit(solution)/shard_map/ppermute | solution.py:92
  73.3 0.2 fusion.77
  73.6 0.2 fusion.10
  74.0 0.2 fusion.11
  74.2 0.3 fusion.19
  74.5 0.2 fusion.38
  74.9 2.5 %collective-permute-done.3 = bf16[136,128]{1,0:T(8,128)(2,1)S(1)} collective-permute-done((bf16[136,128]{1,0:T(8,128)(2,1)S(1)}, bf16[136,128]{1,0:T(8,128)(2,1)S(1)}, u32[]{:S(2)}, u32[]{:S(2)}) %collective-permute-start.3) | collective-permute-done | bytes 34848 | tf_op jit(solution)/shard_map/ppermute | solution.py:92
  77.4 4.4 %collective-permute-done.2 = bf16[136,128]{1,0:T(8,128)(2,1)S(1)} collective-permute-done((bf16[136,128]{1,0:T(8,128)(2,1)S(1)}, bf16[136,128]{1,0:T(8,128)(2,1)S(1)}, u32[]{:S(2)}, u32[]{:S(2)}) %collective-permute-start.2) | collective-permute-done | bytes 34848 | tf_op jit(solution)/shard_map/ppermute | solution.py:92
  82.3 0.8 fusion.2
  83.1 1.1 pad_maximum_fusion
  84.2 53.3 %all_to_all.20 = bf16[64,25,2,128]{3,2,1,0:T(2,128)(2,1)S(1)} all-to-all(bf16[64,25,2,128]{3,2,1,0:T(2,128)(2,1)S(1)} %pad_maximum_fusion), channel_id=1, replica_groups=mesh['seq'=64,'head'=8] {'seq'}, dimensions={0} | all-to-all | bytes 1638400 | tf_op jit(solution)/shard_map/all_to_all | solution.py:176
  137.7 0.5 slice.159
  138.2 0.5 convolution_bitcast_fusion
  138.8 0.9 copy.116
  (60 shorter events, 2.3 us)
Async XLA Ops:
  0.0 7.8 %copy-start.2 = (f32[512]{0:T(512)S(1)}, f32[512]{0:T(512)}, u32[]{:S(2)}) copy-start(f32[512]{0:T(512)} %param.11) | copy-start | bytes 6148
  0.0 7.9 %copy-start = (bf16[128,512]{1,0:T(8,128)(2,1)S(1)}, bf16[128,512]{1,0:T(8,128)(2,1)}, u32[]{:S(2)}) copy-start(bf16[128,512]{1,0:T(8,128)(2,1)} %param.10) | copy-start | bytes 393220
  0.0 7.9 %copy-start.1 = (bf16[128,512]{1,0:T(8,128)(2,1)S(1)}, bf16[128,512]{1,0:T(8,128)(2,1)}, u32[]{:S(2)}) copy-start(bf16[128,512]{1,0:T(8,128)(2,1)} %param.7) | copy-start | bytes 393220
  1.8 15.0 %all-to-all-start = ((bf16[4,264,128]{2,1,0:T(8,128)(2,1)}), bf16[4,264,128]{2,1,0:T(8,128)(2,1)S(1)}, u32[]{:S(2)}, u32[]{:S(2)}) async-start(bf16[4,264,128]{2,1,0:T(8,128)(2,1)} %shard_map.73), calls=%async_computation | async-start | bytes 540672 | tf_op jit(solution)/shard_map/all_to_all | solution.py:64
  17.3 21.8 %collective-permute-start.1 = (bf16[136,128]{1,0:T(8,128)(2,1)S(1)}, bf16[136,128]{1,0:T(8,128)(2,1)S(1)}, u32[]{:S(2)}, u32[]{:S(2)}) collective-permute-start(bf16[136,128]{1,0:T(8,128)(2,1)S(1)} %pad_maximum_fusion.2), channel_id=1, source_target_pairs={{0,64},{8,72},{16,80},{24,88},{32,96},{40,104},{48,112},{56,120},{... | collective-permute-start | bytes 104456 | tf_op jit(solution)/shard_map/ppermute | solution.py:92
  30.8 10.6 %collective-permute-start = (bf16[136,128]{1,0:T(8,128)(2,1)S(1)}, bf16[136,128]{1,0:T(8,128)(2,1)S(1)}, u32[]{:S(2)}, u32[]{:S(2)}) collective-permute-start(bf16[136,128]{1,0:T(8,128)(2,1)S(1)} %pad_maximum_fusion.2), channel_id=1, source_target_pairs={{0,32},{8,40},{16,48},{24,56},{32,64},{40,72},{48,80},{56,88},{64,... | collective-permute-start | bytes 104456 | tf_op jit(solution)/shard_map/ppermute | solution.py:92
  35.4 10.2 %all-to-all-start.1 = ((bf16[4,256,128]{2,1,0:T(8,128)(2,1)}), bf16[4,256,128]{2,1,0:T(8,128)(2,1)S(1)}, u32[]{:S(2)}, u32[]{:S(2)}) async-start(bf16[4,256,128]{2,1,0:T(8,128)(2,1)} %maximum_maximum_fusion), calls=%async_computation.1 | async-start | bytes 524288 | tf_op jit(solution)/shard_map/all_to_all | solution.py:64
  47.0 15.2 %all-to-all-start.2 = ((f32[32,8,128]{2,1,0:T(8,128)}), f32[32,8,128]{2,1,0:T(8,128)S(1)}, u32[]{:S(2)}, u32[]{:S(2)}) async-start(f32[32,8,128]{2,1,0:T(8,128)} %broadcast_in_dim.240), calls=%async_computation.2 | async-start | bytes 262144 | tf_op jit(solution)/shard_map/all_to_all | solution.py:125
  62.8 14.5 %collective-permute-start.3 = (bf16[136,128]{1,0:T(8,128)(2,1)S(1)}, bf16[136,128]{1,0:T(8,128)(2,1)S(1)}, u32[]{:S(2)}, u32[]{:S(2)}) collective-permute-start(bf16[136,128]{1,0:T(8,128)(2,1)S(1)} %pad_maximum_fusion.3), channel_id=1, source_target_pairs={{64,0},{72,8},{80,16},{88,24},{96,32},{104,40},{112,48},{120,56},{... | collective-permute-start | bytes 104456 | tf_op jit(solution)/shard_map/ppermute | solution.py:92
  69.6 12.2 %collective-permute-start.2 = (bf16[136,128]{1,0:T(8,128)(2,1)S(1)}, bf16[136,128]{1,0:T(8,128)(2,1)S(1)}, u32[]{:S(2)}, u32[]{:S(2)}) collective-permute-start(bf16[136,128]{1,0:T(8,128)(2,1)S(1)} %pad_maximum_fusion.3), channel_id=1, source_target_pairs={{32,0},{40,8},{48,16},{56,24},{64,32},{72,40},{80,48},{88,56},{96,... | collective-permute-start | bytes 104456 | tf_op jit(solution)/shard_map/ppermute | solution.py:92

commit v7 on v6

--- a/solution.py
+++ b/solution.py
@@ -82,15 +82,14 @@
     last_rows = (doc == last)[:, :, None]
     zero = jnp.zeros((), jnp.bfloat16)
 
-    def exchange(state, number, sign):
+    def shifted(load, groups_on):
+        step = groups_on * SUB
+        pairs = [(i, i + step) for i in range(seq_count) if 0 <= i + step < seq_count]
+        return lax.ppermute(load, "seq", pairs)
+
+    def payload(state, number):
         number = jnp.broadcast_to(number.astype(jnp.bfloat16), (EXTRA, HS))
-        payload = jnp.concatenate([state.astype(jnp.bfloat16), number], axis=0)
-        pieces = []
-        for far in (1, 2):
-            step = sign * far * SUB
-            pairs = [(i, i + step) for i in range(seq_count) if 0 <= i + step < seq_count]
-            pieces.append(lax.ppermute(payload, "seq", pairs))
-        return pieces
+        return jnp.concatenate([state.astype(jnp.bfloat16), number], axis=0)
 
     def entering(pieces, own, numbers, own_numbers, order):
         state = sum(
@@ -106,10 +105,23 @@
         return (state + inside).astype(jnp.bfloat16)
 
     sent = mixed(jnp.where((doc == last[SUB - 1])[:, :, None], key, zero), value, "bta,btc->ac")
-    pieces = exchange(sent, last[SUB - 1], 1)
+    near = shifted(payload(sent, last[SUB - 1]), 1)
+    pieces = [near, shifted(near, 1)]
     own = mixed(jnp.where(last_rows, key, zero), value, "bta,btc->bac")
     query_grad = jnp.concatenate([heads_first(query), heads_first(grad_normed)], axis=1)
-    query_grad, own = together(query_grad, own)
+    numbers, lanes, all_slots, all_owners, starts = (
+        count.astype(jnp.float32)
+        for count in (
+            places + 1,
+            jnp.arange(HS),
+            jnp.arange(seq_count * slots),
+            jnp.arange(seq_count),
+            blocks * capacity,
+        )
+    )
+    query_grad, own, numbers, lanes, all_slots, all_owners, starts = together(
+        query_grad, own, numbers, lanes, all_slots, all_owners, starts
+    )
     query_grad = regroup(query_grad)
     quer = query_grad[:, :tok_rows]
     normed = query_grad[:, tok_rows:]
@@ -132,7 +144,8 @@
     ).astype(jnp.bfloat16)
 
     sent = mixed(jnp.where((doc == first[0])[:, :, None], quer, zero), grad, "bta,btc->ac")
-    pieces = exchange(sent, first[0], -1)
+    sent = payload(sent, first[0])
+    pieces = [shifted(sent, -1), shifted(sent, -2)]
     back = jnp.where(visible, mixed(grad, value, "btc,bsc->bts"), 0.0).astype(jnp.bfloat16)
     grad_query = mixed(back, key, "bts,bsa->bta") + jnp.where(
         first_rows, mixed(grad, carry, "btc,bac->bta"), 0.0
@@ -140,19 +153,20 @@
     grad_query = grad_query.astype(jnp.bfloat16)
     own = mixed(jnp.where(first_rows, quer, zero), grad, "bta,btc->bac")
 
+    small, grad = together(small, grad)
     owners, ranks, row = (small[:, at].reshape(-1) for at in (1, 2, 5))
-    rank_slot = (small[:, 2] + (blocks * capacity)[:, None]).reshape(-1)
+    rank_slot = (small[:, 2] + starts[:, None]).reshape(-1)
     slot = owners * slots + rank_slot
-    place = slot[None, :] == jnp.arange(seq_count * slots)[:, None].astype(jnp.float32)
-    to_owner = owners[None, :] == jnp.arange(seq_count)[:, None].astype(jnp.float32)
-    at_slot = rank_slot[:, None] == jnp.arange(HS)[None, :].astype(jnp.float32)
+    place = slot[None, :] == all_slots[:, None]
+    to_owner = owners[None, :] == all_owners[:, None]
+    at_slot = rank_slot[:, None] == lanes[None, :]
     index = jnp.dot(
         to_owner.astype(jnp.bfloat16),
         jnp.where(at_slot, row[:, None] + 1.0, 0.0).astype(jnp.bfloat16),
         preferred_element_type=jnp.float32,
     ).astype(jnp.bfloat16)
     index = jnp.pad(index[:, None, None], ((0, 0), (0, 0), (0, 1), (0, 0)))
-    index, grad_query = together(index, grad_query)
+    index, place, grad_query = together(index, place.astype(jnp.bfloat16), grad_query)
 
     carry = entering(pieces, own, last, first, blocks[:, None] < blocks[None, :])
     grad_keys = mixed(back, quer, "bts,bta->bsa") + jnp.where(
@@ -166,13 +180,12 @@
     )
     rows = rows.reshape(SUB * tok_rows, 3 * HS)
     packed = jnp.dot(
-        place.astype(jnp.bfloat16), rows, preferred_element_type=jnp.float32
+        place, rows, preferred_element_type=jnp.float32
     ).astype(jnp.bfloat16)
     halves = slots // 8
     packed = packed.reshape(seq_count, halves, 8, 3, HS).transpose(0, 1, 3, 2, 4)
     packed = packed.reshape(seq_count, halves * 12, 2, HS)
     packed = jnp.concatenate([packed, index], axis=1)
-    packed, numbers = together(packed, (places + 1).astype(jnp.float32))
     received = lax.all_to_all(packed, "seq", 0, 0, tiled=True)
     index = received[::SUB, halves * 12, 0, :slots].astype(jnp.float32)
     choose = (index[None] == numbers[:, None, None]).astype(jnp.bfloat16)

time: 140 us -> 139 us (level)
  blocking collectives: 53.3 us -> 71.3 us
  waiting for transfers between devices: 29.7 us -> 15.9 us
  starting transfers between devices: 44.1 us -> 38.8 us
    all_to_all x0 -> x1, blocking collectives: none -> 17.2 us  [local(): lax.all_to_all(sums, ('seq', 'head'), 0, 0, tiled=True, axis_index_groups...]
    all_to_all x1 -> x0, waiting for transfers between devices: 8.24 us -> none  [local(): lax.all_to_all(sums, ('seq', 'head'), 0, 0, tiled=True, axis_index_groups...]
    all_to_all x1 -> x0, starting transfers between devices: 6.46 us -> none  [local(): lax.all_to_all(sums, ('seq', 'head'), 0, 0, tiled=True, axis_index_groups...]
    all_to_all x2, waiting for transfers between devices: 12.2 us -> 8.13 us  [regroup(): lax.all_to_all(array, 'seq', 0, 0, tiled=True, axis_index_groups=groups)]
    ppermute x4, waiting for transfers between devices: 9.28 us -> 7.73 us  [shifted(): return lax.ppermute(load, 'seq', pairs)]
  transfers between devices with their start and end apart: 7 -> 6, of which waited for: 6 -> 3; matrix products, arithmetic and copies ran while one was open for 2% -> 3% of each run, Pallas kernels for 0% -> 0%
where the time goes in v7:
time: 139 us; the launch traced here: 138 us
  blocking collectives  71.3 us (51%)
  starting transfers between devices  38.8 us (28%)
  waiting for transfers between devices  15.9 us (11%)
  matrix products  5.13 us (4%)
  other arithmetic  3 us (2%)
  Pallas kernels  1.84 us (1%)
  local copies, waits for them, and re-layouts  1.82 us (1%)
    all_to_all x1, blocking collectives, local(): received = lax.all_to_all(packed, 'seq', 0, 0, tiled=True)  54.1 us
    ppermute x4, starting transfers between devices, shifted(): return lax.ppermute(load, 'seq', pairs)  29.5 us
    all_to_all x1, blocking collectives, local(): lax.all_to_all(sums, ('seq', 'head'), 0, 0, tiled=True, axis_index_groups...  17.2 us
    all_to_all x2, starting transfers between devices, regroup(): lax.all_to_all(array, 'seq', 0, 0, tiled=True, axis_index_groups=groups)  9.3 us
    all_to_all x2, waiting for transfers between devices, regroup(): lax.all_to_all(array, 'seq', 0, 0, tiled=True, axis_index_groups=groups)  8.13 us
    ppermute x4, waiting for transfers between devices, shifted(): return lax.ppermute(load, 'seq', pairs)  7.73 us
    dot_general x15, matrix products, mixed(): return jnp.einsum(form, left, right, preferred_element_type=jnp.float32)  4.08 us
  transfers between devices with their start and end apart: 6, of which 3 were waited for; matrix products, arithmetic and copies ran while one was open for 3% of the time, Pallas kernels for 0%

profile of v7, /device:TPU:6, one launch (start us, length us, event | category | flops | bytes accessed | tf_op | source)
XLA Modules:
  0.0 138.2 jit_solution(3337943976373898270)
XLA Ops:
  0.0 1.8 %shard_map.73 = bf16[4,264,128]{2,1,0:T(8,128)(2,1)} custom-call(bf16[128,512]{1,0:T(8,128)(2,1)} %key_ref.1, bf16[128,512]{1,0:T(8,128)(2,1)} %value_ref.1, s32[1,128]{1,0:T(1,128)} %bitcast.138, s32[1,128]{1,0:T(1,128)} %bitcast.139), custom_call_target="tpu_custom_call" | custom-call | tf_op jit(solution)/shard_map/pallas_call | solution.py:66
  1.8 5.9 %all-to-all-start = ((bf16[4,264,128]{2,1,0:T(8,128)(2,1)}), bf16[4,264,128]{2,1,0:T(8,128)(2,1)S(1)}, u32[]{:S(2)}, u32[]{:S(2)}) async-start(bf16[4,264,128]{2,1,0:T(8,128)(2,1)} %shard_map.73), calls=%async_computation | async-start | bytes 540672 | tf_op jit(solution)/shard_map/all_to_all | solution.py:64
  8.0 0.7 maximum_maximum_fusion
  8.7 8.1 %all-to-all-done = bf16[4,264,128]{2,1,0:T(8,128)(2,1)S(1)} async-done(((bf16[4,264,128]{2,1,0:T(8,128)(2,1)}), bf16[4,264,128]{2,1,0:T(8,128)(2,1)S(1)}, u32[]{:S(2)}, u32[]{:S(2)}) %all-to-all-start) | async-done | bytes 270368 | tf_op jit(solution)/shard_map/all_to_all | solution.py:64
  16.9 0.3 fusion.9
  17.3 9.1 %collective-permute-start = (bf16[136,128]{1,0:T(8,128)(2,1)S(1)}, bf16[136,128]{1,0:T(8,128)(2,1)S(1)}, u32[]{:S(2)}, u32[]{:S(2)}) collective-permute-start(bf16[136,128]{1,0:T(8,128)(2,1)S(1)} %pad_maximum_fusion.2), channel_id=1, source_target_pairs={{0,32},{8,40},{16,48},{24,56},{32,64},{40,72},{48,80},{56,88},{64,... | collective-permute-start | bytes 104456 | tf_op jit(solution)/shard_map/ppermute | solution.py:88
  26.4 0.3 fusion.19
  26.7 3.4 %all-to-all-start.1 = ((bf16[4,256,128]{2,1,0:T(8,128)(2,1)}), bf16[4,256,128]{2,1,0:T(8,128)(2,1)S(1)}, u32[]{:S(2)}, u32[]{:S(2)}) async-start(bf16[4,256,128]{2,1,0:T(8,128)(2,1)} %maximum_maximum_fusion), calls=%async_computation.1 | async-start | bytes 524288 | tf_op jit(solution)/shard_map/all_to_all | solution.py:64
  30.3 6.9 %collective-permute-start.1 = (bf16[136,128]{1,0:T(8,128)(2,1)S(1)}, bf16[136,128]{1,0:T(8,128)(2,1)S(1)}, u32[]{:S(2)}, u32[]{:S(2)}) collective-permute-start(bf16[136,128]{1,0:T(8,128)(2,1)S(1)} %collective-permute-done), channel_id=1, source_target_pairs={{0,32},{8,40},{16,48},{24,56},{32,64},{40,72},{48,80},{56,88},{64,... | collective-permute-start | bytes 104456 | tf_op jit(solution)/shard_map/ppermute | solution.py:88
  37.2 3.9 %collective-permute-done.1 = bf16[136,128]{1,0:T(8,128)(2,1)S(1)} collective-permute-done((bf16[136,128]{1,0:T(8,128)(2,1)S(1)}, bf16[136,128]{1,0:T(8,128)(2,1)S(1)}, u32[]{:S(2)}, u32[]{:S(2)}) %collective-permute-start.1) | collective-permute-done | bytes 34848 | tf_op jit(solution)/shard_map/ppermute | solution.py:88
  41.2 0.2 fusion.4
  41.6 0.4 multiply_reduce_fusion.1
  42.0 17.2 %all_to_all.20 = f32[32,8,128]{2,1,0:T(8,128)S(1)} all-to-all(f32[32,8,128]{2,1,0:T(8,128)S(1)} %broadcast_in_dim.237), channel_id=1, replica_groups={{0,1,2,3,4,5,6,7,8,9,10,11,12,13,14,15,16,17,18,19,20,21,22,23,24,25,26..., dimensions={0} | all-to-all | bytes 262144 | tf_op jit(solution)/shard_map/all_to_all | solution.py:137
  59.2 0.2 subtract_convert_fusion
  59.5 0.3 fusion.10
  59.8 8.4 %collective-permute-start.3 = (bf16[136,128]{1,0:T(8,128)(2,1)S(1)}, bf16[136,128]{1,0:T(8,128)(2,1)S(1)}, u32[]{:S(2)}, u32[]{:S(2)}) collective-permute-start(bf16[136,128]{1,0:T(8,128)(2,1)S(1)} %pad_maximum_fusion.3), channel_id=1, source_target_pairs={{64,0},{72,8},{80,16},{88,24},{96,32},{104,40},{112,48},{120,56},{... | collective-permute-start | bytes 104456 | tf_op jit(solution)/shard_map/ppermute | solution.py:88
  68.3 5.1 %collective-permute-start.2 = (bf16[136,128]{1,0:T(8,128)(2,1)S(1)}, bf16[136,128]{1,0:T(8,128)(2,1)S(1)}, u32[]{:S(2)}, u32[]{:S(2)}) collective-permute-start(bf16[136,128]{1,0:T(8,128)(2,1)S(1)} %pad_maximum_fusion.3), channel_id=1, source_target_pairs={{32,0},{40,8},{48,16},{56,24},{64,32},{72,40},{80,48},{88,56},{96,... | collective-permute-start | bytes 104456 | tf_op jit(solution)/shard_map/ppermute | solution.py:88
  73.4 0.2 fusion.71
  73.6 0.2 fusion.5
  74.0 0.2 fusion.6
  74.3 0.3 fusion.12
  74.7 0.2 compare_convert_fusion
  75.0 0.2 fusion.31
  75.2 0.3 fusion.11
  75.7 3.8 %collective-permute-done.2 = bf16[136,128]{1,0:T(8,128)(2,1)S(1)} collective-permute-done((bf16[136,128]{1,0:T(8,128)(2,1)S(1)}, bf16[136,128]{1,0:T(8,128)(2,1)S(1)}, u32[]{:S(2)}, u32[]{:S(2)}) %collective-permute-start.2) | collective-permute-done | bytes 34848 | tf_op jit(solution)/shard_map/ppermute | solution.py:88
  79.8 0.2 fusion.7
  80.1 0.7 convolution_convert_fusion
  80.8 1.1 pad_maximum_fusion
  81.9 54.1 %all_to_all.21 = bf16[64,25,2,128]{3,2,1,0:T(2,128)(2,1)S(1)} all-to-all(bf16[64,25,2,128]{3,2,1,0:T(2,128)(2,1)S(1)} %pad_maximum_fusion), channel_id=1, replica_groups=mesh['seq'=64,'head'=8] {'seq'}, dimensions={0} | all-to-all | bytes 1638400 | tf_op jit(solution)/shard_map/all_to_all | solution.py:189
  136.1 0.5 slice.156
  136.7 0.5 convolution_bitcast_fusion
  137.3 0.9 copy.116
  (60 shorter events, 1.7 us)
Async XLA Ops:
  0.0 7.8 %copy-start.2 = (f32[512]{0:T(512)S(1)}, f32[512]{0:T(512)}, u32[]{:S(2)}) copy-start(f32[512]{0:T(512)} %param.11) | copy-start | bytes 6148
  0.0 7.9 %copy-start = (bf16[128,512]{1,0:T(8,128)(2,1)S(1)}, bf16[128,512]{1,0:T(8,128)(2,1)}, u32[]{:S(2)}) copy-start(bf16[128,512]{1,0:T(8,128)(2,1)} %param.10) | copy-start | bytes 393220
  0.0 7.9 %copy-start.1 = (bf16[128,512]{1,0:T(8,128)(2,1)S(1)}, bf16[128,512]{1,0:T(8,128)(2,1)}, u32[]{:S(2)}) copy-start(bf16[128,512]{1,0:T(8,128)(2,1)} %param.7) | copy-start | bytes 393220
  1.8 15.0 %all-to-all-start = ((bf16[4,264,128]{2,1,0:T(8,128)(2,1)}), bf16[4,264,128]{2,1,0:T(8,128)(2,1)S(1)}, u32[]{:S(2)}, u32[]{:S(2)}) async-start(bf16[4,264,128]{2,1,0:T(8,128)(2,1)} %shard_map.73), calls=%async_computation | async-start | bytes 540672 | tf_op jit(solution)/shard_map/all_to_all | solution.py:64
  17.3 13.0 %collective-permute-start = (bf16[136,128]{1,0:T(8,128)(2,1)S(1)}, bf16[136,128]{1,0:T(8,128)(2,1)S(1)}, u32[]{:S(2)}, u32[]{:S(2)}) collective-permute-start(bf16[136,128]{1,0:T(8,128)(2,1)S(1)} %pad_maximum_fusion.2), channel_id=1, source_target_pairs={{0,32},{8,40},{16,48},{24,56},{32,64},{40,72},{48,80},{56,88},{64,... | collective-permute-start | bytes 104456 | tf_op jit(solution)/shard_map/ppermute | solution.py:88
  26.7 14.5 %all-to-all-start.1 = ((bf16[4,256,128]{2,1,0:T(8,128)(2,1)}), bf16[4,256,128]{2,1,0:T(8,128)(2,1)S(1)}, u32[]{:S(2)}, u32[]{:S(2)}) async-start(bf16[4,256,128]{2,1,0:T(8,128)(2,1)} %maximum_maximum_fusion), calls=%async_computation.1 | async-start | bytes 524288 | tf_op jit(solution)/shard_map/all_to_all | solution.py:64
  30.3 10.8 %collective-permute-start.1 = (bf16[136,128]{1,0:T(8,128)(2,1)S(1)}, bf16[136,128]{1,0:T(8,128)(2,1)S(1)}, u32[]{:S(2)}, u32[]{:S(2)}) collective-permute-start(bf16[136,128]{1,0:T(8,128)(2,1)S(1)} %collective-permute-done), channel_id=1, source_target_pairs={{0,32},{8,40},{16,48},{24,56},{32,64},{40,72},{48,80},{56,88},{64,... | collective-permute-start | bytes 104456 | tf_op jit(solution)/shard_map/ppermute | solution.py:88
  59.8 15.8 %collective-permute-start.3 = (bf16[136,128]{1,0:T(8,128)(2,1)S(1)}, bf16[136,128]{1,0:T(8,128)(2,1)S(1)}, u32[]{:S(2)}, u32[]{:S(2)}) collective-permute-start(bf16[136,128]{1,0:T(8,128)(2,1)S(1)} %pad_maximum_fusion.3), channel_id=1, source_target_pairs={{64,0},{72,8},{80,16},{88,24},{96,32},{104,40},{112,48},{120,56},{... | collective-permute-start | bytes 104456 | tf_op jit(solution)/shard_map/ppermute | solution.py:88
  68.3 11.2 %collective-permute-start.2 = (bf16[136,128]{1,0:T(8,128)(2,1)S(1)}, bf16[136,128]{1,0:T(8,128)(2,1)S(1)}, u32[]{:S(2)}, u32[]{:S(2)}) collective-permute-start(bf16[136,128]{1,0:T(8,128)(2,1)S(1)} %pad_maximum_fusion.3), channel_id=1, source_target_pairs={{32,0},{40,8},{48,16},{56,24},{64,32},{72,40},{80,48},{88,56},{96,... | collective-permute-start | bytes 104456 | tf_op jit(solution)/shard_map/ppermute | solution.py:88

commit v8 on v7

--- a/solution.py
+++ b/solution.py
@@ -2,6 +2,7 @@
 import jax.numpy as jnp
 from jax import lax
 from jax.experimental import pallas as pl
+from jax.experimental.layout import Layout, with_layout_constraint
 from jax.experimental.pallas import tpu as pltpu
 from jax.sharding import PartitionSpec as P
 
@@ -165,7 +166,9 @@
         jnp.where(at_slot, row[:, None] + 1.0, 0.0).astype(jnp.bfloat16),
         preferred_element_type=jnp.float32,
     ).astype(jnp.bfloat16)
-    index = jnp.pad(index[:, None, None], ((0, 0), (0, 0), (0, 1), (0, 0)))
+    tiles = slots // 8 * 12
+    index = jnp.pad(index[:, None, None], ((0, 0), (tiles, 0), (0, 1), (0, 0)))
+    index = with_layout_constraint(index, Layout((0, 1, 2, 3)))
     index, place, grad_query = together(index, place.astype(jnp.bfloat16), grad_query)
 
     carry = entering(pieces, own, last, first, blocks[:, None] < blocks[None, :])
@@ -185,15 +188,15 @@
     halves = slots // 8
     packed = packed.reshape(seq_count, halves, 8, 3, HS).transpose(0, 1, 3, 2, 4)
     packed = packed.reshape(seq_count, halves * 12, 2, HS)
-    packed = jnp.concatenate([packed, index], axis=1)
+    packed = lax.dynamic_update_slice(index, packed, (0, 0, 0, 0))
     received = lax.all_to_all(packed, "seq", 0, 0, tiled=True)
     index = received[::SUB, halves * 12, 0, :slots].astype(jnp.float32)
     choose = (index[None] == numbers[:, None, None]).astype(jnp.bfloat16)
-    choose = choose.reshape(tok_rows, seq_count // SUB, halves, 8)
+    choose = choose.reshape(tok_rows, seq_count // SUB * slots)
     received = received[:, : halves * 12].reshape(seq_count // SUB, SUB, halves, 3, 8, HS)
-    return mixed(choose, received, "rghk,gshjkd->rjsd").astype(jnp.bfloat16).reshape(
-        tok_rows, 3, width
-    )
+    received = received.transpose(3, 0, 2, 4, 1, 5).reshape(3, seq_count // SUB * slots, width)
+    rows = mixed(choose, received, "rk,jkn->jrn").astype(jnp.bfloat16)
+    return rows.transpose(1, 0, 2)
 
 
 def solution(mesh):

time: 139 us -> 138 us (level)
  no operation moved by 1% of the time
where the time goes in v8:
time: 138 us; the launch traced here: 137 us
  blocking collectives  71.3 us (52%)
  starting transfers between devices  38.8 us (28%)
  waiting for transfers between devices  15.4 us (11%)
  matrix products  5.68 us (4%)
  local copies, waits for them, and re-layouts  2.02 us (1%)
  other arithmetic  1.96 us (1%)
  Pallas kernels  1.84 us (1%)
    all_to_all x1, blocking collectives, local(): received = lax.all_to_all(packed, 'seq', 0, 0, tiled=True)  54.1 us
    ppermute x4, starting transfers between devices, shifted(): return lax.ppermute(load, 'seq', pairs)  29.5 us
    all_to_all x1, blocking collectives, local(): lax.all_to_all(sums, ('seq', 'head'), 0, 0, tiled=True, axis_index_groups...  17.2 us
    all_to_all x2, starting transfers between devices, regroup(): lax.all_to_all(array, 'seq', 0, 0, tiled=True, axis_index_groups=groups)  9.3 us
    all_to_all x2, waiting for transfers between devices, regroup(): lax.all_to_all(array, 'seq', 0, 0, tiled=True, axis_index_groups=groups)  8.13 us
    ppermute x4, waiting for transfers between devices, shifted(): return lax.ppermute(load, 'seq', pairs)  7.3 us
    dot_general x15, matrix products, mixed(): return jnp.einsum(form, left, right, preferred_element_type=jnp.float32)  4.62 us
  transfers between devices with their start and end apart: 6, of which 3 were waited for; matrix products, arithmetic and copies ran while one was open for 3% of the time, Pallas kernels for 0%

profile of v8, /device:TPU:6, one launch (start us, length us, event | category | flops | bytes accessed | tf_op | source)
XLA Modules:
  0.0 137.4 jit_solution(9482710096466424031)
XLA Ops:
  0.0 1.8 %shard_map.73 = bf16[4,264,128]{2,1,0:T(8,128)(2,1)} custom-call(bf16[128,512]{1,0:T(8,128)(2,1)} %key_ref.1, bf16[128,512]{1,0:T(8,128)(2,1)} %value_ref.1, s32[1,128]{1,0:T(1,128)} %bitcast.126, s32[1,128]{1,0:T(1,128)} %bitcast.127), custom_call_target="tpu_custom_call" | custom-call | tf_op jit(solution)/shard_map/pallas_call | solution.py:67
  1.8 5.9 %all-to-all-start = ((bf16[4,264,128]{2,1,0:T(8,128)(2,1)}), bf16[4,264,128]{2,1,0:T(8,128)(2,1)S(1)}, u32[]{:S(2)}, u32[]{:S(2)}) async-start(bf16[4,264,128]{2,1,0:T(8,128)(2,1)} %shard_map.73), calls=%async_computation | async-start | bytes 540672 | tf_op jit(solution)/shard_map/all_to_all | solution.py:65
  8.0 0.7 maximum_maximum_fusion
  8.7 8.1 %all-to-all-done = bf16[4,264,128]{2,1,0:T(8,128)(2,1)S(1)} async-done(((bf16[4,264,128]{2,1,0:T(8,128)(2,1)}), bf16[4,264,128]{2,1,0:T(8,128)(2,1)S(1)}, u32[]{:S(2)}, u32[]{:S(2)}) %all-to-all-start) | async-done | bytes 270368 | tf_op jit(solution)/shard_map/all_to_all | solution.py:65
  16.9 0.3 fusion.9
  17.3 9.1 %collective-permute-start = (bf16[136,128]{1,0:T(8,128)(2,1)S(1)}, bf16[136,128]{1,0:T(8,128)(2,1)S(1)}, u32[]{:S(2)}, u32[]{:S(2)}) collective-permute-start(bf16[136,128]{1,0:T(8,128)(2,1)S(1)} %pad_maximum_fusion.1), channel_id=1, source_target_pairs={{0,32},{8,40},{16,48},{24,56},{32,64},{40,72},{48,80},{56,88},{64,... | collective-permute-start | bytes 104456 | tf_op jit(solution)/shard_map/ppermute | solution.py:89
  26.4 0.3 fusion.19
  26.7 3.4 %all-to-all-start.1 = ((bf16[4,256,128]{2,1,0:T(8,128)(2,1)}), bf16[4,256,128]{2,1,0:T(8,128)(2,1)S(1)}, u32[]{:S(2)}, u32[]{:S(2)}) async-start(bf16[4,256,128]{2,1,0:T(8,128)(2,1)} %maximum_maximum_fusion), calls=%async_computation.1 | async-start | bytes 524288 | tf_op jit(solution)/shard_map/all_to_all | solution.py:65
  30.3 6.9 %collective-permute-start.1 = (bf16[136,128]{1,0:T(8,128)(2,1)S(1)}, bf16[136,128]{1,0:T(8,128)(2,1)S(1)}, u32[]{:S(2)}, u32[]{:S(2)}) collective-permute-start(bf16[136,128]{1,0:T(8,128)(2,1)S(1)} %collective-permute-done), channel_id=1, source_target_pairs={{0,32},{8,40},{16,48},{24,56},{32,64},{40,72},{48,80},{56,88},{64,... | collective-permute-start | bytes 104456 | tf_op jit(solution)/shard_map/ppermute | solution.py:89
  37.2 3.9 %collective-permute-done.1 = bf16[136,128]{1,0:T(8,128)(2,1)S(1)} collective-permute-done((bf16[136,128]{1,0:T(8,128)(2,1)S(1)}, bf16[136,128]{1,0:T(8,128)(2,1)S(1)}, u32[]{:S(2)}, u32[]{:S(2)}) %collective-permute-start.1) | collective-permute-done | bytes 34848 | tf_op jit(solution)/shard_map/ppermute | solution.py:89
  41.2 0.2 fusion.4
  41.6 0.4 multiply_reduce_fusion.1
  42.0 17.2 %all_to_all.20 = f32[32,8,128]{2,1,0:T(8,128)S(1)} all-to-all(f32[32,8,128]{2,1,0:T(8,128)S(1)} %broadcast_in_dim.237), channel_id=1, replica_groups={{0,1,2,3,4,5,6,7,8,9,10,11,12,13,14,15,16,17,18,19,20,21,22,23,24,25,26..., dimensions={0} | all-to-all | bytes 262144 | tf_op jit(solution)/shard_map/all_to_all | solution.py:138
  59.5 0.3 fusion.10
  59.8 8.4 %collective-permute-start.3 = (bf16[136,128]{1,0:T(8,128)(2,1)S(1)}, bf16[136,128]{1,0:T(8,128)(2,1)S(1)}, u32[]{:S(2)}, u32[]{:S(2)}) collective-permute-start(bf16[136,128]{1,0:T(8,128)(2,1)S(1)} %pad_maximum_fusion.2), channel_id=1, source_target_pairs={{64,0},{72,8},{80,16},{88,24},{96,32},{104,40},{112,48},{120,56},{... | collective-permute-start | bytes 104456 | tf_op jit(solution)/shard_map/ppermute | solution.py:89
  68.3 5.1 %collective-permute-start.2 = (bf16[136,128]{1,0:T(8,128)(2,1)S(1)}, bf16[136,128]{1,0:T(8,128)(2,1)S(1)}, u32[]{:S(2)}, u32[]{:S(2)}) collective-permute-start(bf16[136,128]{1,0:T(8,128)(2,1)S(1)} %pad_maximum_fusion.2), channel_id=1, source_target_pairs={{32,0},{40,8},{48,16},{56,24},{64,32},{72,40},{80,48},{88,56},{96,... | collective-permute-start | bytes 104456 | tf_op jit(solution)/shard_map/ppermute | solution.py:89
  73.4 0.2 fusion.71
  73.6 0.2 fusion.5
  74.0 0.2 fusion.6
  74.3 0.3 fusion.12
  74.7 0.2 compare_convert_fusion
  75.0 0.2 fusion.31
  75.2 0.3 fusion.11
  75.6 0.4 pad.4
  76.1 3.4 %collective-permute-done.2 = bf16[136,128]{1,0:T(8,128)(2,1)S(1)} collective-permute-done((bf16[136,128]{1,0:T(8,128)(2,1)S(1)}, bf16[136,128]{1,0:T(8,128)(2,1)S(1)}, u32[]{:S(2)}, u32[]{:S(2)}) %collective-permute-start.2) | collective-permute-done | bytes 34848 | tf_op jit(solution)/shard_map/ppermute | solution.py:89
  79.8 0.2 fusion.7
  80.1 0.7 convolution_convert_fusion
  80.8 0.6 constant_dynamic-update-slice_fusion
  81.4 54.1 %all_to_all.21 = bf16[64,25,2,128]{3,2,1,0:T(2,128)(2,1)S(1)} all-to-all(bf16[64,25,2,128]{3,2,1,0:T(2,128)(2,1)S(1)} %constant_dynamic-update-slice_fusion), channel_id=1, replica_groups=mesh['seq'=64,'head'=8] {'seq'}, dimensions={0} | all-to-all | bytes 1638400 | tf_op jit(solution)/shard_map/all_to_all | solution.py:192
  135.6 0.5 slice.156
  136.1 0.2 copy.63
  136.4 1.1 convolution_convert_fusion.1
  (57 shorter events, 1.7 us)
Async XLA Ops:
  0.0 7.8 %copy-start.2 = (f32[512]{0:T(512)S(1)}, f32[512]{0:T(512)}, u32[]{:S(2)}) copy-start(f32[512]{0:T(512)} %param.11) | copy-start | bytes 6148
  0.0 7.9 %copy-start = (bf16[128,512]{1,0:T(8,128)(2,1)S(1)}, bf16[128,512]{1,0:T(8,128)(2,1)}, u32[]{:S(2)}) copy-start(bf16[128,512]{1,0:T(8,128)(2,1)} %param.10) | copy-start | bytes 393220
  0.0 7.9 %copy-start.1 = (bf16[128,512]{1,0:T(8,128)(2,1)S(1)}, bf16[128,512]{1,0:T(8,128)(2,1)}, u32[]{:S(2)}) copy-start(bf16[128,512]{1,0:T(8,128)(2,1)} %param.7) | copy-start | bytes 393220
  1.8 15.0 %all-to-all-start = ((bf16[4,264,128]{2,1,0:T(8,128)(2,1)}), bf16[4,264,128]{2,1,0:T(8,128)(2,1)S(1)}, u32[]{:S(2)}, u32[]{:S(2)}) async-start(bf16[4,264,128]{2,1,0:T(8,128)(2,1)} %shard_map.73), calls=%async_computation | async-start | bytes 540672 | tf_op jit(solution)/shard_map/all_to_all | solution.py:65
  17.3 13.0 %collective-permute-start = (bf16[136,128]{1,0:T(8,128)(2,1)S(1)}, bf16[136,128]{1,0:T(8,128)(2,1)S(1)}, u32[]{:S(2)}, u32[]{:S(2)}) collective-permute-start(bf16[136,128]{1,0:T(8,128)(2,1)S(1)} %pad_maximum_fusion.1), channel_id=1, source_target_pairs={{0,32},{8,40},{16,48},{24,56},{32,64},{40,72},{48,80},{56,88},{64,... | collective-permute-start | bytes 104456 | tf_op jit(solution)/shard_map/ppermute | solution.py:89
  26.7 14.5 %all-to-all-start.1 = ((bf16[4,256,128]{2,1,0:T(8,128)(2,1)}), bf16[4,256,128]{2,1,0:T(8,128)(2,1)S(1)}, u32[]{:S(2)}, u32[]{:S(2)}) async-start(bf16[4,256,128]{2,1,0:T(8,128)(2,1)} %maximum_maximum_fusion), calls=%async_computation.1 | async-start | bytes 524288 | tf_op jit(solution)/shard_map/all_to_all | solution.py:65
  30.3 10.8 %collective-permute-start.1 = (bf16[136,128]{1,0:T(8,128)(2,1)S(1)}, bf16[136,128]{1,0:T(8,128)(2,1)S(1)}, u32[]{:S(2)}, u32[]{:S(2)}) collective-permute-start(bf16[136,128]{1,0:T(8,128)(2,1)S(1)} %collective-permute-done), channel_id=1, source_target_pairs={{0,32},{8,40},{16,48},{24,56},{32,64},{40,72},{48,80},{56,88},{64,... | collective-permute-start | bytes 104456 | tf_op jit(solution)/shard_map/ppermute | solution.py:89
  59.8 16.2 %collective-permute-start.3 = (bf16[136,128]{1,0:T(8,128)(2,1)S(1)}, bf16[136,128]{1,0:T(8,128)(2,1)S(1)}, u32[]{:S(2)}, u32[]{:S(2)}) collective-permute-start(bf16[136,128]{1,0:T(8,128)(2,1)S(1)} %pad_maximum_fusion.2), channel_id=1, source_target_pairs={{64,0},{72,8},{80,16},{88,24},{96,32},{104,40},{112,48},{120,56},{... | collective-permute-start | bytes 104456 | tf_op jit(solution)/shard_map/ppermute | solution.py:89
  68.3 11.2 %collective-permute-start.2 = (bf16[136,128]{1,0:T(8,128)(2,1)S(1)}, bf16[136,128]{1,0:T(8,128)(2,1)S(1)}, u32[]{:S(2)}, u32[]{:S(2)}) collective-permute-start(bf16[136,128]{1,0:T(8,128)(2,1)S(1)} %pad_maximum_fusion.2), channel_id=1, source_target_pairs={{32,0},{40,8},{48,16},{56,24},{64,32},{72,40},{80,48},{88,56},{96,... | collective-permute-start | bytes 104456 | tf_op jit(solution)/shard_map/ppermute | solution.py:89

commit v9 on v8

--- a/solution.py
+++ b/solution.py
@@ -171,6 +171,19 @@
     index = with_layout_constraint(index, Layout((0, 1, 2, 3)))
     index, place, grad_query = together(index, place.astype(jnp.bfloat16), grad_query)
 
+    halves = slots // 8
+
+    def put(buffer, rows, at):
+        arrays = rows.shape[-1] // HS
+        packed = jnp.dot(
+            place, rows.reshape(SUB * tok_rows, arrays * HS), preferred_element_type=jnp.float32
+        ).astype(jnp.bfloat16)
+        packed = packed.reshape(seq_count, halves, 8, arrays, HS).transpose(0, 1, 3, 2, 4)
+        packed = packed.reshape(seq_count, halves * arrays * 4, 2, HS)
+        return lax.dynamic_update_slice(buffer, packed, (0, halves * at * 4, 0, 0))
+
+    packed = put(index, grad_query, 0)
+
     carry = entering(pieces, own, last, first, blocks[:, None] < blocks[None, :])
     grad_keys = mixed(back, quer, "bts,bta->bsa") + jnp.where(
         last_rows, mixed(value, carry, "bsc,bac->bsa"), 0.0
@@ -178,23 +191,18 @@
     grad_values = mixed(attn, grad, "bts,btc->bsc") + jnp.where(
         last_rows, mixed(key, carry, "bsa,bac->bsc"), 0.0
     )
-    rows = jnp.concatenate(
-        [grad_query, grad_keys.astype(jnp.bfloat16), grad_values.astype(jnp.bfloat16)], -1
-    )
-    rows = rows.reshape(SUB * tok_rows, 3 * HS)
-    packed = jnp.dot(
-        place, rows, preferred_element_type=jnp.float32
-    ).astype(jnp.bfloat16)
-    halves = slots // 8
-    packed = packed.reshape(seq_count, halves, 8, 3, HS).transpose(0, 1, 3, 2, 4)
-    packed = packed.reshape(seq_count, halves * 12, 2, HS)
-    packed = lax.dynamic_update_slice(index, packed, (0, 0, 0, 0))
+    rows = jnp.concatenate([grad_keys.astype(jnp.bfloat16), grad_values.astype(jnp.bfloat16)], -1)
+    packed = put(packed, rows, 1)
     received = lax.all_to_all(packed, "seq", 0, 0, tiled=True)
     index = received[::SUB, halves * 12, 0, :slots].astype(jnp.float32)
     choose = (index[None] == numbers[:, None, None]).astype(jnp.bfloat16)
     choose = choose.reshape(tok_rows, seq_count // SUB * slots)
-    received = received[:, : halves * 12].reshape(seq_count // SUB, SUB, halves, 3, 8, HS)
-    received = received.transpose(3, 0, 2, 4, 1, 5).reshape(3, seq_count // SUB * slots, width)
+    parts = []
+    for at, arrays in ((0, 1), (1, 2)):
+        part = received[:, halves * at * 4 : halves * (at + arrays) * 4]
+        part = part.reshape(seq_count // SUB, SUB, halves, arrays, 8, HS).transpose(3, 0, 2, 4, 1, 5)
+        parts.append(part.reshape(arrays, seq_count // SUB * slots, width))
+    received = jnp.concatenate(parts)
     rows = mixed(choose, received, "rk,jkn->jrn").astype(jnp.bfloat16)
     return rows.transpose(1, 0, 2)
 

time: 138 us -> 137 us (level)
  no operation moved by 1% of the time
where the time goes in v9:
time: 137 us
  blocking collectives  71.3 us (52%)
  starting transfers between devices  38.8 us (28%)
  waiting for transfers between devices  14.8 us (11%)
  matrix products  5.83 us (4%)
  local copies, waits for them, and re-layouts  1.99 us (1%)
  other arithmetic  1.93 us (1%)
  Pallas kernels  1.84 us (1%)
    all_to_all x1, blocking collectives, local(): received = lax.all_to_all(packed, 'seq', 0, 0, tiled=True)  54.1 us
    ppermute x4, starting transfers between devices, shifted(): return lax.ppermute(load, 'seq', pairs)  29.5 us
    all_to_all x1, blocking collectives, local(): lax.all_to_all(sums, ('seq', 'head'), 0, 0, tiled=True, axis_index_groups...  17.2 us
    all_to_all x2, starting transfers between devices, regroup(): lax.all_to_all(array, 'seq', 0, 0, tiled=True, axis_index_groups=groups)  9.3 us
    all_to_all x2, waiting for transfers between devices, regroup(): lax.all_to_all(array, 'seq', 0, 0, tiled=True, axis_index_groups=groups)  8.12 us
    ppermute x4, waiting for transfers between devices, shifted(): return lax.ppermute(load, 'seq', pairs)  6.66 us
    dot_general x15, matrix products, mixed(): return jnp.einsum(form, left, right, preferred_element_type=jnp.float32)  4.62 us
  transfers between devices with their start and end apart: 6, of which 3 were waited for; matrix products, arithmetic and copies ran while one was open for 3% of the time, Pallas kernels for 0%

profile of v9, /device:TPU:6, one launch (start us, length us, event | category | flops | bytes accessed | tf_op | source)
XLA Modules:
  0.0 136.9 jit_solution(10430663885347902271)
XLA Ops:
  0.0 1.8 %shard_map.73 = bf16[4,264,128]{2,1,0:T(8,128)(2,1)} custom-call(bf16[128,512]{1,0:T(8,128)(2,1)} %key_ref.1, bf16[128,512]{1,0:T(8,128)(2,1)} %value_ref.1, s32[1,128]{1,0:T(1,128)} %bitcast.137, s32[1,128]{1,0:T(1,128)} %bitcast.138), custom_call_target="tpu_custom_call" | custom-call | tf_op jit(solution)/shard_map/pallas_call | solution.py:67
  1.8 5.9 %all-to-all-start = ((bf16[4,264,128]{2,1,0:T(8,128)(2,1)}), bf16[4,264,128]{2,1,0:T(8,128)(2,1)S(1)}, u32[]{:S(2)}, u32[]{:S(2)}) async-start(bf16[4,264,128]{2,1,0:T(8,128)(2,1)} %shard_map.73), calls=%async_computation | async-start | bytes 540672 | tf_op jit(solution)/shard_map/all_to_all | solution.py:65
  8.0 0.7 maximum_maximum_fusion
  8.7 8.1 %all-to-all-done = bf16[4,264,128]{2,1,0:T(8,128)(2,1)S(1)} async-done(((bf16[4,264,128]{2,1,0:T(8,128)(2,1)}), bf16[4,264,128]{2,1,0:T(8,128)(2,1)S(1)}, u32[]{:S(2)}, u32[]{:S(2)}) %all-to-all-start) | async-done | bytes 270368 | tf_op jit(solution)/shard_map/all_to_all | solution.py:65
  16.9 0.3 fusion.9
  17.3 9.1 %collective-permute-start = (bf16[136,128]{1,0:T(8,128)(2,1)S(1)}, bf16[136,128]{1,0:T(8,128)(2,1)S(1)}, u32[]{:S(2)}, u32[]{:S(2)}) collective-permute-start(bf16[136,128]{1,0:T(8,128)(2,1)S(1)} %pad_maximum_fusion.1), channel_id=1, source_target_pairs={{0,32},{8,40},{16,48},{24,56},{32,64},{40,72},{48,80},{56,88},{64,... | collective-permute-start | bytes 104456 | tf_op jit(solution)/shard_map/ppermute | solution.py:89
  26.4 0.3 fusion.22
  26.7 3.4 %all-to-all-start.1 = ((bf16[4,256,128]{2,1,0:T(8,128)(2,1)}), bf16[4,256,128]{2,1,0:T(8,128)(2,1)S(1)}, u32[]{:S(2)}, u32[]{:S(2)}) async-start(bf16[4,256,128]{2,1,0:T(8,128)(2,1)} %maximum_maximum_fusion), calls=%async_computation.1 | async-start | bytes 524288 | tf_op jit(solution)/shard_map/all_to_all | solution.py:65
  30.3 6.9 %collective-permute-start.1 = (bf16[136,128]{1,0:T(8,128)(2,1)S(1)}, bf16[136,128]{1,0:T(8,128)(2,1)S(1)}, u32[]{:S(2)}, u32[]{:S(2)}) collective-permute-start(bf16[136,128]{1,0:T(8,128)(2,1)S(1)} %collective-permute-done), channel_id=1, source_target_pairs={{0,32},{8,40},{16,48},{24,56},{32,64},{40,72},{48,80},{56,88},{64,... | collective-permute-start | bytes 104456 | tf_op jit(solution)/shard_map/ppermute | solution.py:89
  37.2 3.9 %collective-permute-done.1 = bf16[136,128]{1,0:T(8,128)(2,1)S(1)} collective-permute-done((bf16[136,128]{1,0:T(8,128)(2,1)S(1)}, bf16[136,128]{1,0:T(8,128)(2,1)S(1)}, u32[]{:S(2)}, u32[]{:S(2)}) %collective-permute-start.1) | collective-permute-done | bytes 34848 | tf_op jit(solution)/shard_map/ppermute | solution.py:89
  41.2 0.2 fusion.4
  41.6 0.4 multiply_reduce_fusion.1
  42.0 17.2 %all_to_all.20 = f32[32,8,128]{2,1,0:T(8,128)S(1)} all-to-all(f32[32,8,128]{2,1,0:T(8,128)S(1)} %broadcast_in_dim.237), channel_id=1, replica_groups={{0,1,2,3,4,5,6,7,8,9,10,11,12,13,14,15,16,17,18,19,20,21,22,23,24,25,26..., dimensions={0} | all-to-all | bytes 262144 | tf_op jit(solution)/shard_map/all_to_all | solution.py:138
  59.5 0.3 fusion.10
  59.8 8.4 %collective-permute-start.3 = (bf16[136,128]{1,0:T(8,128)(2,1)S(1)}, bf16[136,128]{1,0:T(8,128)(2,1)S(1)}, u32[]{:S(2)}, u32[]{:S(2)}) collective-permute-start(bf16[136,128]{1,0:T(8,128)(2,1)S(1)} %pad_maximum_fusion.2), channel_id=1, source_target_pairs={{64,0},{72,8},{80,16},{88,24},{96,32},{104,40},{112,48},{120,56},{... | collective-permute-start | bytes 104456 | tf_op jit(solution)/shard_map/ppermute | solution.py:89
  68.3 5.1 %collective-permute-start.2 = (bf16[136,128]{1,0:T(8,128)(2,1)S(1)}, bf16[136,128]{1,0:T(8,128)(2,1)S(1)}, u32[]{:S(2)}, u32[]{:S(2)}) collective-permute-start(bf16[136,128]{1,0:T(8,128)(2,1)S(1)} %pad_maximum_fusion.2), channel_id=1, source_target_pairs={{32,0},{40,8},{48,16},{56,24},{64,32},{72,40},{80,48},{88,56},{96,... | collective-permute-start | bytes 104456 | tf_op jit(solution)/shard_map/ppermute | solution.py:89
  73.4 0.2 fusion.75
  73.6 0.2 fusion.5
  74.0 0.2 fusion.6
  74.3 0.3 fusion.11
  74.7 0.2 compare_convert_fusion
  75.0 0.4 pad.4
  75.4 0.3 fusion.15
  75.8 0.4 convolution_convert_fusion.2
  76.3 0.2 fusion.34
  76.7 2.8 %collective-permute-done.2 = bf16[136,128]{1,0:T(8,128)(2,1)S(1)} collective-permute-done((bf16[136,128]{1,0:T(8,128)(2,1)S(1)}, bf16[136,128]{1,0:T(8,128)(2,1)S(1)}, u32[]{:S(2)}, u32[]{:S(2)}) %collective-permute-start.2) | collective-permute-done | bytes 34848 | tf_op jit(solution)/shard_map/ppermute | solution.py:89
  79.6 0.2 fusion.7
  80.1 0.4 convolution_convert_fusion
  80.5 0.4 constant_dynamic-update-slice_fusion
  80.9 54.1 %all_to_all.21 = bf16[64,25,2,128]{3,2,1,0:T(2,128)(2,1)S(1)} all-to-all(bf16[64,25,2,128]{3,2,1,0:T(2,128)(2,1)S(1)} %constant_dynamic-update-slice_fusion), channel_id=1, replica_groups=mesh['seq'=64,'head'=8] {'seq'}, dimensions={0} | all-to-all | bytes 1638400 | tf_op jit(solution)/shard_map/all_to_all | solution.py:196
  135.0 0.4 slice.161
  135.9 1.1 convolution_convert_fusion.1
  (61 shorter events, 2.3 us)
Async XLA Ops:
  0.0 7.8 %copy-start.2 = (f32[512]{0:T(512)S(1)}, f32[512]{0:T(512)}, u32[]{:S(2)}) copy-start(f32[512]{0:T(512)} %param.11) | copy-start | bytes 6148
  0.0 7.9 %copy-start = (bf16[128,512]{1,0:T(8,128)(2,1)S(1)}, bf16[128,512]{1,0:T(8,128)(2,1)}, u32[]{:S(2)}) copy-start(bf16[128,512]{1,0:T(8,128)(2,1)} %param.10) | copy-start | bytes 393220
  0.0 7.9 %copy-start.1 = (bf16[128,512]{1,0:T(8,128)(2,1)S(1)}, bf16[128,512]{1,0:T(8,128)(2,1)}, u32[]{:S(2)}) copy-start(bf16[128,512]{1,0:T(8,128)(2,1)} %param.7) | copy-start | bytes 393220
  1.8 15.0 %all-to-all-start = ((bf16[4,264,128]{2,1,0:T(8,128)(2,1)}), bf16[4,264,128]{2,1,0:T(8,128)(2,1)S(1)}, u32[]{:S(2)}, u32[]{:S(2)}) async-start(bf16[4,264,128]{2,1,0:T(8,128)(2,1)} %shard_map.73), calls=%async_computation | async-start | bytes 540672 | tf_op jit(solution)/shard_map/all_to_all | solution.py:65
  17.3 13.0 %collective-permute-start = (bf16[136,128]{1,0:T(8,128)(2,1)S(1)}, bf16[136,128]{1,0:T(8,128)(2,1)S(1)}, u32[]{:S(2)}, u32[]{:S(2)}) collective-permute-start(bf16[136,128]{1,0:T(8,128)(2,1)S(1)} %pad_maximum_fusion.1), channel_id=1, source_target_pairs={{0,32},{8,40},{16,48},{24,56},{32,64},{40,72},{48,80},{56,88},{64,... | collective-permute-start | bytes 104456 | tf_op jit(solution)/shard_map/ppermute | solution.py:89
  26.7 14.5 %all-to-all-start.1 = ((bf16[4,256,128]{2,1,0:T(8,128)(2,1)}), bf16[4,256,128]{2,1,0:T(8,128)(2,1)S(1)}, u32[]{:S(2)}, u32[]{:S(2)}) async-start(bf16[4,256,128]{2,1,0:T(8,128)(2,1)} %maximum_maximum_fusion), calls=%async_computation.1 | async-start | bytes 524288 | tf_op jit(solution)/shard_map/all_to_all | solution.py:65
  30.3 10.8 %collective-permute-start.1 = (bf16[136,128]{1,0:T(8,128)(2,1)S(1)}, bf16[136,128]{1,0:T(8,128)(2,1)S(1)}, u32[]{:S(2)}, u32[]{:S(2)}) collective-permute-start(bf16[136,128]{1,0:T(8,128)(2,1)S(1)} %collective-permute-done), channel_id=1, source_target_pairs={{0,32},{8,40},{16,48},{24,56},{32,64},{40,72},{48,80},{56,88},{64,... | collective-permute-start | bytes 104456 | tf_op jit(solution)/shard_map/ppermute | solution.py:89
  59.8 16.9 %collective-permute-start.3 = (bf16[136,128]{1,0:T(8,128)(2,1)S(1)}, bf16[136,128]{1,0:T(8,128)(2,1)S(1)}, u32[]{:S(2)}, u32[]{:S(2)}) collective-permute-start(bf16[136,128]{1,0:T(8,128)(2,1)S(1)} %pad_maximum_fusion.2), channel_id=1, source_target_pairs={{64,0},{72,8},{80,16},{88,24},{96,32},{104,40},{112,48},{120,56},{... | collective-permute-start | bytes 104456 | tf_op jit(solution)/shard_map/ppermute | solution.py:89
  68.3 11.2 %collective-permute-start.2 = (bf16[136,128]{1,0:T(8,128)(2,1)S(1)}, bf16[136,128]{1,0:T(8,128)(2,1)S(1)}, u32[]{:S(2)}, u32[]{:S(2)}) collective-permute-start(bf16[136,128]{1,0:T(8,128)(2,1)S(1)} %pad_maximum_fusion.2), channel_id=1, source_target_pairs={{32,0},{40,8},{48,16},{56,24},{64,32},{72,40},{80,48},{88,56},{96,... | collective-permute-start | bytes 104456 | tf_op jit(solution)/shard_map/ppermute | solution.py:89

commit v10 on v9

--- a/solution.py
+++ b/solution.py
@@ -57,7 +57,7 @@
     capacity = 2 * tok_rows // seq_count
     slots = SUB * capacity
     groups = [[g * SUB + s for s in range(SUB)] for g in range(seq_count // SUB)]
-    wide_groups = [[i * head_count + h for i in one for h in range(head_count)] for one in groups]
+    wide_groups = [[i * head_count + h for h in range(head_count) for i in one] for one in groups]
     places = jnp.arange(tok_rows)
     blocks = jnp.arange(SUB)
 

time: 137 us -> 135 us (0.985)
  blocking collectives: 71.3 us -> 69.3 us
    all_to_all x1, blocking collectives: 54.1 us -> 51.8 us  [local(): received = lax.all_to_all(packed, 'seq', 0, 0, tiled=True)]
  transfers between devices with their start and end apart: 6 -> 6, of which waited for: 3 -> 3; matrix products, arithmetic and copies ran while one was open for 3% -> 4% of each run, Pallas kernels for 0% -> 0%
where the time goes in v10:
time: 135 us
  blocking collectives  69.3 us (51%)
  starting transfers between devices  38.8 us (29%)
  waiting for transfers between devices  14.3 us (11%)
  matrix products  5.83 us (4%)
  local copies, waits for them, and re-layouts  1.99 us (1%)
  other arithmetic  1.93 us (1%)
  Pallas kernels  1.84 us (1%)
    all_to_all x1, blocking collectives, local(): received = lax.all_to_all(packed, 'seq', 0, 0, tiled=True)  51.8 us
    ppermute x4, starting transfers between devices, shifted(): return lax.ppermute(load, 'seq', pairs)  29.5 us
    all_to_all x1, blocking collectives, local(): lax.all_to_all(sums, ('seq', 'head'), 0, 0, tiled=True, axis_index_groups...  17.6 us
    all_to_all x2, starting transfers between devices, regroup(): lax.all_to_all(array, 'seq', 0, 0, tiled=True, axis_index_groups=groups)  9.3 us
    all_to_all x2, waiting for transfers between devices, regroup(): lax.all_to_all(array, 'seq', 0, 0, tiled=True, axis_index_groups=groups)  8.12 us
    ppermute x4, waiting for transfers between devices, shifted(): return lax.ppermute(load, 'seq', pairs)  6.18 us
    dot_general x15, matrix products, mixed(): return jnp.einsum(form, left, right, preferred_element_type=jnp.float32)  4.62 us
  transfers between devices with their start and end apart: 6, of which 3 were waited for; matrix products, arithmetic and copies ran while one was open for 4% of the time, Pallas kernels for 0%

profile of v10, /device:TPU:6, one launch (start us, length us, event | category | flops | bytes accessed | tf_op | source)
XLA Modules:
  0.0 134.5 jit_solution(16263304877931210959)
XLA Ops:
  0.0 1.8 %shard_map.73 = bf16[4,264,128]{2,1,0:T(8,128)(2,1)} custom-call(bf16[128,512]{1,0:T(8,128)(2,1)} %key_ref.1, bf16[128,512]{1,0:T(8,128)(2,1)} %value_ref.1, s32[1,128]{1,0:T(1,128)} %bitcast.137, s32[1,128]{1,0:T(1,128)} %bitcast.138), custom_call_target="tpu_custom_call" | custom-call | tf_op jit(solution)/shard_map/pallas_call | solution.py:67
  1.8 5.9 %all-to-all-start = ((bf16[4,264,128]{2,1,0:T(8,128)(2,1)}), bf16[4,264,128]{2,1,0:T(8,128)(2,1)S(1)}, u32[]{:S(2)}, u32[]{:S(2)}) async-start(bf16[4,264,128]{2,1,0:T(8,128)(2,1)} %shard_map.73), calls=%async_computation | async-start | bytes 540672 | tf_op jit(solution)/shard_map/all_to_all | solution.py:65
  8.0 0.7 maximum_maximum_fusion
  8.7 8.1 %all-to-all-done = bf16[4,264,128]{2,1,0:T(8,128)(2,1)S(1)} async-done(((bf16[4,264,128]{2,1,0:T(8,128)(2,1)}), bf16[4,264,128]{2,1,0:T(8,128)(2,1)S(1)}, u32[]{:S(2)}, u32[]{:S(2)}) %all-to-all-start) | async-done | bytes 270368 | tf_op jit(solution)/shard_map/all_to_all | solution.py:65
  16.9 0.3 fusion.9
  17.3 9.1 %collective-permute-start = (bf16[136,128]{1,0:T(8,128)(2,1)S(1)}, bf16[136,128]{1,0:T(8,128)(2,1)S(1)}, u32[]{:S(2)}, u32[]{:S(2)}) collective-permute-start(bf16[136,128]{1,0:T(8,128)(2,1)S(1)} %pad_maximum_fusion.1), channel_id=1, source_target_pairs={{0,32},{8,40},{16,48},{24,56},{32,64},{40,72},{48,80},{56,88},{64,... | collective-permute-start | bytes 104456 | tf_op jit(solution)/shard_map/ppermute | solution.py:89
  26.4 0.3 fusion.22
  26.7 3.4 %all-to-all-start.1 = ((bf16[4,256,128]{2,1,0:T(8,128)(2,1)}), bf16[4,256,128]{2,1,0:T(8,128)(2,1)S(1)}, u32[]{:S(2)}, u32[]{:S(2)}) async-start(bf16[4,256,128]{2,1,0:T(8,128)(2,1)} %maximum_maximum_fusion), calls=%async_computation.1 | async-start | bytes 524288 | tf_op jit(solution)/shard_map/all_to_all | solution.py:65
  30.3 6.9 %collective-permute-start.1 = (bf16[136,128]{1,0:T(8,128)(2,1)S(1)}, bf16[136,128]{1,0:T(8,128)(2,1)S(1)}, u32[]{:S(2)}, u32[]{:S(2)}) collective-permute-start(bf16[136,128]{1,0:T(8,128)(2,1)S(1)} %collective-permute-done), channel_id=1, source_target_pairs={{0,32},{8,40},{16,48},{24,56},{32,64},{40,72},{48,80},{56,88},{64,... | collective-permute-start | bytes 104456 | tf_op jit(solution)/shard_map/ppermute | solution.py:89
  37.2 3.9 %collective-permute-done.1 = bf16[136,128]{1,0:T(8,128)(2,1)S(1)} collective-permute-done((bf16[136,128]{1,0:T(8,128)(2,1)S(1)}, bf16[136,128]{1,0:T(8,128)(2,1)S(1)}, u32[]{:S(2)}, u32[]{:S(2)}) %collective-permute-start.1) | collective-permute-done | bytes 34848 | tf_op jit(solution)/shard_map/ppermute | solution.py:89
  41.2 0.2 fusion.4
  41.6 0.4 multiply_reduce_fusion.1
  42.0 17.6 %all_to_all.20 = f32[32,8,128]{2,1,0:T(8,128)S(1)} all-to-all(f32[32,8,128]{2,1,0:T(8,128)S(1)} %broadcast_in_dim.237), channel_id=1, replica_groups={{0,8,16,24,1,9,17,25,2,10,18,26,3,11,19,27,4,12,20,28,5,13,21,29,6,14,2..., dimensions={0} | all-to-all | bytes 262144 | tf_op jit(solution)/shard_map/all_to_all | solution.py:138
  59.8 0.3 fusion.10
  60.2 8.4 %collective-permute-start.3 = (bf16[136,128]{1,0:T(8,128)(2,1)S(1)}, bf16[136,128]{1,0:T(8,128)(2,1)S(1)}, u32[]{:S(2)}, u32[]{:S(2)}) collective-permute-start(bf16[136,128]{1,0:T(8,128)(2,1)S(1)} %pad_maximum_fusion.2), channel_id=1, source_target_pairs={{64,0},{72,8},{80,16},{88,24},{96,32},{104,40},{112,48},{120,56},{... | collective-permute-start | bytes 104456 | tf_op jit(solution)/shard_map/ppermute | solution.py:89
  68.7 5.1 %collective-permute-start.2 = (bf16[136,128]{1,0:T(8,128)(2,1)S(1)}, bf16[136,128]{1,0:T(8,128)(2,1)S(1)}, u32[]{:S(2)}, u32[]{:S(2)}) collective-permute-start(bf16[136,128]{1,0:T(8,128)(2,1)S(1)} %pad_maximum_fusion.2), channel_id=1, source_target_pairs={{32,0},{40,8},{48,16},{56,24},{64,32},{72,40},{80,48},{88,56},{96,... | collective-permute-start | bytes 104456 | tf_op jit(solution)/shard_map/ppermute | solution.py:89
  73.8 0.2 fusion.75
  74.0 0.2 fusion.5
  74.4 0.2 fusion.6
  74.7 0.3 fusion.11
  75.1 0.2 compare_convert_fusion
  75.3 0.4 pad.4
  75.8 0.3 fusion.15
  76.2 0.4 convolution_convert_fusion.2
  76.6 0.2 fusion.34
  77.1 2.3 %collective-permute-done.2 = bf16[136,128]{1,0:T(8,128)(2,1)S(1)} collective-permute-done((bf16[136,128]{1,0:T(8,128)(2,1)S(1)}, bf16[136,128]{1,0:T(8,128)(2,1)S(1)}, u32[]{:S(2)}, u32[]{:S(2)}) %collective-permute-start.2) | collective-permute-done | bytes 34848 | tf_op jit(solution)/shard_map/ppermute | solution.py:89
  79.5 0.2 fusion.7
  80.0 0.4 convolution_convert_fusion
  80.4 0.4 constant_dynamic-update-slice_fusion
  80.8 51.8 %all_to_all.21 = bf16[64,25,2,128]{3,2,1,0:T(2,128)(2,1)S(1)} all-to-all(bf16[64,25,2,128]{3,2,1,0:T(2,128)(2,1)S(1)} %constant_dynamic-update-slice_fusion), channel_id=1, replica_groups=mesh['seq'=64,'head'=8] {'seq'}, dimensions={0} | all-to-all | bytes 1638400 | tf_op jit(solution)/shard_map/all_to_all | solution.py:196
  132.6 0.4 slice.161
  133.4 1.1 convolution_convert_fusion.1
  (61 shorter events, 2.3 us)
Async XLA Ops:
  0.0 7.8 %copy-start.2 = (f32[512]{0:T(512)S(1)}, f32[512]{0:T(512)}, u32[]{:S(2)}) copy-start(f32[512]{0:T(512)} %param.11) | copy-start | bytes 6148
  0.0 7.9 %copy-start = (bf16[128,512]{1,0:T(8,128)(2,1)S(1)}, bf16[128,512]{1,0:T(8,128)(2,1)}, u32[]{:S(2)}) copy-start(bf16[128,512]{1,0:T(8,128)(2,1)} %param.10) | copy-start | bytes 393220
  0.0 7.9 %copy-start.1 = (bf16[128,512]{1,0:T(8,128)(2,1)S(1)}, bf16[128,512]{1,0:T(8,128)(2,1)}, u32[]{:S(2)}) copy-start(bf16[128,512]{1,0:T(8,128)(2,1)} %param.7) | copy-start | bytes 393220
  1.8 15.0 %all-to-all-start = ((bf16[4,264,128]{2,1,0:T(8,128)(2,1)}), bf16[4,264,128]{2,1,0:T(8,128)(2,1)S(1)}, u32[]{:S(2)}, u32[]{:S(2)}) async-start(bf16[4,264,128]{2,1,0:T(8,128)(2,1)} %shard_map.73), calls=%async_computation | async-start | bytes 540672 | tf_op jit(solution)/shard_map/all_to_all | solution.py:65
  17.3 13.0 %collective-permute-start = (bf16[136,128]{1,0:T(8,128)(2,1)S(1)}, bf16[136,128]{1,0:T(8,128)(2,1)S(1)}, u32[]{:S(2)}, u32[]{:S(2)}) collective-permute-start(bf16[136,128]{1,0:T(8,128)(2,1)S(1)} %pad_maximum_fusion.1), channel_id=1, source_target_pairs={{0,32},{8,40},{16,48},{24,56},{32,64},{40,72},{48,80},{56,88},{64,... | collective-permute-start | bytes 104456 | tf_op jit(solution)/shard_map/ppermute | solution.py:89
  26.7 14.5 %all-to-all-start.1 = ((bf16[4,256,128]{2,1,0:T(8,128)(2,1)}), bf16[4,256,128]{2,1,0:T(8,128)(2,1)S(1)}, u32[]{:S(2)}, u32[]{:S(2)}) async-start(bf16[4,256,128]{2,1,0:T(8,128)(2,1)} %maximum_maximum_fusion), calls=%async_computation.1 | async-start | bytes 524288 | tf_op jit(solution)/shard_map/all_to_all | solution.py:65
  30.3 10.8 %collective-permute-start.1 = (bf16[136,128]{1,0:T(8,128)(2,1)S(1)}, bf16[136,128]{1,0:T(8,128)(2,1)S(1)}, u32[]{:S(2)}, u32[]{:S(2)}) collective-permute-start(bf16[136,128]{1,0:T(8,128)(2,1)S(1)} %collective-permute-done), channel_id=1, source_target_pairs={{0,32},{8,40},{16,48},{24,56},{32,64},{40,72},{48,80},{56,88},{64,... | collective-permute-start | bytes 104456 | tf_op jit(solution)/shard_map/ppermute | solution.py:89
  60.2 16.9 %collective-permute-start.3 = (bf16[136,128]{1,0:T(8,128)(2,1)S(1)}, bf16[136,128]{1,0:T(8,128)(2,1)S(1)}, u32[]{:S(2)}, u32[]{:S(2)}) collective-permute-start(bf16[136,128]{1,0:T(8,128)(2,1)S(1)} %pad_maximum_fusion.2), channel_id=1, source_target_pairs={{64,0},{72,8},{80,16},{88,24},{96,32},{104,40},{112,48},{120,56},{... | collective-permute-start | bytes 104456 | tf_op jit(solution)/shard_map/ppermute | solution.py:89
  68.7 10.7 %collective-permute-start.2 = (bf16[136,128]{1,0:T(8,128)(2,1)S(1)}, bf16[136,128]{1,0:T(8,128)(2,1)S(1)}, u32[]{:S(2)}, u32[]{:S(2)}) collective-permute-start(bf16[136,128]{1,0:T(8,128)(2,1)S(1)} %pad_maximum_fusion.2), channel_id=1, source_target_pairs={{32,0},{40,8},{48,16},{56,24},{64,32},{72,40},{80,48},{88,56},{96,... | collective-permute-start | bytes 104456 | tf_op jit(solution)/shard_map/ppermute | solution.py:89

commit v11 on v10

--- a/solution.py
+++ b/solution.py
@@ -57,7 +57,7 @@
     capacity = 2 * tok_rows // seq_count
     slots = SUB * capacity
     groups = [[g * SUB + s for s in range(SUB)] for g in range(seq_count // SUB)]
-    wide_groups = [[i * head_count + h for h in range(head_count) for i in one] for one in groups]
+    wide_groups = [[i * head_count + h for h in reversed(range(head_count)) for i in one] for one in groups]
     places = jnp.arange(tok_rows)
     blocks = jnp.arange(SUB)
 

time: 135 us -> 136 us (level)
    all_to_all x1, blocking collectives: 51.8 us -> 53.7 us  [local(): received = lax.all_to_all(packed, 'seq', 0, 0, tiled=True)]
where the time goes in v11:
time: 136 us; the launch traced here: 135 us
  blocking collectives  69.9 us (51%)
  starting transfers between devices  38.8 us (29%)
  waiting for transfers between devices  14.3 us (11%)
  matrix products  5.83 us (4%)
  local copies, waits for them, and re-layouts  1.99 us (1%)
  other arithmetic  1.93 us (1%)
  Pallas kernels  1.84 us (1%)
    all_to_all x1, blocking collectives, local(): received = lax.all_to_all(packed, 'seq', 0, 0, tiled=True)  53.7 us
    ppermute x4, starting transfers between devices, shifted(): return lax.ppermute(load, 'seq', pairs)  29.5 us
    all_to_all x1, blocking collectives, local(): lax.all_to_all(sums, ('seq', 'head'), 0, 0, tiled=True, axis_index_groups...  16.2 us
    all_to_all x2, starting transfers between devices, regroup(): lax.all_to_all(array, 'seq', 0, 0, tiled=True, axis_index_groups=groups)  9.3 us
    all_to_all x2, waiting for transfers between devices, regroup(): lax.all_to_all(array, 'seq', 0, 0, tiled=True, axis_index_groups=groups)  8.12 us
    ppermute x4, waiting for transfers between devices, shifted(): return lax.ppermute(load, 'seq', pairs)  6.15 us
    dot_general x15, matrix products, mixed(): return jnp.einsum(form, left, right, preferred_element_type=jnp.float32)  4.62 us
  transfers between devices with their start and end apart: 6, of which 3 were waited for; matrix products, arithmetic and copies ran while one was open for 4% of the time, Pallas kernels for 0%

profile of v11, /device:TPU:6, one launch (start us, length us, event | category | flops | bytes accessed | tf_op | source)
XLA Modules:
  0.0 135.1 jit_solution(8266341384313479289)
XLA Ops:
  0.0 1.8 %shard_map.73 = bf16[4,264,128]{2,1,0:T(8,128)(2,1)} custom-call(bf16[128,512]{1,0:T(8,128)(2,1)} %key_ref.1, bf16[128,512]{1,0:T(8,128)(2,1)} %value_ref.1, s32[1,128]{1,0:T(1,128)} %bitcast.137, s32[1,128]{1,0:T(1,128)} %bitcast.138), custom_call_target="tpu_custom_call" | custom-call | tf_op jit(solution)/shard_map/pallas_call | solution.py:67
  1.8 5.9 %all-to-all-start = ((bf16[4,264,128]{2,1,0:T(8,128)(2,1)}), bf16[4,264,128]{2,1,0:T(8,128)(2,1)S(1)}, u32[]{:S(2)}, u32[]{:S(2)}) async-start(bf16[4,264,128]{2,1,0:T(8,128)(2,1)} %shard_map.73), calls=%async_computation | async-start | bytes 540672 | tf_op jit(solution)/shard_map/all_to_all | solution.py:65
  8.0 0.7 maximum_maximum_fusion
  8.7 8.1 %all-to-all-done = bf16[4,264,128]{2,1,0:T(8,128)(2,1)S(1)} async-done(((bf16[4,264,128]{2,1,0:T(8,128)(2,1)}), bf16[4,264,128]{2,1,0:T(8,128)(2,1)S(1)}, u32[]{:S(2)}, u32[]{:S(2)}) %all-to-all-start) | async-done | bytes 270368 | tf_op jit(solution)/shard_map/all_to_all | solution.py:65
  16.9 0.3 fusion.9
  17.3 9.1 %collective-permute-start = (bf16[136,128]{1,0:T(8,128)(2,1)S(1)}, bf16[136,128]{1,0:T(8,128)(2,1)S(1)}, u32[]{:S(2)}, u32[]{:S(2)}) collective-permute-start(bf16[136,128]{1,0:T(8,128)(2,1)S(1)} %pad_maximum_fusion.1), channel_id=1, source_target_pairs={{0,32},{8,40},{16,48},{24,56},{32,64},{40,72},{48,80},{56,88},{64,... | collective-permute-start | bytes 104456 | tf_op jit(solution)/shard_map/ppermute | solution.py:89
  26.4 0.3 fusion.22
  26.7 3.4 %all-to-all-start.1 = ((bf16[4,256,128]{2,1,0:T(8,128)(2,1)}), bf16[4,256,128]{2,1,0:T(8,128)(2,1)S(1)}, u32[]{:S(2)}, u32[]{:S(2)}) async-start(bf16[4,256,128]{2,1,0:T(8,128)(2,1)} %maximum_maximum_fusion), calls=%async_computation.1 | async-start | bytes 524288 | tf_op jit(solution)/shard_map/all_to_all | solution.py:65
  30.3 6.9 %collective-permute-start.1 = (bf16[136,128]{1,0:T(8,128)(2,1)S(1)}, bf16[136,128]{1,0:T(8,128)(2,1)S(1)}, u32[]{:S(2)}, u32[]{:S(2)}) collective-permute-start(bf16[136,128]{1,0:T(8,128)(2,1)S(1)} %collective-permute-done), channel_id=1, source_target_pairs={{0,32},{8,40},{16,48},{24,56},{32,64},{40,72},{48,80},{56,88},{64,... | collective-permute-start | bytes 104456 | tf_op jit(solution)/shard_map/ppermute | solution.py:89
  37.2 3.9 %collective-permute-done.1 = bf16[136,128]{1,0:T(8,128)(2,1)S(1)} collective-permute-done((bf16[136,128]{1,0:T(8,128)(2,1)S(1)}, bf16[136,128]{1,0:T(8,128)(2,1)S(1)}, u32[]{:S(2)}, u32[]{:S(2)}) %collective-permute-start.1) | collective-permute-done | bytes 34848 | tf_op jit(solution)/shard_map/ppermute | solution.py:89
  41.2 0.2 fusion.4
  41.6 0.4 multiply_reduce_fusion.1
  42.0 16.2 %all_to_all.20 = f32[32,8,128]{2,1,0:T(8,128)S(1)} all-to-all(f32[32,8,128]{2,1,0:T(8,128)S(1)} %broadcast_in_dim.237), channel_id=1, replica_groups={{7,15,23,31,6,14,22,30,5,13,21,29,4,12,20,28,3,11,19,27,2,10,18,26,1,9,..., dimensions={0} | all-to-all | bytes 262144 | tf_op jit(solution)/shard_map/all_to_all | solution.py:138
  58.5 0.3 fusion.10
  58.9 8.4 %collective-permute-start.3 = (bf16[136,128]{1,0:T(8,128)(2,1)S(1)}, bf16[136,128]{1,0:T(8,128)(2,1)S(1)}, u32[]{:S(2)}, u32[]{:S(2)}) collective-permute-start(bf16[136,128]{1,0:T(8,128)(2,1)S(1)} %pad_maximum_fusion.2), channel_id=1, source_target_pairs={{64,0},{72,8},{80,16},{88,24},{96,32},{104,40},{112,48},{120,56},{... | collective-permute-start | bytes 104456 | tf_op jit(solution)/shard_map/ppermute | solution.py:89
  67.3 5.1 %collective-permute-start.2 = (bf16[136,128]{1,0:T(8,128)(2,1)S(1)}, bf16[136,128]{1,0:T(8,128)(2,1)S(1)}, u32[]{:S(2)}, u32[]{:S(2)}) collective-permute-start(bf16[136,128]{1,0:T(8,128)(2,1)S(1)} %pad_maximum_fusion.2), channel_id=1, source_target_pairs={{32,0},{40,8},{48,16},{56,24},{64,32},{72,40},{80,48},{88,56},{96,... | collective-permute-start | bytes 104456 | tf_op jit(solution)/shard_map/ppermute | solution.py:89
  72.4 0.2 fusion.75
  72.7 0.2 fusion.5
  73.1 0.2 fusion.6
  73.4 0.3 fusion.11
  73.8 0.2 compare_convert_fusion
  74.0 0.4 pad.4
  74.5 0.3 fusion.15
  74.9 0.4 convolution_convert_fusion.2
  75.3 0.2 fusion.34
  75.8 2.3 %collective-permute-done.2 = bf16[136,128]{1,0:T(8,128)(2,1)S(1)} collective-permute-done((bf16[136,128]{1,0:T(8,128)(2,1)S(1)}, bf16[136,128]{1,0:T(8,128)(2,1)S(1)}, u32[]{:S(2)}, u32[]{:S(2)}) %collective-permute-start.2) | collective-permute-done | bytes 34848 | tf_op jit(solution)/shard_map/ppermute | solution.py:89
  78.1 0.2 fusion.7
  78.6 0.4 convolution_convert_fusion
  79.0 0.4 constant_dynamic-update-slice_fusion
  79.4 53.7 %all_to_all.21 = bf16[64,25,2,128]{3,2,1,0:T(2,128)(2,1)S(1)} all-to-all(bf16[64,25,2,128]{3,2,1,0:T(2,128)(2,1)S(1)} %constant_dynamic-update-slice_fusion), channel_id=1, replica_groups=mesh['seq'=64,'head'=8] {'seq'}, dimensions={0} | all-to-all | bytes 1638400 | tf_op jit(solution)/shard_map/all_to_all | solution.py:196
  133.2 0.4 slice.161
  134.0 1.1 convolution_convert_fusion.1
  (61 shorter events, 2.3 us)
Async XLA Ops:
  0.0 7.8 %copy-start.2 = (f32[512]{0:T(512)S(1)}, f32[512]{0:T(512)}, u32[]{:S(2)}) copy-start(f32[512]{0:T(512)} %param.11) | copy-start | bytes 6148
  0.0 7.9 %copy-start = (bf16[128,512]{1,0:T(8,128)(2,1)S(1)}, bf16[128,512]{1,0:T(8,128)(2,1)}, u32[]{:S(2)}) copy-start(bf16[128,512]{1,0:T(8,128)(2,1)} %param.10) | copy-start | bytes 393220
  0.0 7.9 %copy-start.1 = (bf16[128,512]{1,0:T(8,128)(2,1)S(1)}, bf16[128,512]{1,0:T(8,128)(2,1)}, u32[]{:S(2)}) copy-start(bf16[128,512]{1,0:T(8,128)(2,1)} %param.7) | copy-start | bytes 393220
  1.8 15.0 %all-to-all-start = ((bf16[4,264,128]{2,1,0:T(8,128)(2,1)}), bf16[4,264,128]{2,1,0:T(8,128)(2,1)S(1)}, u32[]{:S(2)}, u32[]{:S(2)}) async-start(bf16[4,264,128]{2,1,0:T(8,128)(2,1)} %shard_map.73), calls=%async_computation | async-start | bytes 540672 | tf_op jit(solution)/shard_map/all_to_all | solution.py:65
  17.3 13.0 %collective-permute-start = (bf16[136,128]{1,0:T(8,128)(2,1)S(1)}, bf16[136,128]{1,0:T(8,128)(2,1)S(1)}, u32[]{:S(2)}, u32[]{:S(2)}) collective-permute-start(bf16[136,128]{1,0:T(8,128)(2,1)S(1)} %pad_maximum_fusion.1), channel_id=1, source_target_pairs={{0,32},{8,40},{16,48},{24,56},{32,64},{40,72},{48,80},{56,88},{64,... | collective-permute-start | bytes 104456 | tf_op jit(solution)/shard_map/ppermute | solution.py:89
  26.7 14.5 %all-to-all-start.1 = ((bf16[4,256,128]{2,1,0:T(8,128)(2,1)}), bf16[4,256,128]{2,1,0:T(8,128)(2,1)S(1)}, u32[]{:S(2)}, u32[]{:S(2)}) async-start(bf16[4,256,128]{2,1,0:T(8,128)(2,1)} %maximum_maximum_fusion), calls=%async_computation.1 | async-start | bytes 524288 | tf_op jit(solution)/shard_map/all_to_all | solution.py:65
  30.3 10.8 %collective-permute-start.1 = (bf16[136,128]{1,0:T(8,128)(2,1)S(1)}, bf16[136,128]{1,0:T(8,128)(2,1)S(1)}, u32[]{:S(2)}, u32[]{:S(2)}) collective-permute-start(bf16[136,128]{1,0:T(8,128)(2,1)S(1)} %collective-permute-done), channel_id=1, source_target_pairs={{0,32},{8,40},{16,48},{24,56},{32,64},{40,72},{48,80},{56,88},{64,... | collective-permute-start | bytes 104456 | tf_op jit(solution)/shard_map/ppermute | solution.py:89
  58.9 16.9 %collective-permute-start.3 = (bf16[136,128]{1,0:T(8,128)(2,1)S(1)}, bf16[136,128]{1,0:T(8,128)(2,1)S(1)}, u32[]{:S(2)}, u32[]{:S(2)}) collective-permute-start(bf16[136,128]{1,0:T(8,128)(2,1)S(1)} %pad_maximum_fusion.2), channel_id=1, source_target_pairs={{64,0},{72,8},{80,16},{88,24},{96,32},{104,40},{112,48},{120,56},{... | collective-permute-start | bytes 104456 | tf_op jit(solution)/shard_map/ppermute | solution.py:89
  67.3 10.7 %collective-permute-start.2 = (bf16[136,128]{1,0:T(8,128)(2,1)S(1)}, bf16[136,128]{1,0:T(8,128)(2,1)S(1)}, u32[]{:S(2)}, u32[]{:S(2)}) collective-permute-start(bf16[136,128]{1,0:T(8,128)(2,1)S(1)} %pad_maximum_fusion.2), channel_id=1, source_target_pairs={{32,0},{40,8},{48,16},{56,24},{64,32},{72,40},{80,48},{88,56},{96,... | collective-permute-start | bytes 104456 | tf_op jit(solution)/shard_map/ppermute | solution.py:89
